TPU v7x, 32 devices: a whole 2x2x4 slice. The times are simulated.
32 devices in a mesh: row: 4 (over y, x), col: 8 (over z, core).
Axes of the slice: x: 2, y: 2, z: 4, core: 2. Of those that a mesh axis runs over, the one named last changes fastest.
Arguments:
- text: bfloat16 [32, 2, 502, 768], P(('row', 'col')), may hold values from -6 to 6
- memory: bfloat16 [32, 10, 768], P(('row', 'col')), may hold values from -6 to 6
- tail_lengths: int32 [32], P(('row', 'col')), may hold values from 125 to 502, as said below
- picture_starts: int32 [32, 2], P(('row', 'col')), may hold values from 0 to 246, as said below
- grad_out: bfloat16 [32, 2, 522, 768], P(('row', 'col')), may hold values from -6 to 6
- query_weight: bfloat16 [768, 768], P('row', 'col'), may hold values from -0.21875 to 0.21875
- key_weight: bfloat16 [768, 768], P('row', 'col'), may hold values from -0.21875 to 0.21875
- value_weight: bfloat16 [768, 768], P('row', 'col'), may hold values from -0.21875 to 0.21875
- out_weight: bfloat16 [768, 768], P('row', 'col'), may hold values from -2.5 to 2.5
- up_weight: bfloat16 [768, 3072], P('row', 'col'), may hold values from -0.21875 to 0.21875
- down_weight: bfloat16 [3072, 768], P('row', 'col'), may hold values from -0.109375 to 0.109375
- query_bias: bfloat16 [768], P('col'), may hold values from -4 to 4
- value_bias: bfloat16 [768], P('col'), may hold values from -4 to 4
- out_bias: bfloat16 [768], P('col'), may hold values from -4 to 4
- attention_gain: bfloat16 [768], P('col'), may hold values from 0.5 to 1.5
- attention_shift: bfloat16 [768], P('col'), may hold values from -4 to 4
- up_bias: bfloat16 [3072], P('col'), may hold values from -4 to 4
- down_bias: bfloat16 [768], P('col'), may hold values from -4 to 4
- output_gain: bfloat16 [768], P('col'), may hold values from 0.5 to 1.5
- output_shift: bfloat16 [768], P('col'), may hold values from -4 to 4
Outputs:
- layer_output: bfloat16 [32, 2, 522, 768], P(('row', 'col'))
- text_grad: bfloat16 [32, 2, 502, 768], P(('row', 'col'))
- memory_grad: bfloat16 [32, 10, 768], P(('row', 'col'))
- query_weight_grad: float32 [768, 768], P('row', 'col')
- key_weight_grad: float32 [768, 768], P('row', 'col')
- value_weight_grad: float32 [768, 768], P('row', 'col')
- out_weight_grad: float32 [768, 768], P('row', 'col')
- up_weight_grad: float32 [768, 3072], P('row', 'col')
- down_weight_grad: float32 [3072, 768], P('row', 'col')
- query_bias_grad: float32 [768], P('col')
- value_bias_grad: float32 [768], P('col')
- out_bias_grad: float32 [768], P('col')
- attention_gain_grad: float32 [768], P('col')
- attention_shift_grad: float32 [768], P('col')
- up_bias_grad: float32 [3072], P('col')
- down_bias_grad: float32 [768], P('col')
- output_gain_grad: float32 [768], P('col')
- output_shift_grad: float32 [768], P('col')
Inputs may be any that keep to these rules, and one draw needn't show every extreme that they name: `tail_lengths`: valid text positions of each sequence's second segment; some sequence has 502 and some 502 // 4. `picture_starts`: start of each segment's picture span among its 502 text positions; the span of 256 tokens ends inside them.
All inputs are finite; a program needn't handle non-finite values.
Results may differ from a plain program's by a relative error of at most 0.02.
Values may be sent and summed in bfloat16 or wider, within the bound.
A program may use at most 192 MiB of HBM per device.

v0:
```python
import jax
import jax.numpy as jnp
from jax import lax
from jax.sharding import PartitionSpec as P

HEADS = 12
HEAD_DIM = 64
MEMORY = 10
TEXT = 502
PICTURE = 256
GROUP_HEADS = 4
SEG_ROWS = 522


epsilon = 1e-06
masked_score = -1e30


def layer_norm(inputs, gain, shift):
    center = jnp.mean(inputs, axis=-1, keepdims=True)
    centred = inputs - center
    spread = jnp.mean(centred * centred, axis=-1, keepdims=True)
    return centred * lax.rsqrt(spread + epsilon) * gain + shift


def gelu_exact(inputs):
    return jax.nn.gelu(inputs, approximate=False)


def allowed_pairs(length, start):
    place = jnp.arange(SEG_ROWS)
    offset = place - MEMORY
    is_text = (offset >= 0) & (offset < TEXT)
    usable = jnp.logical_not(is_text & (offset >= length))
    picture = is_text & (offset >= start) & (offset < start + PICTURE)
    causal = place[None, :] <= place[:, None]
    inside = picture[:, None] & picture[None, :]
    return usable[None, :] & (causal | inside)


def product(left, right):
    return jnp.dot(left, right, preferred_element_type=jnp.float32)


def product_left(left, right):
    return jnp.einsum("rd,re->de", left, right, preferred_element_type=jnp.float32)


def product_right(left, right):
    return jnp.einsum("re,de->rd", left, right, preferred_element_type=jnp.float32)


def column_sums(narrow):
    return jnp.sum(narrow.astype(jnp.float32), axis=0)


def head_block(array, index):
    width = GROUP_HEADS * HEAD_DIM
    piece = lax.dynamic_slice_in_dim(array, index * width, width, 1)
    return piece.reshape(SEG_ROWS, GROUP_HEADS, HEAD_DIM)


def attend_forward(items):
    query, keys, values, length, start = items
    allowed = allowed_pairs(length, start)[None]
    width = GROUP_HEADS * HEAD_DIM
    scale = HEAD_DIM ** (-0.5)

    def group_step(index, carry):
        mixed, logsums = carry
        scores = (
            jnp.einsum(
                "qgd,kgd->gqk",
                head_block(query, index),
                head_block(keys, index),
                preferred_element_type=jnp.float32,
            )
            * scale
        )
        scores = jnp.where(allowed, scores, masked_score)
        peak = jnp.max(scores, axis=-1, keepdims=True)
        expos = jnp.exp(scores - peak)
        total = jnp.sum(expos, axis=-1, keepdims=True)
        probs = (expos / total).astype(jnp.bfloat16)
        block_out = jnp.einsum(
            "gqk,kgd->qgd", probs, head_block(values, index), preferred_element_type=jnp.float32
        )
        mixed = lax.dynamic_update_slice_in_dim(
            mixed, block_out.reshape(SEG_ROWS, width), index * width, 1
        )
        block_sums = peak[..., 0] + jnp.log(total[..., 0])
        logsums = lax.dynamic_update_slice_in_dim(logsums, block_sums, index * GROUP_HEADS, 0)
        return (mixed, logsums)

    start_state = (
        jnp.zeros((SEG_ROWS, HEADS * HEAD_DIM), jnp.float32),
        jnp.zeros((HEADS, SEG_ROWS), jnp.float32),
    )
    return lax.fori_loop(0, HEADS // GROUP_HEADS, group_step, start_state)


def attend_backward(items):
    query, keys, values, logsums, mixed_grad, length, start = items
    allowed = allowed_pairs(length, start)[None]
    width = GROUP_HEADS * HEAD_DIM
    scale = HEAD_DIM ** (-0.5)

    def group_step(index, carry):
        query_grad, key_grad, value_grad = carry
        query_part = head_block(query, index)
        key_part = head_block(keys, index)
        value_part = head_block(values, index)
        grad_part = head_block(mixed_grad, index)
        block_sums = lax.dynamic_slice_in_dim(logsums, index * GROUP_HEADS, GROUP_HEADS, 0)
        scores = (
            jnp.einsum("qgd,kgd->gqk", query_part, key_part, preferred_element_type=jnp.float32)
            * scale
        )
        probs = jnp.where(allowed, jnp.exp(scores - block_sums[..., None]), 0.0)
        narrow_probs = probs.astype(jnp.bfloat16)
        prob_grad = jnp.einsum(
            "qgd,kgd->gqk", grad_part, value_part, preferred_element_type=jnp.float32
        )
        value_block = jnp.einsum(
            "gqk,qgd->kgd", narrow_probs, grad_part, preferred_element_type=jnp.float32
        )
        inner = jnp.sum(probs * prob_grad, axis=-1, keepdims=True)
        score_grad = (probs * (prob_grad - inner)).astype(jnp.bfloat16)
        query_block = (
            jnp.einsum("gqk,kgd->qgd", score_grad, key_part, preferred_element_type=jnp.float32)
            * scale
        )
        key_block = (
            jnp.einsum("gqk,qgd->kgd", score_grad, query_part, preferred_element_type=jnp.float32)
            * scale
        )
        begin = index * width
        query_grad = lax.dynamic_update_slice_in_dim(
            query_grad, query_block.reshape(SEG_ROWS, width), begin, 1
        )
        key_grad = lax.dynamic_update_slice_in_dim(
            key_grad, key_block.reshape(SEG_ROWS, width), begin, 1
        )
        value_grad = lax.dynamic_update_slice_in_dim(
            value_grad, value_block.reshape(SEG_ROWS, width), begin, 1
        )
        return (query_grad, key_grad, value_grad)

    zeros = jnp.zeros((SEG_ROWS, HEADS * HEAD_DIM), jnp.float32)
    return lax.fori_loop(0, HEADS // GROUP_HEADS, group_step, (zeros, zeros, zeros))


def segment_forward(inputs, lengths, starts, weights):
    (
        query_weight,
        key_weight,
        value_weight,
        out_weight,
        up_weight,
        down_weight,
        query_bias,
        value_bias,
        out_bias,
        attention_gain,
        attention_shift,
        up_bias,
        down_bias,
        output_gain,
        output_shift,
    ) = weights
    count = inputs.shape[0]
    width = inputs.shape[2]
    row_shape = (count, SEG_ROWS, width)
    flat = inputs.reshape(count * SEG_ROWS, width)
    narrow_in = flat.astype(jnp.bfloat16)
    query = (product(narrow_in, query_weight) + query_bias).astype(jnp.bfloat16)
    keys = product(narrow_in, key_weight).astype(jnp.bfloat16)
    values = (product(narrow_in, value_weight) + value_bias).astype(jnp.bfloat16)
    mixed, logsums = lax.map(
        attend_forward,
        (
            query.reshape(row_shape),
            keys.reshape(row_shape),
            values.reshape(row_shape),
            lengths,
            starts,
        ),
    )
    narrow_mixed = mixed.reshape(count * SEG_ROWS, width).astype(jnp.bfloat16)
    first_sum = flat + (product(narrow_mixed, out_weight) + out_bias)
    hidden = layer_norm(first_sum, attention_gain, attention_shift)
    narrow_hidden = hidden.astype(jnp.bfloat16)
    upward = product(narrow_hidden, up_weight) + up_bias
    activated = gelu_exact(upward).astype(jnp.bfloat16)
    second_sum = hidden + (product(activated, down_weight) + down_bias)
    result = layer_norm(second_sum, output_gain, output_shift)
    saved = (
        narrow_in,
        query,
        keys,
        values,
        logsums,
        narrow_mixed,
        first_sum,
        narrow_hidden,
        upward,
        activated,
        second_sum,
    )
    return (result.reshape(row_shape), saved)


def segment_backward(result_grad, saved, lengths, starts, weights):
    (
        query_weight,
        key_weight,
        value_weight,
        out_weight,
        up_weight,
        down_weight,
        query_bias,
        value_bias,
        out_bias,
        attention_gain,
        attention_shift,
        up_bias,
        down_bias,
        output_gain,
        output_shift,
    ) = weights
    (
        narrow_in,
        query,
        keys,
        values,
        logsums,
        narrow_mixed,
        first_sum,
        narrow_hidden,
        upward,
        activated,
        second_sum,
    ) = saved
    count = result_grad.shape[0]
    width = result_grad.shape[2]
    row_shape = (count, SEG_ROWS, width)
    flat_grad = result_grad.reshape(count * SEG_ROWS, width)
    unused, second_pull = jax.vjp(layer_norm, second_sum, output_gain, output_shift)
    second_grad, output_gain_grad, output_shift_grad = second_pull(flat_grad)
    down_grad = second_grad.astype(jnp.bfloat16)
    down_weight_grad = product_left(activated, down_grad)
    down_bias_grad = column_sums(down_grad)
    unused, gelu_pull = jax.vjp(gelu_exact, upward)
    up_grad = gelu_pull(product_right(down_grad, down_weight))[0].astype(jnp.bfloat16)
    up_weight_grad = product_left(narrow_hidden, up_grad)
    up_bias_grad = column_sums(up_grad)
    hidden_grad = product_right(up_grad, up_weight) + second_grad
    unused, first_pull = jax.vjp(layer_norm, first_sum, attention_gain, attention_shift)
    first_grad, attention_gain_grad, attention_shift_grad = first_pull(hidden_grad)
    branch_grad = first_grad.astype(jnp.bfloat16)
    out_weight_grad = product_left(narrow_mixed, branch_grad)
    out_bias_grad = column_sums(branch_grad)
    mixed_grad = product_right(branch_grad, out_weight).astype(jnp.bfloat16)
    query_grad, key_grad, value_grad = lax.map(
        attend_backward,
        (
            query.reshape(row_shape),
            keys.reshape(row_shape),
            values.reshape(row_shape),
            logsums,
            mixed_grad.reshape(row_shape),
            lengths,
            starts,
        ),
    )
    query_grad = query_grad.reshape(count * SEG_ROWS, width).astype(jnp.bfloat16)
    key_grad = key_grad.reshape(count * SEG_ROWS, width).astype(jnp.bfloat16)
    value_grad = value_grad.reshape(count * SEG_ROWS, width).astype(jnp.bfloat16)
    query_weight_grad = product_left(narrow_in, query_grad)
    key_weight_grad = product_left(narrow_in, key_grad)
    value_weight_grad = product_left(narrow_in, value_grad)
    query_bias_grad = column_sums(query_grad)
    value_bias_grad = column_sums(value_grad)
    input_grad = (
        first_grad
        + product_right(query_grad, query_weight)
        + product_right(key_grad, key_weight)
        + product_right(value_grad, value_weight)
    )
    grads = (
        query_weight_grad,
        key_weight_grad,
        value_weight_grad,
        out_weight_grad,
        up_weight_grad,
        down_weight_grad,
        query_bias_grad,
        value_bias_grad,
        out_bias_grad,
        attention_gain_grad,
        attention_shift_grad,
        up_bias_grad,
        down_bias_grad,
        output_gain_grad,
        output_shift_grad,
    )
    return (input_grad.reshape(row_shape), grads)


def fetch(
    query_weight,
    key_weight,
    value_weight,
    out_weight,
    up_weight,
    down_weight,
    query_bias,
    value_bias,
    out_bias,
    attention_gain,
    attention_shift,
    up_bias,
    down_bias,
    output_gain,
    output_shift,
):
    query_weight, key_weight, value_weight, out_weight, up_weight, down_weight = (
        lax.all_gather(query_weight, "row", axis=0, tiled=True),
        lax.all_gather(key_weight, "row", axis=0, tiled=True),
        lax.all_gather(value_weight, "row", axis=0, tiled=True),
        lax.all_gather(out_weight, "row", axis=0, tiled=True),
        lax.all_gather(up_weight, "row", axis=0, tiled=True),
        lax.all_gather(down_weight, "row", axis=0, tiled=True),
    )
    gathered = (
        lax.all_gather(query_weight, "col", axis=1, tiled=True),
        lax.all_gather(key_weight, "col", axis=1, tiled=True),
        lax.all_gather(value_weight, "col", axis=1, tiled=True),
        lax.all_gather(out_weight, "col", axis=1, tiled=True),
        lax.all_gather(up_weight, "col", axis=1, tiled=True),
        lax.all_gather(down_weight, "col", axis=1, tiled=True),
        lax.all_gather(query_bias, "col", axis=0, tiled=True),
        lax.all_gather(value_bias, "col", axis=0, tiled=True),
        lax.all_gather(out_bias, "col", axis=0, tiled=True),
        lax.all_gather(attention_gain, "col", axis=0, tiled=True),
        lax.all_gather(attention_shift, "col", axis=0, tiled=True),
        lax.all_gather(up_bias, "col", axis=0, tiled=True),
        lax.all_gather(down_bias, "col", axis=0, tiled=True),
        lax.all_gather(output_gain, "col", axis=0, tiled=True),
        lax.all_gather(output_shift, "col", axis=0, tiled=True),
    )
    gathered = tuple(gathered)
    return gathered[:6] + tuple((item.astype(jnp.float32) for item in gathered[6:]))


def reduce_grads(grads):
    (
        query_weight_grad,
        key_weight_grad,
        value_weight_grad,
        out_weight_grad,
        up_weight_grad,
        down_weight_grad,
        query_bias_grad,
        value_bias_grad,
        out_bias_grad,
        attention_gain_grad,
        attention_shift_grad,
        up_bias_grad,
        down_bias_grad,
        output_gain_grad,
        output_shift_grad,
    ) = grads
    summed = (
        lax.psum_scatter(query_weight_grad, "col", scatter_dimension=1, tiled=True),
        lax.psum_scatter(key_weight_grad, "col", scatter_dimension=1, tiled=True),
        lax.psum_scatter(value_weight_grad, "col", scatter_dimension=1, tiled=True),
        lax.psum_scatter(out_weight_grad, "col", scatter_dimension=1, tiled=True),
        lax.psum_scatter(up_weight_grad, "col", scatter_dimension=1, tiled=True),
        lax.psum_scatter(down_weight_grad, "col", scatter_dimension=1, tiled=True),
        lax.psum_scatter(query_bias_grad, "col", scatter_dimension=0, tiled=True),
        lax.psum_scatter(value_bias_grad, "col", scatter_dimension=0, tiled=True),
        lax.psum_scatter(out_bias_grad, "col", scatter_dimension=0, tiled=True),
        lax.psum_scatter(attention_gain_grad, "col", scatter_dimension=0, tiled=True),
        lax.psum_scatter(attention_shift_grad, "col", scatter_dimension=0, tiled=True),
        lax.psum_scatter(up_bias_grad, "col", scatter_dimension=0, tiled=True),
        lax.psum_scatter(down_bias_grad, "col", scatter_dimension=0, tiled=True),
        lax.psum_scatter(output_gain_grad, "col", scatter_dimension=0, tiled=True),
        lax.psum_scatter(output_shift_grad, "col", scatter_dimension=0, tiled=True),
    )
    matrices = (
        lax.psum_scatter(
            summed[0].astype(jnp.bfloat16), "row", scatter_dimension=0, tiled=True
        ).astype(jnp.float32),
        lax.psum_scatter(
            summed[1].astype(jnp.bfloat16), "row", scatter_dimension=0, tiled=True
        ).astype(jnp.float32),
        lax.psum_scatter(
            summed[2].astype(jnp.bfloat16), "row", scatter_dimension=0, tiled=True
        ).astype(jnp.float32),
        lax.psum_scatter(
            summed[3].astype(jnp.bfloat16), "row", scatter_dimension=0, tiled=True
        ).astype(jnp.float32),
        lax.psum_scatter(
            summed[4].astype(jnp.bfloat16), "row", scatter_dimension=0, tiled=True
        ).astype(jnp.float32),
        lax.psum_scatter(
            summed[5].astype(jnp.bfloat16), "row", scatter_dimension=0, tiled=True
        ).astype(jnp.float32),
    )
    vectors = tuple(summed[6:])
    vectors = lax.psum(
        (
            vectors[0],
            vectors[1],
            vectors[2],
            vectors[3],
            vectors[4],
            vectors[5],
            vectors[6],
            vectors[7],
            vectors[8],
        ),
        "row",
    )
    return tuple(matrices) + tuple(vectors)


def body(
    text,
    memory,
    tail_lengths,
    picture_starts,
    grad_out,
    query_weight,
    key_weight,
    value_weight,
    out_weight,
    up_weight,
    down_weight,
    query_bias,
    value_bias,
    out_bias,
    attention_gain,
    attention_shift,
    up_bias,
    down_bias,
    output_gain,
    output_shift,
):
    weights = fetch(
        query_weight,
        key_weight,
        value_weight,
        out_weight,
        up_weight,
        down_weight,
        query_bias,
        value_bias,
        out_bias,
        attention_gain,
        attention_shift,
        up_bias,
        down_bias,
        output_gain,
        output_shift,
    )
    count = text.shape[0]
    full_lengths = jnp.full((count,), TEXT, jnp.int32)
    start_memory = memory.astype(jnp.float32)
    first_inputs = jnp.concatenate(
        [start_memory, text[:, 0].astype(jnp.float32), start_memory], axis=1
    )
    first_result, first_saved = segment_forward(
        first_inputs, full_lengths, picture_starts[:, 0], weights
    )
    carried = first_result[:, MEMORY + TEXT :]
    second_inputs = jnp.concatenate([carried, text[:, 1].astype(jnp.float32), carried], axis=1)
    second_result, second_saved = segment_forward(
        second_inputs, tail_lengths, picture_starts[:, 1], weights
    )
    layer_output = jnp.stack([first_result, second_result], axis=1).astype(jnp.bfloat16)
    cotangent = grad_out.astype(jnp.float32)
    second_input_grad, second_grads = segment_backward(
        cotangent[:, 1], second_saved, tail_lengths, picture_starts[:, 1], weights
    )
    carried_grad = second_input_grad[:, :MEMORY] + second_input_grad[:, MEMORY + TEXT :]
    first_cotangent = cotangent[:, 0].at[:, MEMORY + TEXT :].add(carried_grad)
    first_input_grad, first_grads = segment_backward(
        first_cotangent, first_saved, full_lengths, picture_starts[:, 0], weights
    )
    memory_grad = (first_input_grad[:, :MEMORY] + first_input_grad[:, MEMORY + TEXT :]).astype(
        jnp.bfloat16
    )
    text_grad = jnp.stack(
        [first_input_grad[:, MEMORY : MEMORY + TEXT], second_input_grad[:, MEMORY : MEMORY + TEXT]],
        axis=1,
    ).astype(jnp.bfloat16)
    totals = tuple(
        (
            jnp.add(first_item, second_item)
            for first_item, second_item in zip(first_grads, second_grads)
        )
    )
    reduced = reduce_grads(totals)
    return (
        layer_output,
        text_grad,
        memory_grad,
        reduced[0],
        reduced[1],
        reduced[2],
        reduced[3],
        reduced[4],
        reduced[5],
        reduced[6],
        reduced[7],
        reduced[8],
        reduced[9],
        reduced[10],
        reduced[11],
        reduced[12],
        reduced[13],
        reduced[14],
    )


def solution(mesh):
    return jax.shard_map(
        body,
        mesh=mesh,
        in_specs=(
            P(("row", "col"), None, None, None),
            P(("row", "col"), None, None),
            P(("row", "col")),
            P(("row", "col"), None),
            P(("row", "col"), None, None, None),
            P("row", "col"),
            P("row", "col"),
            P("row", "col"),
            P("row", "col"),
            P("row", "col"),
            P("row", "col"),
            P("col"),
            P("col"),
            P("col"),
            P("col"),
            P("col"),
            P("col"),
            P("col"),
            P("col"),
            P("col"),
        ),
        out_specs=(
            P(("row", "col"), None, None, None),
            P(("row", "col"), None, None, None),
            P(("row", "col"), None, None),
            P("row", "col"),
            P("row", "col"),
            P("row", "col"),
            P("row", "col"),
            P("row", "col"),
            P("row", "col"),
            P("col"),
            P("col"),
            P("col"),
            P("col"),
            P("col"),
            P("col"),
            P("col"),
            P("col"),
            P("col"),
        ),
        check_vma=False,
    )
```

profile of v0, /device:TPU:0, one launch (start us, length us, event | category | flops | bytes accessed | tf_op | source)
XLA Modules:
  0.0 1252.2 jit_solution(11367170205742036020)
XLA Ops:
  7.3 10.6 all_gather.63
  18.7 8.5 all_gather.66
  28.2 8.1 all_gather.69
  37.2 8.3 all_gather.71
  46.4 11.7 all_gather.76
  58.2 11.4 all_gather.79
  72.8 26.4 %all-reduce.19 = (bf16[768]{0:T(1024)(128)(2,1)S(1)}, bf16[768]{0:T(1024)(128)(2,1)S(1)}, bf16[768]{0:T(1024)(128)(2,1)S(1)}, bf16[768]{0:T(1024)(128)(2,1)S(1)}...) all-reduce(bf16[768]{0:T(1024)(128)(2,1)S(1)} %dynamic-update-slice, ...), channel_id=1, replica_groups=mesh['row'=4,'col'=8] {'col'}, use_global_device_ids=true, to_apply=%add.2 | all-reduce | flops 6144 | bytes 24576
  104.3 13.1 %all-gather = bf16[8,1,384]{2,1,0:T(2,128)(2,1)S(1)} all-gather(bf16[1,1,384]{2,1,0:T(2,128)(2,1)S(1)} %reshape.831), channel_id=1, replica_groups=mesh['row'=4,'col'=8] {'col'}, dimensions={0}, use_global_device_ids=true | all-gather | bytes 6912 | tf_op jit(solution)/shard_map/all_gather | solution.py:347
  141.8 30.7 %while.109 = (s32[]{:T(128)}, bf16[522,768]{0,1:T(8,128)(2,1)}, f32[12,522]{1,0:T(8,128)S(1)}, bf16[522,768]{0,1:T(8,128)(2,1)S(1)}, bf16[522,768]{0,1:T(8,128)(...) while((s32[]{:T(128)}, bf16[522,768]{0,1:T(8,128)(2,1)}, ...), condition=%wide.region_3.4_spmd.clone, body=%wide.region_0.3_spmd.clone.sunk | while | flops 293190688 | bytes 34949516 | solution.py:99
  147.0 4.3 fusion.304
  157.3 4.3 fusion.304
  167.5 4.2 fusion.304
  172.6 4.4 fusion.158
  178.6 21.9 %multiply_convert_fusion.3 = (bf16[522,3072]{1,0:T(8,128)(2,1)}, f32[522,3072]{1,0:T(8,128)}, f32[522,3072]{1,0:T(8,128)}) fusion(f32[3072]{0:T(1024)S(1)} %bitcast.325, bf16[768,3072]{1,0:T(8,128)(2,1)} %all-gather.16.cloned.1.call-done, f32[522,768]{1,0:T(8,128)} %copy-done.15, f32[768]{0:T(1024)S(1)} %convert_element_type.312, ...), kind=kOutput, calls=%fused_computation.111 | convolution fusion | flops 2570946048 | bytes 22380624 | tf_op jit(solution)/shard_map/dot_general | solution.py:42
  200.5 18.3 %all-gather.18.cloned.1.call-done = bf16[3072,768]{0,1:T(8,128)(2,1)} async-done(((bf16[3072,96]{0,1:T(8,128)(2,1)}), bf16[3072,768]{0,1:T(8,128)(2,1)}) %all-gather.18.cloned.1.call-update) | async-done | bytes 4718608 | tf_op jit(solution)/shard_map/all_gather | solution.py:341
  218.8 6.2 fusion.159
  239.2 33.9 %while.110 = (s32[]{:T(128)}, bf16[522,768]{0,1:T(8,128)(2,1)}, f32[12,522]{1,0:T(8,128)S(1)}, bf16[522,768]{0,1:T(8,128)(2,1)S(1)}, bf16[522,768]{0,1:T(8,128)(...) while((s32[]{:T(128)}, bf16[522,768]{0,1:T(8,128)(2,1)}, ...), condition=%wide.region_11.12_spmd.clone, body=%wide.region_8.11_spmd.clone.sunk | while | flops 293190688 | bytes 34949516 | solution.py:99
  245.8 4.2 fusion.311
  257.0 4.2 fusion.311
  268.1 4.2 fusion.311
  276.8 19.7 %multiply_convert_fusion.2 = (bf16[522,3072]{1,0:T(8,128)(2,1)S(1)}, f32[522,3072]{1,0:T(8,128)S(1)}, f32[522,3072]{1,0:T(8,128)}) fusion(f32[3072]{0:T(1024)S(1)} %bitcast.326, bf16[768,3072]{1,0:T(8,128)(2,1)} %all-gather.16.cloned.1.call-done, f32[522,768]{1,0:T(8,128)S(1)} %get-tuple-element.1268, f32[522]{0:T(1024)S(1)} %fusion.122, ...), kind=kOutput, calls=%fused_computation.98 | convolution fusion | flops 2570946048 | bytes 22380624 | tf_op jit(solution)/shard_map/dot_general | solution.py:42
  303.6 7.9 convert_reduce_fusion
  322.8 198.1 %while.111 = (s32[]{:T(128)}, bf16[522,768]{0,1:T(8,128)(2,1)}, bf16[522,768]{0,1:T(8,128)(2,1)}, bf16[522,768]{0,1:T(8,128)(2,1)}, bf16[522,768]{0,1:T(8,128)(2...) while((s32[]{:T(128)}, bf16[522,768]{0,1:T(8,128)(2,1)}, ...), condition=%wide.region_22.23_spmd.clone, body=%wide.region_20.22_spmd.clone.sunk | while | flops 714445184 | bytes 74171936 | solution.py:150
  327.3 8.4 copy.243
  340.2 8.5 copy.241
  349.1 29.7 %multiply_convert_fusion.6 = bf16[4,522,522]{2,0,1:T(4,128)(2,1)S(1)} fusion(f32[4,522,522]{2,0,1:T(4,128)} %copy.241, f32[4,522]{0,1:T(8,128)S(1)} %copy.242, f32[4,522,522]{2,0,1:T(4,128)} %copy.243, pred[522,522]{1,0:T(8,128)(4,1)S(1)} %fusion.325), kind=kOutput, calls=%fused_computation.39.clone.1 | output fusion | flops 10901969 | bytes 11180196 | tf_op jit(solution)/shard_map/while/body/eval_jaxpr/while/body/eval_jaxpr/sub | solution.py:128
  379.5 6.0 fusion.327
  393.2 8.4 copy.243
  406.1 8.5 copy.241
  415.0 29.7 %multiply_convert_fusion.6 = bf16[4,522,522]{2,0,1:T(4,128)(2,1)S(1)} fusion(f32[4,522,522]{2,0,1:T(4,128)} %copy.241, f32[4,522]{0,1:T(8,128)S(1)} %copy.242, f32[4,522,522]{2,0,1:T(4,128)} %copy.243, pred[522,522]{1,0:T(8,128)(4,1)S(1)} %fusion.325), kind=kOutput, calls=%fused_computation.39.clone.1 | output fusion | flops 10901969 | bytes 11180196 | tf_op jit(solution)/shard_map/while/body/eval_jaxpr/while/body/eval_jaxpr/sub | solution.py:128
  445.4 6.0 fusion.327
  459.0 8.4 copy.243
  471.9 8.5 copy.241
  480.8 29.7 %multiply_convert_fusion.6 = bf16[4,522,522]{2,0,1:T(4,128)(2,1)S(1)} fusion(f32[4,522,522]{2,0,1:T(4,128)} %copy.241, f32[4,522]{0,1:T(8,128)S(1)} %copy.242, f32[4,522,522]{2,0,1:T(4,128)} %copy.243, pred[522,522]{1,0:T(8,128)(4,1)S(1)} %fusion.325), kind=kOutput, calls=%fused_computation.39.clone.1 | output fusion | flops 10901969 | bytes 11180196 | tf_op jit(solution)/shard_map/while/body/eval_jaxpr/while/body/eval_jaxpr/sub | solution.py:128
  511.2 6.0 fusion.327
  531.9 9.2 convert_reduce_fusion.1
  549.0 3.8 convolution_add_fusion.2
  557.0 203.0 %while.112 = (s32[]{:T(128)}, bf16[522,768]{0,1:T(8,128)(2,1)S(1)}, bf16[522,768]{0,1:T(8,128)(2,1)}, bf16[522,768]{0,1:T(8,128)(2,1)S(1)}, bf16[522,768]{0,1:T(...) while((s32[]{:T(128)}, bf16[522,768]{0,1:T(8,128)(2,1)S(1)}, ...), condition=%wide.region_29.30_spmd.clone, body=%wide.region_27.29_spmd.clone.sunk | while | flops 714445184 | bytes 74353184 | solution.py:150
  562.3 8.4 copy.250
  576.2 8.3 copy.248
  585.7 29.7 %multiply_convert_fusion.7 = bf16[4,522,522]{2,0,1:T(4,128)(2,1)S(1)} fusion(f32[4,522,522]{2,0,1:T(4,128)} %copy.248, f32[4,522]{0,1:T(8,128)S(1)} %copy.249, f32[4,522,522]{2,0,1:T(4,128)} %copy.250, pred[522,522]{1,0:T(8,128)(4,1)S(1)} %fusion.343), kind=kOutput, calls=%fused_computation.65.clone.1 | output fusion | flops 10901969 | bytes 11180196 | tf_op jit(solution)/shard_map/while/body/eval_jaxpr/while/body/eval_jaxpr/sub | solution.py:128
  616.1 6.0 fusion.345
  630.0 8.3 copy.250
  643.8 8.3 copy.248
  653.3 29.7 %multiply_convert_fusion.7 = bf16[4,522,522]{2,0,1:T(4,128)(2,1)S(1)} fusion(f32[4,522,522]{2,0,1:T(4,128)} %copy.248, f32[4,522]{0,1:T(8,128)S(1)} %copy.249, f32[4,522,522]{2,0,1:T(4,128)} %copy.250, pred[522,522]{1,0:T(8,128)(4,1)S(1)} %fusion.343), kind=kOutput, calls=%fused_computation.65.clone.1 | output fusion | flops 10901969 | bytes 11180196 | tf_op jit(solution)/shard_map/while/body/eval_jaxpr/while/body/eval_jaxpr/sub | solution.py:128
  683.6 6.0 fusion.345
  697.5 8.3 copy.250
  711.3 8.3 copy.248
  720.8 29.7 %multiply_convert_fusion.7 = bf16[4,522,522]{2,0,1:T(4,128)(2,1)S(1)} fusion(f32[4,522,522]{2,0,1:T(4,128)} %copy.248, f32[4,522]{0,1:T(8,128)S(1)} %copy.249, f32[4,522,522]{2,0,1:T(4,128)} %copy.250, pred[522,522]{1,0:T(8,128)(4,1)S(1)} %fusion.343), kind=kOutput, calls=%fused_computation.65.clone.1 | output fusion | flops 10901969 | bytes 11180196 | tf_op jit(solution)/shard_map/while/body/eval_jaxpr/while/body/eval_jaxpr/sub | solution.py:128
  751.2 6.0 fusion.345
  778.5 6.3 fusion.166
  784.8 6.9 convolution_add_fusion
  792.4 6.7 fusion.139
  799.2 7.1 convolution_add_fusion.1
  810.2 30.9 %reduce-scatter.23.cloned.1.call-done = f32[768,96]{0,1:T(8,128)} async-done(((f32[768,768]{0,1:T(8,128)}), f32[768,96]{0,1:T(8,128)}) %reduce-scatter.23.cloned.1.call-update) | async-done | bytes 294928 | tf_op jit(solution)/shard_map/reduce_scatter | solution.py:376
  844.3 34.9 %reduce-scatter.21.cloned.1.call-done = f32[768,96]{0,1:T(8,128)} async-done(((f32[768,768]{0,1:T(8,128)}), f32[768,96]{0,1:T(8,128)}) %reduce-scatter.21.cloned.1.call-update) | async-done | bytes 294928 | tf_op jit(solution)/shard_map/reduce_scatter | solution.py:375
  882.8 97.1 %reduce-scatter.33.cloned.1.call-done = f32[3072,96]{0,1:T(8,128)} async-done(((f32[3072,768]{0,1:T(8,128)}), f32[3072,96]{0,1:T(8,128)}) %reduce-scatter.33.cloned.1.call-update) | async-done | bytes 1179664 | tf_op jit(solution)/shard_map/reduce_scatter | solution.py:380
  988.1 91.8 %reduce-scatter.29.cloned.1.call-done = f32[768,384]{1,0:T(8,128)} async-done(((f32[768,3072]{1,0:T(8,128)}), f32[768,384]{1,0:T(8,128)}) %reduce-scatter.29.cloned.1.call-update) | async-done | bytes 1179664 | tf_op jit(solution)/shard_map/reduce_scatter | solution.py:379
  1083.8 26.4 %all-reduce.17 = (f32[768]{0:T(1024)S(1)}, f32[768]{0:T(1024)S(1)}, f32[768]{0:T(1024)S(1)}, f32[768]{0:T(1024)S(1)}, f32[768]{0:T(1024)S(1)}, /*index=5*/f32[30...) all-reduce(f32[768]{0:T(1024)S(1)} %add.541, ...), channel_id=14, replica_groups=mesh['row'=4,'col'=8] {'col'}, use_global_device_ids=true, to_apply=%region_44.45.clone | all-reduce | flops 9216 | bytes 73728
  1117.6 10.6 all-reduce.18
  1133.9 25.8 %reduce-scatter.39.cloned.1.call-done = bf16[192,96]{1,0:T(8,128)(2,1)} async-done(((bf16[768,96]{1,0:T(8,128)(2,1)}), bf16[192,96]{1,0:T(8,128)(2,1)}) %reduce-scatter.39.cloned.1.call-update) | async-done | bytes 36880
  1161.4 25.8 %reduce-scatter.37.cloned.1.call-done = bf16[192,96]{1,0:T(8,128)(2,1)} async-done(((bf16[768,96]{1,0:T(8,128)(2,1)}), bf16[192,96]{1,0:T(8,128)(2,1)}) %reduce-scatter.37.cloned.1.call-update) | async-done | bytes 36880
  1188.9 26.5 %reduce-scatter.35.cloned.1.call-done = bf16[768,96]{0,1:T(8,128)(2,1)} async-done(((bf16[3072,96]{0,1:T(8,128)(2,1)}), bf16[768,96]{0,1:T(8,128)(2,1)}) %reduce-scatter.35.cloned.1.call-update) | async-done | bytes 147472 | tf_op jit(solution)/shard_map/reduce_scatter | solution.py:407
  1217.0 26.5 %reduce-scatter.31.cloned.1.call-done = bf16[192,384]{1,0:T(8,128)(2,1)} async-done(((bf16[768,384]{1,0:T(8,128)(2,1)}), bf16[192,384]{1,0:T(8,128)(2,1)}) %reduce-scatter.31.cloned.1.call-update) | async-done | bytes 147472 | tf_op jit(solution)/shard_map/reduce_scatter | solution.py:404
  (626 shorter events, 276.8 us)
Async XLA Ops:
  7.2 39.2 %copy-start.45 = (bf16[192,384]{1,0:T(8,128)(2,1)S(1)}, bf16[192,384]{1,0:T(8,128)(2,1)}, u32[]{:S(2)}) copy-start(bf16[192,384]{1,0:T(8,128)(2,1)} %param.39) | copy-start | bytes 442372
  7.2 51.0 %copy-start.46 = (bf16[768,96]{0,1:T(8,128)(2,1)S(1)}, bf16[768,96]{0,1:T(8,128)(2,1)}, u32[]{:S(2)}) copy-start(bf16[768,96]{0,1:T(8,128)(2,1)} %param.40) | copy-start | bytes 442372
  7.2 118.8 %all-gather.8.cloned.1.call-start = ((), (), s32[]{:S(2)}) async-start(), calls=%async_computation.12 | async-start | bytes 1327104 | tf_op jit(solution)/shard_map/all_gather | solution.py:338
  18.7 112.5 %all-gather.10.cloned.1.call-start = ((), (), s32[]{:S(2)}) async-start(), calls=%async_computation.13 | async-start | bytes 1327104 | tf_op jit(solution)/shard_map/all_gather | solution.py:336
  27.2 42.5 %copy-start.94 = (u32[32]{0:T(128)S(1)}, u32[32]{0:T(128)}, u32[]{:S(2)}) copy-start(u32[32]{0:T(128)} %constant.457) | copy-start | bytes 388
  27.2 43.7 %copy-start.103 = (bf16[96]{0:T(256)(128)(2,1)S(1)}, bf16[96]{0:T(256)(128)(2,1)}, u32[]{:S(2)}) copy-start(bf16[96]{0:T(256)(128)(2,1)} %param.48) | copy-start | bytes 580
  27.2 44.0 %copy-start.104 = (bf16[96]{0:T(256)(128)(2,1)S(1)}, bf16[96]{0:T(256)(128)(2,1)}, u32[]{:S(2)}) copy-start(bf16[96]{0:T(256)(128)(2,1)} %param.49) | copy-start | bytes 580
  27.2 44.2 %copy-start.105 = (bf16[96]{0:T(256)(128)(2,1)S(1)}, bf16[96]{0:T(256)(128)(2,1)}, u32[]{:S(2)}) copy-start(bf16[96]{0:T(256)(128)(2,1)} %param.42) | copy-start | bytes 580
  27.2 44.4 %copy-start.106 = (bf16[96]{0:T(256)(128)(2,1)S(1)}, bf16[96]{0:T(256)(128)(2,1)}, u32[]{:S(2)}) copy-start(bf16[96]{0:T(256)(128)(2,1)} %param.41) | copy-start | bytes 580
  27.2 44.7 %copy-start.107 = (bf16[96]{0:T(256)(128)(2,1)S(1)}, bf16[96]{0:T(256)(128)(2,1)}, u32[]{:S(2)}) copy-start(bf16[96]{0:T(256)(128)(2,1)} %param.43) | copy-start | bytes 580
  27.2 44.9 %copy-start.108 = (bf16[96]{0:T(256)(128)(2,1)S(1)}, bf16[96]{0:T(256)(128)(2,1)}, u32[]{:S(2)}) copy-start(bf16[96]{0:T(256)(128)(2,1)} %param.44) | copy-start | bytes 580
  27.2 45.1 %copy-start.109 = (bf16[96]{0:T(256)(128)(2,1)S(1)}, bf16[96]{0:T(256)(128)(2,1)}, u32[]{:S(2)}) copy-start(bf16[96]{0:T(256)(128)(2,1)} %param.45) | copy-start | bytes 580
  27.3 45.3 %copy-start.110 = (bf16[96]{0:T(256)(128)(2,1)S(1)}, bf16[96]{0:T(256)(128)(2,1)}, u32[]{:S(2)}) copy-start(bf16[96]{0:T(256)(128)(2,1)} %param.47) | copy-start | bytes 580
  27.3 72.0 %copy-start.20 = (bf16[1,2,502,768]{3,1,2,0:T(2,128)(2,1)S(1)}, bf16[1,2,502,768]{3,1,2,0:T(2,128)(2,1)}, u32[]{:S(2)}) copy-start(bf16[1,2,502,768]{3,1,2,0:T(2,128)(2,1)} %param.30) | copy-start | bytes 4626436
  28.1 107.7 %all-gather.12.cloned.1.call-start = ((), (), s32[]{:S(2)}) async-start(), calls=%async_computation.14 | async-start | bytes 1327104 | tf_op jit(solution)/shard_map/all_gather | solution.py:337
  37.1 135.4 %all-gather.14.cloned.1.call-start = ((), (), s32[]{:S(2)}) async-start(), calls=%async_computation.15 | async-start | bytes 1327104 | tf_op jit(solution)/shard_map/all_gather | solution.py:339
  46.3 132.3 %all-gather.16.cloned.1.call-start = ((), (), s32[]{:S(2)}) async-start(), calls=%async_computation.16 | async-start | bytes 5308416 | tf_op jit(solution)/shard_map/all_gather | solution.py:340
  58.1 160.7 %all-gather.18.cloned.1.call-start = ((), (), s32[]{:S(2)}) async-start(), calls=%async_computation.17 | async-start | bytes 5308416 | tf_op jit(solution)/shard_map/all_gather | solution.py:341
  69.6 736.9 %reduce-scatter.27.cloned.1.call-start = ((), (), s32[]{:S(2)}) async-start(), calls=%async_computation.21 | async-start | bytes 2654208 | tf_op jit(solution)/shard_map/reduce_scatter | solution.py:378
  104.2 210.9 %copy-start.66 = (f32[768]{0:T(1024)}, f32[768]{0:T(1024)S(1)}, u32[]{:S(2)}) copy-start(f32[768]{0:T(1024)S(1)} %convert_element_type.311) | copy-start | bytes 9220
  104.3 192.3 %copy-start.92 = (f32[768]{0:T(1024)}, f32[768]{0:T(1024)S(1)}, u32[]{:S(2)}) copy-start(f32[768]{0:T(1024)S(1)} %convert_element_type.312) | copy-start | bytes 9220
  117.4 186.2 %copy-start.84 = (f32[8,1,384]{2,1,0:T(1,128)}, f32[8,1,384]{2,1,0:T(1,128)S(1)}, u32[]{:S(2)}) copy-start(f32[8,1,384]{2,1,0:T(1,128)S(1)} %convert_element_type.370) | copy-start | bytes 36868
  117.4 183.7 %copy-start.47 = (f32[768]{0:T(1024)}, f32[768]{0:T(1024)S(1)}, u32[]{:S(2)}) copy-start(f32[768]{0:T(1024)S(1)} %convert_element_type.317) | copy-start | bytes 9220
  177.0 41.8 %copy-start.61 = (f32[522]{0:T(1024)}, f32[522]{0:T(1024)S(1)}, u32[]{:S(2)}) copy-start(f32[522]{0:T(1024)S(1)} %broadcast_multiply_fusion.3) | copy-start | bytes 6268
  178.6 40.3 %copy-start.79 = (f32[522]{0:T(1024)}, f32[522]{0:T(1024)S(1)}, u32[]{:S(2)}) copy-start(f32[522]{0:T(1024)S(1)} %fusion.120) | copy-start | bytes 6268
  178.6 40.3 %copy-start.16 = (f32[522,768]{1,0:T(8,128)S(1)}, f32[522,768]{1,0:T(8,128)}, u32[]{:S(2)}) copy-start(f32[522,768]{1,0:T(8,128)} %copy-done.15) | copy-start | bytes 4810756
  276.4 38.8 %copy-start.18 = (f32[522,768]{1,0:T(8,128)}, f32[522,768]{1,0:T(8,128)S(1)}, u32[]{:S(2)}) copy-start(f32[522,768]{1,0:T(8,128)S(1)} %get-tuple-element.1268) | copy-start | bytes 4810756
  276.5 38.7 %copy-start.64 = (f32[522]{0:T(1024)}, f32[522]{0:T(1024)S(1)}, u32[]{:S(2)}) copy-start(f32[522]{0:T(1024)S(1)} %broadcast_multiply_fusion.1) | copy-start | bytes 6268
  276.8 38.4 %copy-start.82 = (f32[522]{0:T(1024)}, f32[522]{0:T(1024)S(1)}, u32[]{:S(2)}) copy-start(f32[522]{0:T(1024)S(1)} %fusion.122) | copy-start | bytes 6268
  348.8 30.7 %slice-start = ((s8[5345280]{0:T(1024)(128)(4,1)}), s8[4194304]{0:T(1024)(128)(4,1)S(1)}, s32[]{:S(2)}) async-start(s8[5345280]{0:T(1024)(128)(4,1)} %bitcast.290), calls=%async_computation.30 | async-start | bytes 8388608 | tf_op jit(solution)/shard_map/while/body/eval_jaxpr/while
  414.7 30.7 %slice-start = ((s8[5345280]{0:T(1024)(128)(4,1)}), s8[4194304]{0:T(1024)(128)(4,1)S(1)}, s32[]{:S(2)}) async-start(s8[5345280]{0:T(1024)(128)(4,1)} %bitcast.290), calls=%async_computation.30 | async-start | bytes 8388608 | tf_op jit(solution)/shard_map/while/body/eval_jaxpr/while
  415.0 30.4 %slice-start.1 = ((s8[5345280]{0:T(1024)(128)(4,1)}), s8[1150976]{0:T(1024)(128)(4,1)S(1)}, s32[]{:S(2)}) async-start(s8[5345280]{0:T(1024)(128)(4,1)} %bitcast.290), calls=%async_computation.31 | async-start | bytes 2301952 | tf_op jit(solution)/shard_map/while/body/eval_jaxpr/while
  480.5 30.7 %slice-start = ((s8[5345280]{0:T(1024)(128)(4,1)}), s8[4194304]{0:T(1024)(128)(4,1)S(1)}, s32[]{:S(2)}) async-start(s8[5345280]{0:T(1024)(128)(4,1)} %bitcast.290), calls=%async_computation.30 | async-start | bytes 8388608 | tf_op jit(solution)/shard_map/while/body/eval_jaxpr/while
  552.8 255.6 %reduce-scatter.25.cloned.1.call-start = ((), (), s32[]{:S(2)}) async-start(), calls=%async_computation.20 | async-start | bytes 2654208 | tf_op jit(solution)/shard_map/reduce_scatter | solution.py:377
  557.0 203.8 %copy-start.70 = (bf16[1,10,768]{2,1,0:T(8,128)(2,1)S(1)}, bf16[1,10,768]{2,1,0:T(8,128)(2,1)}, u32[]{:S(2)}) copy-start(bf16[1,10,768]{2,1,0:T(8,128)(2,1)} %param.31) | copy-start | bytes 46084
  585.4 30.7 %slice-start.2 = ((s8[5345280]{0:T(1024)(128)(4,1)}), s8[4194304]{0:T(1024)(128)(4,1)S(1)}, s32[]{:S(2)}) async-start(s8[5345280]{0:T(1024)(128)(4,1)} %bitcast.292), calls=%async_computation.32 | async-start | bytes 8388608 | tf_op jit(solution)/shard_map/while/body/eval_jaxpr/while
  653.0 30.7 %slice-start.2 = ((s8[5345280]{0:T(1024)(128)(4,1)}), s8[4194304]{0:T(1024)(128)(4,1)S(1)}, s32[]{:S(2)}) async-start(s8[5345280]{0:T(1024)(128)(4,1)} %bitcast.292), calls=%async_computation.32 | async-start | bytes 8388608 | tf_op jit(solution)/shard_map/while/body/eval_jaxpr/while
  720.5 30.7 %slice-start.2 = ((s8[5345280]{0:T(1024)(128)(4,1)}), s8[4194304]{0:T(1024)(128)(4,1)S(1)}, s32[]{:S(2)}) async-start(s8[5345280]{0:T(1024)(128)(4,1)} %bitcast.292), calls=%async_computation.32 | async-start | bytes 8388608 | tf_op jit(solution)/shard_map/while/body/eval_jaxpr/while
  766.9 74.2 %reduce-scatter.23.cloned.1.call-start = ((), (), s32[]{:S(2)}) async-start(), calls=%async_computation.19 | async-start | bytes 2654208 | tf_op jit(solution)/shard_map/reduce_scatter | solution.py:376
  772.3 106.9 %reduce-scatter.21.cloned.1.call-start = ((), (), s32[]{:S(2)}) async-start(), calls=%async_computation.18 | async-start | bytes 2654208 | tf_op jit(solution)/shard_map/reduce_scatter | solution.py:375
  778.4 201.4 %reduce-scatter.33.cloned.1.call-start = ((), (), s32[]{:S(2)}) async-start(), calls=%async_computation.24 | async-start | bytes 10616832 | tf_op jit(solution)/shard_map/reduce_scatter | solution.py:380
  791.8 288.1 %reduce-scatter.29.cloned.1.call-start = ((), (), s32[]{:S(2)}) async-start(), calls=%async_computation.22 | async-start | bytes 10616832 | tf_op jit(solution)/shard_map/reduce_scatter | solution.py:379
  806.4 322.4 %reduce-scatter.43.cloned.1.call-start = ((), (), s32[]{:S(2)}) async-start(), calls=%async_computation.29 | async-start | bytes 245760
  808.3 324.0 %reduce-scatter.41.cloned.1.call-start = ((), (), s32[]{:S(2)}) async-start(), calls=%async_computation.28 | async-start | bytes 245760
  810.2 349.6 %reduce-scatter.39.cloned.1.call-start = ((), (), s32[]{:S(2)}) async-start(), calls=%async_computation.27 | async-start | bytes 245760
  842.9 344.3 %reduce-scatter.37.cloned.1.call-start = ((), (), s32[]{:S(2)}) async-start(), calls=%async_computation.26 | async-start | bytes 245760
  881.0 334.4 %reduce-scatter.35.cloned.1.call-start = ((), (), s32[]{:S(2)}) async-start(), calls=%async_computation.25 | async-start | bytes 737280 | tf_op jit(solution)/shard_map/reduce_scatter | solution.py:407
  881.2 101.2 %copy-start.97 = (bf16[768,768]{0,1:T(8,128)(2,1)S(1)}, bf16[768,768]{0,1:T(8,128)(2,1)}, u32[]{:S(2)}) copy-start(bf16[768,768]{0,1:T(8,128)(2,1)} %all-gather.10.cloned.1.call-done) | copy-start | bytes 3538948
  982.0 261.5 %reduce-scatter.31.cloned.1.call-start = ((), (), s32[]{:S(2)}) async-start(), calls=%async_computation.23 | async-start | bytes 737280 | tf_op jit(solution)/shard_map/reduce_scatter | solution.py:404
  988.0 95.5 %copy-start.86 = (f32[3072]{0:T(1024)S(1)}, f32[3072]{0:T(1024)}, u32[]{:S(2)}) copy-start(f32[3072]{0:T(1024)} %get-tuple-element.1215) | copy-start | bytes 36868
  988.0 95.6 %copy-start.87 = (f32[3072]{0:T(1024)S(1)}, f32[3072]{0:T(1024)}, u32[]{:S(2)}) copy-start(f32[3072]{0:T(1024)} %get-tuple-element.1217) | copy-start | bytes 36868
  988.0 95.6 %copy-start.89 = (f32[768]{0:T(1024)S(1)}, f32[768]{0:T(1024)}, u32[]{:S(2)}) copy-start(f32[768]{0:T(1024)} %get-tuple-element.1107) | copy-start | bytes 9220
  988.0 95.6 %copy-start.91 = (f32[768]{0:T(1024)S(1)}, f32[768]{0:T(1024)}, u32[]{:S(2)}) copy-start(f32[768]{0:T(1024)} %get-tuple-element.1108) | copy-start | bytes 9220
  988.0 95.6 %copy-start.88 = (f32[768]{0:T(1024)S(1)}, f32[768]{0:T(1024)}, u32[]{:S(2)}) copy-start(f32[768]{0:T(1024)} %get-tuple-element.1102) | copy-start | bytes 9220
  988.0 95.6 %copy-start.90 = (f32[768]{0:T(1024)S(1)}, f32[768]{0:T(1024)}, u32[]{:S(2)}) copy-start(f32[768]{0:T(1024)} %get-tuple-element.1104) | copy-start | bytes 9220
  988.0 95.6 %copy-start.73 = (f32[768]{0:T(1024)S(1)}, f32[768]{0:T(1024)}, u32[]{:S(2)}) copy-start(f32[768]{0:T(1024)} %get-tuple-element.1219) | copy-start | bytes 9220
  988.0 95.6 %copy-start.77 = (f32[768]{0:T(1024)S(1)}, f32[768]{0:T(1024)}, u32[]{:S(2)}) copy-start(f32[768]{0:T(1024)} %get-tuple-element.1221) | copy-start | bytes 9220
  988.0 95.6 %copy-start.72 = (f32[768]{0:T(1024)S(1)}, f32[768]{0:T(1024)}, u32[]{:S(2)}) copy-start(f32[768]{0:T(1024)} %get-tuple-element.1211) | copy-start | bytes 9220
  988.0 95.6 %copy-start.76 = (f32[768]{0:T(1024)S(1)}, f32[768]{0:T(1024)}, u32[]{:S(2)}) copy-start(f32[768]{0:T(1024)} %get-tuple-element.1213) | copy-start | bytes 9220
  988.0 95.7 %copy-start.71 = (f32[768]{0:T(1024)S(1)}, f32[768]{0:T(1024)}, u32[]{:S(2)}) copy-start(f32[768]{0:T(1024)} %get-tuple-element.1098) | copy-start | bytes 9220
  988.0 95.7 %copy-start.75 = (f32[768]{0:T(1024)S(1)}, f32[768]{0:T(1024)}, u32[]{:S(2)}) copy-start(f32[768]{0:T(1024)} %get-tuple-element.1100) | copy-start | bytes 9220
  988.1 95.7 %copy-start.74 = (f32[768]{0:T(1024)S(1)}, f32[768]{0:T(1024)}, u32[]{:S(2)}) copy-start(f32[768]{0:T(1024)} %get-tuple-element.1106) | copy-start | bytes 9220
  988.1 95.7 %copy-start.78 = (f32[768]{0:T(1024)S(1)}, f32[768]{0:T(1024)}, u32[]{:S(2)}) copy-start(f32[768]{0:T(1024)} %get-tuple-element.1247) | copy-start | bytes 9220
  988.1 124.3 %copy-start.30 = (f32[1,522,768]{2,1,0:T(8,128)S(1)}, f32[1,522,768]{2,1,0:T(8,128)}, u32[]{:S(2)}) copy-start(f32[1,522,768]{2,1,0:T(8,128)} %add_bitcast_fusion) | copy-start | bytes 4810756
  (92 other events, 532.9 us)
Sparse Core Ops, SparseCore 0:
  18.8 23.0 all-gather.7
  44.1 22.4 all-gather.9
  68.2 22.5 all-gather.11
  92.3 22.5 all-gather.13
  116.3 51.1 all-gather.15
  169.0 49.8 all-gather.17
  552.9 35.8 reduce-scatter.26
  767.0 35.7 reduce-scatter.24
  805.1 35.9 reduce-scatter.22
  843.3 35.8 reduce-scatter.20
  881.5 98.3 reduce-scatter.32
  982.0 97.8 reduce-scatter.28
  1082.7 22.6 reduce-scatter.42
  1108.0 24.2 reduce-scatter.40
  1135.5 24.2 reduce-scatter.38
  1163.0 24.2 reduce-scatter.36
  1190.0 25.3 reduce-scatter.34
  1218.1 25.3 reduce-scatter.30
where the time goes:
time: 1260 us; the launch traced here: 1250 us
  waiting for transfers between devices  380 us (30%)
  other arithmetic  261 us (21%)
  matrix products  249 us (20%)
  local copies, waits for them, and re-layouts  203 us (16%)
  blocking collectives  135 us (11%)
  between operations  20.3 us (2%)
    sub x6, other arithmetic, group_step(): score_grad = (probs * (prob_grad - inner)).astype(jnp.bfloat16)  178 us
    reduce_scatter x1, waiting for transfers between devices, reduce_grads(): lax.psum_scatter(down_weight_grad, 'col', scatter_dimension=1, tiled=True)  97.1 us
    reduce_scatter x1, waiting for transfers between devices, reduce_grads(): lax.psum_scatter(up_weight_grad, 'col', scatter_dimension=1, tiled=True)  91.8 us
    dot_general x12, matrix products, product(): return jnp.dot(left, right, preferred_element_type=jnp.float32)  75.2 us
    unnamed x22, waiting for transfers between devices  53.9 us
    unnamed x2, blocking collectives  52.9 us
    dot_general x12, matrix products, product_left(): jnp.einsum('rd,re->de', left, right, preferred_element_type=jnp.float32)  50.7 us
    dot_general x6, local copies, waits for them, and re-layouts, group_step(): jnp.einsum('qgd,kgd->gqk', grad_part, value_part, preferred_element_type=...  50.3 us
  transfers between devices with their start and end apart: 18, of which 10 were waited for; matrix products, arithmetic and copies ran while one was open for 29% of the time, Pallas kernels for 0%

commit v1 on v0

v1 whole, which is shorter than its diff:
```python
import functools

import jax
import jax.numpy as jnp
from jax import lax
from jax.experimental import pallas as pl
from jax.experimental.pallas import tpu as pltpu
from jax.sharding import PartitionSpec as P

HEADS = 12
HEAD_DIM = 64
MEMORY = 10
TEXT = 502
PICTURE = 256
SEG_ROWS = 522
ROWS = 528
KEYS = 640
QUAD = 256
F32 = jnp.float32
BF16 = jnp.bfloat16

EPSILON = 1e-06
MASKED = -1e30
LOG2E = 1.4426950408889634

ERFC_SLOPE = 0.4 * 0.7071067811865476
ERFC_POLY = (0.22562816739082336, 0.2265406847000122, 0.20122945308685303, 0.19582846760749817, 0.07433333992958069, 0.09543049335479736, 0.07776277512311935, -0.1374378800392151, 0.040684547275304794)


def nn(left, right):
    return lax.dot_general(left, right, (((1,), (0,)), ((), ())), preferred_element_type=F32)


def nt(left, right):
    return lax.dot_general(left, right, (((1,), (1,)), ((), ())), preferred_element_type=F32)


def norm_forward(inputs, gain, shift):
    center = jnp.mean(inputs, axis=-1, keepdims=True)
    centred = inputs - center
    spread = jnp.mean(centred * centred, axis=-1, keepdims=True)
    inverse = lax.rsqrt(spread + EPSILON)
    normed = centred * inverse
    return normed * gain + shift, normed, inverse


def norm_backward(grad, normed, inverse, gain):
    scaled = grad * gain
    first = jnp.mean(scaled, axis=-1, keepdims=True)
    second = jnp.mean(scaled * normed, axis=-1, keepdims=True)
    return (scaled - first - normed * second) * inverse


def column_sum(values):
    return jnp.sum(values, axis=0, keepdims=True)


def gelu_pair(upward):
    size = jnp.abs(upward)
    t = 1.0 / (1.0 + ERFC_SLOPE * size)
    poly = jnp.full_like(t, ERFC_POLY[-1])
    for coefficient in ERFC_POLY[-2::-1]:
        poly = poly * t + coefficient
    bell = jnp.exp2(upward * upward * (-0.5 * LOG2E))
    tail = 0.5 * bell * t * poly
    phi = jnp.where(upward < 0.0, tail, 1.0 - tail)
    return upward * phi, phi + upward * (bell * 0.3989422804014327)


def attention_forward_kernel(
    info, x, wq, wk, wv, wo, vq, vv, vo, gain, shift,
    q_out, k_out, v_out, e_out, total_out, mixed_out, hidden_out, normed_out, inverse_out,
    narrow, bias, k_pad, v_pad, branch,
):
    step = pl.program_id(0)

    @pl.when(step == 0)
    def _():
        narrow[...] = x[...].astype(BF16)
        branch[...] = jnp.zeros_like(branch)
        total_out[...] = jnp.ones_like(total_out)
        k_pad[...] = jnp.zeros_like(k_pad)
        v_pad[...] = jnp.zeros_like(v_pad)
        length, start = info[0], info[1]
        row = lax.broadcasted_iota(jnp.int32, (ROWS, KEYS), 0)
        col = lax.broadcasted_iota(jnp.int32, (ROWS, KEYS), 1)
        low, high = start + MEMORY, start + MEMORY + PICTURE
        text = (col >= MEMORY) & (col < MEMORY + TEXT)
        usable = jnp.logical_not(text & (col >= MEMORY + length)) & (col < SEG_ROWS)
        inside = (row >= low) & (row < high) & (col >= low) & (col < high)
        allowed = usable & ((col <= row) | inside)
        bias[...] = jnp.where(allowed, 0.0, MASKED)

    xb = narrow[...]
    q = ((nt(xb, wq[...]) + vq[...]).astype(BF16).astype(F32) * HEAD_DIM**-0.5).astype(BF16)
    q_out[...] = q
    k_pad[:ROWS, :] = nt(xb, wk[...]).astype(BF16)
    v_pad[:ROWS, :] = (nt(xb, wv[...]) + vv[...]).astype(BF16)
    k_out[...] = k_pad[:ROWS, :]
    v_out[...] = v_pad[:ROWS, :]
    lane = lax.broadcasted_iota(jnp.int32, (ROWS, 128), 1)
    totals = total_out[...]
    for pair in range(2):
        at = slice(128 * pair, 128 * pair + 128)
        halves = []
        for half in range(2):
            mine = (lane < HEAD_DIM) if half == 0 else (lane >= HEAD_DIM)
            qm = jnp.where(mine, q_out[:, at], jnp.zeros((), BF16))
            scores = nt(qm, k_pad[:, at]) + bias[...]
            peak = jnp.max(scores, axis=-1, keepdims=True)
            expos = jnp.exp2((scores - peak) * LOG2E)
            total = jnp.sum(expos, axis=-1, keepdims=True)
            narrow_e = expos.astype(BF16)
            e_out[2 * pair + half] = narrow_e
            totals = jnp.where(lane == step * 4 + 2 * pair + half, total, totals)
            halves.append(nn(narrow_e, v_pad[:, at]) / total)
        mixed_out[:, at] = jnp.where(lane < HEAD_DIM, halves[0], halves[1]).astype(BF16)
    total_out[...] = totals
    branch[...] += nt(mixed_out[...], wo[...])

    @pl.when(step == pl.num_programs(0) - 1)
    def _():
        hidden, normed, inverse = norm_forward(
            x[...] + (branch[...] + vo[...]), gain[...], shift[...]
        )
        hidden_out[...] = hidden
        normed_out[...] = normed
        inverse_out[...] = jnp.broadcast_to(inverse, inverse_out.shape)


def whole(shape):
    return pl.BlockSpec(shape, lambda i: (0,) * len(shape))


def params(limit=58):
    return pltpu.CompilerParams(
        dimension_semantics=("arbitrary",), vmem_limit_bytes=limit * 1024 * 1024
    )


def attention_forward(info, x, weights):
    width = x.shape[1]
    steps = width // QUAD
    row_block = pl.BlockSpec((QUAD, width), lambda i: (i, 0))
    col_block = pl.BlockSpec((width, QUAD), lambda i: (0, i))
    bias_block = pl.BlockSpec((1, QUAD), lambda i: (0, i))
    rows_block = pl.BlockSpec((ROWS, QUAD), lambda i: (0, i))
    vector = whole((1, width))
    full = whole((ROWS, width))
    stats = whole((ROWS, 128))
    shape = jax.ShapeDtypeStruct
    return pl.pallas_call(
        attention_forward_kernel,
        grid=(steps,),
        in_specs=[
            pl.BlockSpec(memory_space=pltpu.SMEM),
            full, row_block, row_block, row_block, col_block,
            bias_block, bias_block, vector, vector, vector,
        ],
        out_specs=[
            rows_block, rows_block, rows_block,
            pl.BlockSpec((4, ROWS, KEYS), lambda i: (i, 0, 0)),
            stats, rows_block, full, full, stats,
        ],
        out_shape=[
            shape((ROWS, width), BF16), shape((ROWS, width), BF16), shape((ROWS, width), BF16),
            shape((HEADS, ROWS, KEYS), BF16),
            shape((ROWS, 128), F32), shape((ROWS, width), BF16),
            shape((ROWS, width), F32), shape((ROWS, width), F32), shape((ROWS, 128), F32),
        ],
        scratch_shapes=[
            pltpu.VMEM((ROWS, width), BF16),
            pltpu.VMEM((ROWS, KEYS), F32),
            pltpu.VMEM((KEYS, QUAD), BF16),
            pltpu.VMEM((KEYS, QUAD), BF16),
            pltpu.VMEM((ROWS, width), F32),
        ],
        compiler_params=params(),
        name="attention_forward",
    )(
        info, x, weights["q"], weights["k"], weights["v"], weights["o"],
        weights["vq"], weights["vv"], weights["vo"], weights["ag"], weights["as"],
    )


def feed_forward_kernel(
    hidden, wu, wd, vu, vd, gain, shift, act_out, slope_out, y_out, normed_out, inverse_out,
    narrow, total,
):
    step = pl.program_id(0)

    @pl.when(step == 0)
    def _():
        narrow[...] = hidden[...].astype(BF16)
        total[...] = jnp.zeros_like(total)

    upward = nt(narrow[...], wu[...]) + vu[...]
    act, slope = gelu_pair(upward)
    act_out[...] = act.astype(BF16)
    slope_out[...] = slope.astype(BF16)
    total[...] += nt(act_out[...], wd[...])

    @pl.when(step == pl.num_programs(0) - 1)
    def _():
        y, normed, inverse = norm_forward(
            hidden[...] + (total[...] + vd[...]), gain[...], shift[...]
        )
        y_out[...] = y
        normed_out[...] = normed
        inverse_out[...] = jnp.broadcast_to(inverse, inverse_out.shape)


UNITS = 512


def feed_forward(hidden, weights):
    width = hidden.shape[1]
    units = weights["u"].shape[0]
    vector = whole((1, width))
    full = whole((ROWS, width))
    block = pl.BlockSpec((ROWS, UNITS), lambda i: (0, i))
    shape = jax.ShapeDtypeStruct
    return pl.pallas_call(
        feed_forward_kernel,
        grid=(units // UNITS,),
        in_specs=[
            full,
            pl.BlockSpec((UNITS, width), lambda i: (i, 0)),
            pl.BlockSpec((width, UNITS), lambda i: (0, i)),
            pl.BlockSpec((1, UNITS), lambda i: (0, i)),
            vector, vector, vector,
        ],
        out_specs=[block, block, full, full, whole((ROWS, 128))],
        out_shape=[
            shape((ROWS, units), BF16), shape((ROWS, units), BF16),
            shape((ROWS, width), F32), shape((ROWS, width), F32), shape((ROWS, 128), F32),
        ],
        scratch_shapes=[pltpu.VMEM((ROWS, width), BF16), pltpu.VMEM((ROWS, width), F32)],
        compiler_params=params(),
        name="feed_forward",
    )(
        hidden, weights["u"], weights["d"], weights["vu"], weights["vd"],
        weights["og"], weights["os"],
    )


def feed_backward_kernel(
    dy, normed2, inverse2, normed1, inverse1, slope, wd, wu, wo, gain2, gain1,
    gd_out, gu_out, gb_out, dfirst_out, gm_out, vu_out, sums_out,
    dsecond, dhidden,
):
    step = pl.program_id(0)

    @pl.when(step == 0)
    def _():
        grad, normed = dy[...], normed2[...]
        sums_out[0:1, :] = column_sum(grad * normed)
        sums_out[1:2, :] = column_sum(grad)
        second = norm_backward(grad, normed, inverse2[:, 0:1], gain2[...])
        dsecond[...] = second
        narrow = second.astype(BF16)
        gd_out[...] = narrow
        sums_out[2:3, :] = column_sum(narrow.astype(F32))
        dhidden[...] = jnp.zeros_like(dhidden)

    up = (nn(gd_out[...], wd[...]) * slope[...].astype(F32)).astype(BF16)
    gu_out[...] = up
    vu_out[...] = column_sum(up.astype(F32))
    dhidden[...] += nn(up, wu[...])

    @pl.when(step == pl.num_programs(0) - 1)
    def _():
        grad, normed = dhidden[...] + dsecond[...], normed1[...]
        sums_out[3:4, :] = column_sum(grad * normed)
        sums_out[4:5, :] = column_sum(grad)
        first = norm_backward(grad, normed, inverse1[:, 0:1], gain1[...])
        dfirst_out[...] = first
        narrow = first.astype(BF16)
        gb_out[...] = narrow
        sums_out[5:6, :] = column_sum(narrow.astype(F32))
        sums_out[6:8, :] = jnp.zeros((2, narrow.shape[1]), F32)
        gm_out[...] = nn(narrow, wo[...]).astype(BF16)


def feed_backward(dy, saved, weights):
    width = dy.shape[1]
    units = weights["u"].shape[0]
    vector = whole((1, width))
    full = whole((ROWS, width))
    stats = whole((ROWS, 128))
    block = pl.BlockSpec((ROWS, UNITS), lambda i: (0, i))
    shape = jax.ShapeDtypeStruct
    return pl.pallas_call(
        feed_backward_kernel,
        grid=(units // UNITS,),
        in_specs=[
            full, full, stats, full, stats, block,
            pl.BlockSpec((width, UNITS), lambda i: (0, i)),
            pl.BlockSpec((UNITS, width), lambda i: (i, 0)),
            whole((width, width)), vector, vector,
        ],
        out_specs=[
            full, block, full, full, full,
            pl.BlockSpec((1, UNITS), lambda i: (0, i)), whole((8, width)),
        ],
        out_shape=[
            shape((ROWS, width), BF16), shape((ROWS, units), BF16), shape((ROWS, width), BF16),
            shape((ROWS, width), F32), shape((ROWS, width), BF16),
            shape((1, units), F32), shape((8, width), F32),
        ],
        scratch_shapes=[pltpu.VMEM((ROWS, width), F32), pltpu.VMEM((ROWS, width), F32)],
        compiler_params=params(),
        name="feed_backward",
    )(
        dy, saved["normed2"], saved["inverse2"], saved["normed1"], saved["inverse1"],
        saved["slope"], weights["d"], weights["u"], weights["o"], weights["og"], weights["ag"],
    )


def attention_backward_kernel(
    q, k, v, e, total, mixed, gm, dfirst, wq, wk, wv,
    gq_out, gk_out, gv_out, dx_out, vq_out, vv_out,
    k_pad, v_pad,
):
    step = pl.program_id(0)

    @pl.when(step == 0)
    def _():
        dx_out[...] = dfirst[...]
        k_pad[...] = jnp.zeros_like(k_pad)
        v_pad[...] = jnp.zeros_like(v_pad)

    k_pad[:ROWS, :] = k[...]
    v_pad[:ROWS, :] = v[...]
    lane = lax.broadcasted_iota(jnp.int32, (ROWS, 128), 1)
    for pair in range(2):
        at = slice(128 * pair, 128 * pair + 128)
        grad = gm[:, at].astype(F32)
        product = grad * mixed[:, at].astype(F32)
        totals = total[...]
        rates, inners = [], []
        for half in range(2):
            mine = (lane < HEAD_DIM) if half == 0 else (lane >= HEAD_DIM)
            head = step * 4 + 2 * pair + half
            rate = 1.0 / jnp.sum(jnp.where(lane == head, totals, 0.0), axis=-1, keepdims=True)
            rates.append(rate)
            inners.append(jnp.sum(jnp.where(mine, product, 0.0), axis=-1, keepdims=True) * rate)
        scaled = (grad * jnp.where(lane < HEAD_DIM, rates[0], rates[1])).astype(BF16)
        scaled_t = scaled.T
        query_t = q[:, at].T
        gq, gk, gv = [], [], []
        for half in range(2):
            mine = (lane < HEAD_DIM) if half == 0 else (lane >= HEAD_DIM)
            rows = slice(HEAD_DIM * half, HEAD_DIM * half + HEAD_DIM)
            gmm = jnp.where(mine, scaled, jnp.zeros((), BF16))
            dp = nt(gmm, v_pad[:, at])
            narrow_e = e[2 * pair + half]
            ds = (narrow_e.astype(F32) * (dp - inners[half])).astype(BF16)
            gq.append(nn(ds, k_pad[:, at]))
            gk.append(nn(query_t[rows, :], ds))
            gv.append(nn(scaled_t[rows, :], narrow_e))
        gq_pair = jnp.where(lane < HEAD_DIM, gq[0], gq[1]) * HEAD_DIM**-0.5
        gq_out[:, at] = gq_pair.astype(BF16)
        gk_out[:, at] = jnp.concatenate(gk, axis=0).T[:ROWS].astype(BF16)
        gv_out[:, at] = jnp.concatenate(gv, axis=0).T[:ROWS].astype(BF16)
    vq_out[...] = column_sum(gq_out[...].astype(F32))
    vv_out[...] = column_sum(gv_out[...].astype(F32))
    dx_out[...] += (
        nn(gq_out[...], wq[...]) + nn(gk_out[...], wk[...]) + nn(gv_out[...], wv[...])
    )


def attention_backward(saved, gm, dfirst, weights):
    width = dfirst.shape[1]
    row_block = pl.BlockSpec((QUAD, width), lambda i: (i, 0))
    rows_block = pl.BlockSpec((ROWS, QUAD), lambda i: (0, i))
    full = whole((ROWS, width))
    sums = pl.BlockSpec((1, QUAD), lambda i: (0, i))
    shape = jax.ShapeDtypeStruct
    return pl.pallas_call(
        attention_backward_kernel,
        grid=(width // QUAD,),
        in_specs=[
            rows_block, rows_block, rows_block,
            pl.BlockSpec((4, ROWS, KEYS), lambda i: (i, 0, 0)),
            whole((ROWS, 128)), rows_block, rows_block, full, row_block, row_block, row_block,
        ],
        out_specs=[rows_block, rows_block, rows_block, full, sums, sums],
        out_shape=[
            shape((ROWS, width), BF16), shape((ROWS, width), BF16), shape((ROWS, width), BF16),
            shape((ROWS, width), F32), shape((1, width), F32), shape((1, width), F32),
        ],
        scratch_shapes=[pltpu.VMEM((KEYS, QUAD), BF16), pltpu.VMEM((KEYS, QUAD), BF16)],
        compiler_params=params(),
        name="attention_backward",
    )(
        saved["q"], saved["k"], saved["v"], saved["e"], saved["total"], saved["mixed"],
        gm, dfirst, weights["q"], weights["k"], weights["v"],
    )


def gather_all(part):
    return lax.all_gather(part, ("row", "col"), axis=0, tiled=False)


def fetch(arguments):
    matrices, vectors = arguments[:6], arguments[6:]
    rows, cols = lax.axis_size("row"), lax.axis_size("col")
    depth, across = matrices[0].shape
    width = depth * rows
    names = ("q", "k", "v", "o")
    square = jnp.concatenate([item.T for item in matrices[:4]], axis=1)
    upper = matrices[4].T.reshape(4, across, depth).transpose(1, 0, 2).reshape(across, 4 * depth)
    lower = matrices[5].T
    line = jnp.concatenate(vectors)
    extra = -(-line.shape[0] // (4 * depth))
    extra += -(across + extra) % 16
    line = jnp.pad(line, (0, extra * 4 * depth - line.shape[0])).reshape(extra, 4 * depth)
    first = gather_all(jnp.concatenate([square, line], axis=0))
    second = gather_all(upper)
    third = gather_all(lower)
    whole_square = (
        first[:, :across].reshape(rows, cols, across, 4, depth)
        .transpose(3, 1, 2, 0, 4).reshape(4, width, width)
    )
    weights = {name: whole_square[at] for at, name in enumerate(names)}
    weights["u"] = (
        second.reshape(rows, cols, across, 4, depth)
        .transpose(1, 3, 2, 0, 4).reshape(4 * width, width)
    )
    weights["d"] = third.reshape(rows, cols, across, 4 * depth).transpose(1, 2, 0, 3).reshape(width, 4 * width)
    lines = first[:cols, across:].reshape(cols, -1).astype(F32)
    at = 0
    for name, item in zip(("vq", "vv", "vo", "ag", "as", "vu", "vd", "og", "os"), vectors):
        weights[name] = lines[:, at : at + item.shape[0]].reshape(1, -1)
        at += item.shape[0]
    return weights


def scatter_all(terms):
    return lax.psum_scatter(terms, ("row", "col"), scatter_dimension=0, tiled=False)


def product_t(left, right):
    return jnp.einsum("rd,re->de", left, right, preferred_element_type=F32).astype(BF16)


def solution_body(
    text, memory, tail_lengths, picture_starts, grad_out, *parameters
):
    rows, cols = lax.axis_size("row"), lax.axis_size("col")
    depth, across = parameters[0].shape
    width = depth * rows
    weights = fetch(parameters)
    full_length = jnp.full((1,), TEXT, jnp.int32)
    pad = jnp.zeros((ROWS - SEG_ROWS, width), F32)

    def forward(edge, words, length, start):
        info = jnp.concatenate([length, start])
        x = jnp.concatenate([edge, words.astype(F32), edge, pad], axis=0)
        q, k, v, e, total, mixed, hidden, normed1, inverse1 = attention_forward(info, x, weights)
        act, slope, y, normed2, inverse2 = feed_forward(hidden, weights)
        saved = dict(
            x=x.astype(BF16), q=q, k=k, v=v, e=e, total=total, mixed=mixed, hidden=hidden.astype(BF16),
            normed1=normed1, inverse1=inverse1, act=act, slope=slope, normed2=normed2, inverse2=inverse2,
        )
        return y, saved

    y1, saved1 = forward(memory[0].astype(F32), text[0, 0], full_length, picture_starts[:, 0])
    y2, saved2 = forward(y1[MEMORY + TEXT : SEG_ROWS], text[0, 1], tail_lengths, picture_starts[:, 1])
    layer_output = jnp.stack([y1[:SEG_ROWS], y2[:SEG_ROWS]]).astype(BF16)[None]

    def backward(dy, saved):
        gd, gu, gb, dfirst, gm, vu, sums = feed_backward(dy, saved, weights)
        gq, gk, gv, dx, vq, vv = attention_backward(saved, gm, dfirst, weights)
        return dx, dict(gd=gd, gu=gu, gb=gb, gq=gq, gk=gk, gv=gv, vu=vu, sums=sums, vq=vq, vv=vv)

    cotangent = jnp.pad(grad_out[0].astype(F32), ((0, 0), (0, ROWS - SEG_ROWS), (0, 0)))
    dx2, grads2 = backward(cotangent[1], saved2)
    edge = dx2[:MEMORY] + dx2[MEMORY + TEXT : SEG_ROWS]
    dy1 = cotangent[0].at[MEMORY + TEXT : SEG_ROWS].add(edge)
    dx1, grads1 = backward(dy1, saved1)
    memory_grad = (dx1[:MEMORY] + dx1[MEMORY + TEXT : SEG_ROWS]).astype(BF16)[None]
    text_grad = jnp.stack(
        [dx1[MEMORY : MEMORY + TEXT], dx2[MEMORY : MEMORY + TEXT]]
    ).astype(BF16)[None]

    def both(name):
        return jnp.concatenate([grads1[name], grads2[name]], axis=0)

    def kept(name):
        return jnp.concatenate([saved1[name], saved2[name]], axis=0)

    lower = product_t(both("gd"), kept("act"))
    lower = lower.reshape(cols, across, rows, 4 * depth).transpose(2, 0, 1, 3)
    lower = scatter_all(lower.reshape(rows * cols, across, 4 * depth))
    upper = product_t(both("gu"), kept("hidden"))
    upper = upper.reshape(cols, 4, across, rows, depth).transpose(3, 0, 2, 1, 4)
    upper = scatter_all(upper.reshape(rows * cols, across, 4 * depth))
    xb = kept("x")
    square = jnp.stack(
        [
            product_t(both("gq"), xb), product_t(both("gk"), xb), product_t(both("gv"), xb),
            product_t(both("gb"), kept("mixed")),
        ]
    )
    square = square.reshape(4, cols, across, rows, depth).transpose(3, 1, 2, 0, 4)
    sums = grads1["sums"] + grads2["sums"]
    vectors = (
        grads1["vq"] + grads2["vq"], grads1["vv"] + grads2["vv"], sums[5], sums[3], sums[4],
        grads1["vu"] + grads2["vu"], sums[2], sums[0], sums[1],
    )
    lines = jnp.concatenate([item.reshape(cols, -1) for item in vectors], axis=1)
    count = lines.shape[1]
    extra = -(-count // (4 * depth))
    extra += -(across + extra) % 16
    lines = jnp.pad(lines, ((0, 0), (0, extra * 4 * depth - count))).astype(BF16)
    lines = jnp.broadcast_to(lines.reshape(1, cols, extra, 4 * depth), (rows, cols, extra, 4 * depth))
    square = jnp.concatenate([square.reshape(rows, cols, across, 4 * depth), lines], axis=2)
    square = scatter_all(square.reshape(rows * cols, across + extra, 4 * depth))
    own = square[:across].astype(F32).reshape(across, 4, depth)
    line = square[across:].astype(F32).reshape(-1)
    result = [own[:, at].T for at in range(4)]
    upper = upper.astype(F32).reshape(across, 4, depth).transpose(2, 1, 0).reshape(depth, 4 * across)
    result += [upper, lower.astype(F32).T]
    at = 0
    for item in vectors:
        size = item.size // cols
        result.append(line[at : at + size])
        at += size
    return (layer_output, text_grad, memory_grad, *result)


def solution(mesh):
    batch, matrix, vector = P(("row", "col")), P("row", "col"), P("col")
    return jax.shard_map(
        solution_body,
        mesh=mesh,
        in_specs=(batch,) * 5 + (matrix,) * 6 + (vector,) * 9,
        out_specs=(batch,) * 3 + (matrix,) * 6 + (vector,) * 9,
        check_vma=False,
    )
```

time: 1260 us -> 825 us (0.65)
  other arithmetic: 261 us -> 42.1 us
  matrix products: 249 us -> 36.1 us
  Pallas kernels: 0 us -> 143 us
  blocking collectives: 135 us -> 0 us
  waiting for transfers between devices: 380 us -> 328 us
  local copies, waits for them, and re-layouts: 203 us -> 250 us
    dot_general x78 -> x6, matrix products: 249 us -> 36.1 us  [product_t(): jnp.einsum('rd,re->de', left, right, preferred_element_type=F32)]
    sub x6 -> x0, other arithmetic: 178 us -> none  [group_step(): score_grad = (probs * (prob_grad - inner)).astype(jnp.bfloat16)]
    pallas_call x0 -> x8, Pallas kernels: none -> 143 us  [the longest x2 36.7 us: attention_backward(): pl.pallas_call(attention_backward_kernel, grid=(width // QUAD,), in_specs...]
    all_gather x6 -> x3, waiting for transfers between devices: 18.4 us -> 136 us  [gather_all(): return lax.all_gather(part, ('row', 'col'), axis=0, tiled=False)]
    reduce_scatter x8 -> x3, waiting for transfers between devices: 308 us -> 191 us  [scatter_all(): lax.psum_scatter(terms, ('row', 'col'), scatter_dimension=0, tiled=False)]
    dot_general x12 -> x0, local copies, waits for them, and re-layouts: 100 us -> none  [the longest x6 50.3 us: group_step(): jnp.einsum('qgd,kgd->gqk', grad_part, value_part, preferred_element_type=...]
    reshape x0 -> x25, local copies, waits for them, and re-layouts: none -> 97.9 us  [the longest x2 23.7 us: solution_body(): upper = upper.reshape(cols, 4, across, rows, depth).transpose(3, 0, 2, 1, 4)]
    all_gather x7 -> x0, blocking collectives: 71.7 us -> none  [the longest x1 13.1 us: fetch(): lax.all_gather(up_bias, 'col', axis=0, tiled=True)]
  transfers between devices with their start and end apart: 18 -> 6, of which waited for: 10 -> 5; matrix products, arithmetic and copies ran while one was open for 29% -> 23% of each run, Pallas kernels for 0% -> 2%
where the time goes in v1:
time: 825 us; the launch traced here: 814 us
  waiting for transfers between devices  328 us (40%)
  local copies, waits for them, and re-layouts  250 us (30%)
  Pallas kernels  143 us (17%)
  other arithmetic  42.1 us (5%)
  matrix products  36.1 us (4%)
  between operations  15.5 us (2%)
    reduce_scatter x3, waiting for transfers between devices, scatter_all(): lax.psum_scatter(terms, ('row', 'col'), scatter_dimension=0, tiled=False)  191 us
    all_gather x3, waiting for transfers between devices, gather_all(): return lax.all_gather(part, ('row', 'col'), axis=0, tiled=False)  136 us
    slice x5, local copies, waits for them, and re-layouts, fetch(): weights = {name: whole_square[at] for at, name in enumerate(names)}  38 us
    pallas_call x2, Pallas kernels, attention_backward(): pl.pallas_call(attention_backward_kernel, grid=(width // QUAD,), in_specs...  36.7 us
    dot_general x6, matrix products, product_t(): jnp.einsum('rd,re->de', left, right, preferred_element_type=F32)  36.1 us
    pallas_call x2, Pallas kernels, attention_forward(): pl.pallas_call(attention_forward_kernel, grid=(steps,), in_specs=[pl.Bloc...  36.1 us
    pallas_call x2, Pallas kernels, feed_forward(): pl.pallas_call(feed_forward_kernel, grid=(units // UNITS,), in_specs=[ful...  35.9 us
    pallas_call x2, Pallas kernels, feed_backward(): pl.pallas_call(feed_backward_kernel, grid=(units // UNITS,), in_specs=[fu...  33.9 us
  transfers between devices with their start and end apart: 6, of which 5 were waited for; matrix products, arithmetic and copies ran while one was open for 23% of the time, Pallas kernels for 2%

profile of v1, /device:TPU:0, one launch (start us, length us, event | category | flops | bytes accessed | tf_op | source)
XLA Modules:
  0.0 814.2 jit_solution(9420296169485494605)
XLA Ops:
  10.2 6.1 concatenate.85
  23.3 1.9 fusion.14
  26.1 2.2 fusion.72
  28.6 1.4 maximum_maximum_fusion.x
  30.0 47.4 %all-gather.10.cloned.1.call-done = bf16[3072,768]{1,0:T(8,128)(2,1)} async-done(((bf16[96,768]{1,0:T(8,128)(2,1)}), bf16[3072,768]{1,0:T(8,128)(2,1)}) %all-gather.10.cloned.1.call-update) | async-done | bytes 4718608 | tf_op jit(solution)/shard_map/all_gather | solution.py:403
  77.4 6.0 copy.113
  83.4 3.2 copy.134
  86.7 56.3 %all-gather.6.cloned.1.call-done = bf16[32,96,768]{2,1,0:T(8,128)(2,1)} async-done(((bf16[1,96,768]{2,1,0:T(8,128)(2,1)}), bf16[32,96,768]{2,1,0:T(8,128)(2,1)}) %all-gather.6.cloned.1.call-update) | async-done | bytes 4718608 | tf_op jit(solution)/shard_map/all_gather | solution.py:403
  143.0 13.1 %reshape.269 = bf16[4,8,96,4,192]{4,3,2,1,0:T(4,128)(2,1)} reshape(bf16[32,96,768]{2,1,0:T(8,128)(2,1)} %all-gather.6.cloned.1.call-done) | data formatting | bytes 9437184 | tf_op jit(solution)/shard_map/reshape | solution.py:428
  156.1 11.5 %copy.112 = bf16[8,4,96,4,192]{4,3,2,1,0:T(4,128)(2,1)} copy(bf16[8,4,96,4,192]{4,1,2,0,3:T(4,128)(2,1)} %bitcast.97) | data formatting | bytes 9437184 | tf_op jit(solution)/shard_map/transpose | solution.py:429
  167.6 11.6 %reshape.270.wu = bf16[3072,768]{1,0:T(8,128)(2,1)} reshape(bf16[8,4,96,4,192]{4,3,2,1,0:T(4,128)(2,1)} %copy.112) | data formatting | bytes 9437184 | tf_op jit(solution)/shard_map/reshape | solution.py:429
  179.2 32.1 %all-gather.8.cloned.1.call-done = bf16[3584,768]{1,0:T(8,128)(2,1)} async-done(((bf16[112,768]{1,0:T(8,128)(2,1)}), bf16[3584,768]{1,0:T(8,128)(2,1)}) %all-gather.8.cloned.1.call-update) | async-done | bytes 5505040 | tf_op jit(solution)/shard_map/all_gather | solution.py:403
  212.2 4.9 slice.242
  223.3 12.9 %reshape.262 = bf16[4,8,96,4,192]{4,3,2,1,0:T(4,128)(2,1)} reshape(bf16[32,96,768]{2,1,0:T(8,128)(2,1)} %slice.242) | data formatting | bytes 9437184 | tf_op jit(solution)/shard_map/reshape | solution.py:423
  236.2 19.6 %fusion.71 = (bf16[1,8,96,4,192]{4,0,2,1,3:T(2,128)(2,1)S(1)}, bf16[1,8,96,4,192]{4,0,2,1,3:T(2,128)(2,1)}, bf16[1,8,96,4,192]{4,0,2,1,3:T(2,128)(2,1)}, bf16[1,8,96,4,192]{4,0,2,1,3:T(2,128)(2,1)}) fusion(bf16[4,8,96,4,192]{4,0,2,1,3:T(4,128)(2,1)} %bitcast.96), kind=kLoop, calls=%fused_computation.99 | loop fusion | bytes 9437184 | tf_op jit(solution)/shard_map/slice | solution.py:426
  255.9 3.2 copy.110
  259.0 4.0 squeeze.44.wo
  263.0 5.1 copy.109
  268.1 4.0 squeeze.43.wv
  272.1 5.1 copy.108
  277.2 4.0 squeeze.42.wk
  281.2 5.1 copy.107
  286.2 4.2 squeeze.41.wq
  290.4 17.9 %attention_forward.2 = (bf16[528,768]{1,0:T(8,128)(2,1)}, bf16[528,768]{1,0:T(8,128)(2,1)}, bf16[528,768]{1,0:T(8,128)(2,1)}, bf16[12,528,640]{2,1,0:T(8,128)(2,...) custom-call(s32[2]{0:T(128)} %pad_add_fusion.info, ...), custom_call_target="tpu_custom_call" | custom-call | tf_op jit(solution)/shard_map/attention_forward/pallas_call | solution.py:152
  308.3 2.4 convert_element_type.128
  310.7 17.9 %feed_forward.2 = (bf16[528,3072]{1,0:T(8,128)(2,1)}, bf16[528,3072]{1,0:T(8,128)(2,1)}, f32[528,768]{1,0:T(8,128)}, f32[528,768]{1,0:T(8,128)}, f32[528,128]{1,0:T(8,128)}) custom-call(f32[528,768]{1,0:T(8,128)} %get-tuple-element.84.hidden, bf16[3072,768]{1,0:T(8,128)(2,1)} %reshape.270.wu, bf16[768,3072]{1,0:T(8,128)(2,1)} %bitcast.92, ...), custom_call_target="tpu_custom_call" | custom-call | tf_op jit(solution)/shard_map/feed_forward/pallas_call | solution.py:223
  329.5 1.4 maximum_maximum_fusion.1.x
  330.9 18.2 %attention_forward.3 = (bf16[528,768]{1,0:T(8,128)(2,1)}, bf16[528,768]{1,0:T(8,128)(2,1)}, bf16[528,768]{1,0:T(8,128)(2,1)}, bf16[12,528,640]{2,1,0:T(8,128)(2,...) custom-call(s32[2]{0:T(128)} %pad_add_fusion.1.info, ...), custom_call_target="tpu_custom_call" | custom-call | tf_op jit(solution)/shard_map/attention_forward/pallas_call | solution.py:152
  349.1 2.4 convert_element_type.129
  351.5 17.9 %feed_forward.3 = (bf16[528,3072]{1,0:T(8,128)(2,1)}, bf16[528,3072]{1,0:T(8,128)(2,1)}, f32[528,768]{1,0:T(8,128)}, f32[528,768]{1,0:T(8,128)}, f32[528,128]{1,0:T(8,128)}) custom-call(f32[528,768]{1,0:T(8,128)} %get-tuple-element.86.hidden, bf16[3072,768]{1,0:T(8,128)(2,1)} %reshape.270.wu, bf16[768,3072]{1,0:T(8,128)(2,1)} %bitcast.93, ...), custom_call_target="tpu_custom_call" | custom-call | tf_op jit(solution)/shard_map/feed_forward/pallas_call | solution.py:223
  369.4 16.9 %feed_backward.2 = (bf16[528,768]{1,0:T(8,128)(2,1)}, bf16[528,3072]{1,0:T(8,128)(2,1)}, bf16[528,768]{1,0:T(8,128)(2,1)}, f32[528,768]{1,0:T(8,128)}, bf16[528,...) custom-call(f32[528,768]{1,0:T(8,128)} %get-tuple-element.221.dy, f32[528,768]{1,0:T(8,128)} %get-tuple-element.100.normed2, ...), custom_call_target="tpu_custom_call" | custom-call | tf_op jit(solution)/shard_map/feed_backward/pallas_call | solution.py:293
  386.3 18.2 %attention_backward.2 = (bf16[528,768]{1,0:T(8,128)(2,1)}, bf16[528,768]{1,0:T(8,128)(2,1)}, bf16[528,768]{1,0:T(8,128)(2,1)}, f32[528,768]{1,0:T(8,128)}, f32[1,768]{1,0:T(1,128)}, /*index=5*/f32[1,768]{1,0:T(1,128)}) custom-call(bf16[528,768]{1,0:T(8,128)(2,1)} %get-tuple-element.94.q, bf16[528,768]{1,0:T(8,128)(2,1)} %get-tuple-element.95.k, ...), custom_call_target="tpu_custom_call" | custom-call | tf_op jit(solution)/shard_map/attention_backward/pallas_call | solution.py:380
  405.4 1.4 scatter-add.4.dy
  406.8 17.0 %feed_backward.3 = (bf16[528,768]{1,0:T(8,128)(2,1)}, bf16[528,3072]{1,0:T(8,128)(2,1)}, bf16[528,768]{1,0:T(8,128)(2,1)}, f32[528,768]{1,0:T(8,128)}, bf16[528,...) custom-call(f32[528,768]{1,0:T(8,128)} %scatter-add.4.dy, f32[528,768]{1,0:T(8,128)} %get-tuple-element.108.normed2, ...), custom_call_target="tpu_custom_call" | custom-call | tf_op jit(solution)/shard_map/feed_backward/pallas_call | solution.py:293
  423.9 10.0 %fusion.11 = bf16[3072,768]{1,0:T(8,128)(2,1)} fusion(bf16[528,3072]{1,0:T(8,128)(2,1)} %get-tuple-element.133, bf16[528,3072]{1,0:T(8,128)(2,1)} %get-tuple-element.132, bf16[528,768]{1,0:T(8,128)(2,1)S(1)} %copy-done.5, bf16[528,768]{1,0:T(8,128)(2,1)S(1)} %copy-done.4), kind=kOutput, calls=%fused_computation.12 | convolution fusion | flops 5001412608 | bytes 12828672 | tf_op jit(solution)/shard_map/rd,re->de/dot_general | solution.py:445
  433.9 13.0 %reshape.281 = bf16[8,4,96,4,192]{4,3,2,1,0:T(4,128)(2,1)} reshape(bf16[3072,768]{1,0:T(8,128)(2,1)} %fusion.11) | data formatting | bytes 9437184 | tf_op jit(solution)/shard_map/reshape | solution.py:498
  446.9 10.7 %copy.144 = bf16[8,4,96,4,192]{4,1,2,0,3:T(4,128)(2,1)} copy(bf16[8,4,96,4,192]{4,3,2,1,0:T(4,128)(2,1)} %reshape.281) | data formatting | bytes 9437184 | tf_op jit(solution)/shard_map/reshape | solution.py:498
  457.6 11.6 %reshape.282 = bf16[32,96,768]{2,1,0:T(8,128)(2,1)} reshape(bf16[4,8,96,4,192]{4,3,2,1,0:T(4,128)(2,1)} %bitcast.98) | data formatting | bytes 9437184 | tf_op jit(solution)/shard_map/reshape | solution.py:499
  469.3 10.4 %fusion.8 = bf16[768,3072]{1,0:T(8,128)(2,1)} fusion(bf16[528,3072]{1,0:T(8,128)(2,1)} %get-tuple-element.137, bf16[528,3072]{1,0:T(8,128)(2,1)} %get-tuple-element.136, bf16[528,768]{1,0:T(8,128)(2,1)} %get-tuple-element.135, bf16[528,768]{1,0:T(8,128)(2,1)} %get-tuple-element.134), kind=kOutput, calls=%fused_computation.11 | convolution fusion | flops 5001412608 | bytes 12828672 | tf_op jit(solution)/shard_map/rd,re->de/dot_general | solution.py:445
  479.7 9.8 %reshape.285 = bf16[8,96,4,768]{3,2,1,0:T(4,128)(2,1)} reshape(bf16[768,3072]{1,0:T(8,128)(2,1)} %fusion.8) | data formatting | bytes 9437184 | tf_op jit(solution)/shard_map/reshape | solution.py:495
  489.5 5.4 copy.127
  495.7 18.5 %attention_backward.3 = (bf16[528,768]{1,0:T(8,128)(2,1)}, bf16[528,768]{1,0:T(8,128)(2,1)}, bf16[528,768]{1,0:T(8,128)(2,1)}, f32[528,768]{1,0:T(8,128)}, f32[1,768]{1,0:T(1,128)}, /*index=5*/f32[1,768]{1,0:T(1,128)}) custom-call(bf16[528,768]{1,0:T(8,128)(2,1)} %get-tuple-element.88.q, bf16[528,768]{1,0:T(8,128)(2,1)} %get-tuple-element.89.k, ...), custom_call_target="tpu_custom_call" | custom-call | tf_op jit(solution)/shard_map/attention_backward/pallas_call | solution.py:380
  518.9 1.8 fusion.41
  520.6 1.4 stack.41
  522.1 4.7 fusion.44
  526.7 3.5 stack.40
  530.2 4.7 fusion.47
  534.9 4.6 stack.39
  539.4 4.6 fusion.50
  544.1 4.4 stack.42
  548.5 4.9 copy.119
  553.4 3.3 copy.116
  556.7 3.3 copy.117
  560.0 3.3 copy.118
  563.4 17.6 %maximum_bitcast_fusion = bf16[4,8,96,4,192]{4,3,2,1,0:T(4,128)(2,1)} fusion(bf16[1,8,96,4,192]{4,0,2,1,3:T(2,128)(2,1)S(1)} %copy.119, bf16[1,8,96,4,192]{4,0,2,1,3:T(2,128)(2,1)S(1)} %copy.118, bf16[1,8,96,4,192]{4,0,2,1,3:T(2,128)(2,1)S(1)} %copy.117, bf16[1,8,96,4,192]{4,0,2,1,3:T(2,128)(2,1)S(1)} %copy.116), kind=kLoop, calls=%fused_computation.8 | loop fusion | flops 18874368 | bytes 9437184 | tf_op jit(solution)/shard_map/transpose | solution.py:507
  580.9 11.7 %concatenate.95 = bf16[32,96,768]{2,1,0:T(8,128)(2,1)} reshape(bf16[4,8,96,4,192]{4,3,2,1,0:T(4,128)(2,1)} %maximum_bitcast_fusion) | data formatting | bytes 9437184 | tf_op jit(solution)/shard_map/concatenate | solution.py:519
  592.7 5.2 pad_maximum_fusion
  597.9 1.4 copy-done.9
  601.1 2.4 copy.128
  603.4 1.6 fusion.58
  605.3 2.3 copy.129
  610.7 77.3 %reduce-scatter.8.cloned.1.call-done = bf16[1,96,768]{2,1,0:T(8,128)(2,1)} async-done(((bf16[32,96,768]{2,1,0:T(8,128)(2,1)}), bf16[1,96,768]{2,1,0:T(8,128)(2,1)}) %reduce-scatter.8.cloned.1.call-update) | async-done | bytes 147472 | tf_op jit(solution)/shard_map/reduce_scatter | solution.py:441
  687.9 1.6 convert_bitcast_fusion.1
  689.6 113.7 %reduce-scatter.4.cloned.1.call-done = bf16[1,112,768]{2,1,0:T(8,128)(2,1)} async-done(((bf16[32,112,768]{2,1,0:T(8,128)(2,1)}), bf16[1,112,768]{2,1,0:T(8,128)(2,1)}) %reduce-scatter.4.cloned.1.call-update) | async-done | bytes 172048 | tf_op jit(solution)/shard_map/reduce_scatter | solution.py:441
  (126 shorter events, 33.5 us)
Async XLA Ops:
  7.2 11.0 %copy-start.11 = (bf16[192,96]{1,0:T(8,128)(2,1)S(1)}, bf16[192,96]{1,0:T(8,128)(2,1)}, u32[]{:S(2)}) copy-start(bf16[192,96]{1,0:T(8,128)(2,1)} %param.29) | copy-start | bytes 110596
  7.2 11.1 %copy-start.12 = (bf16[192,96]{1,0:T(8,128)(2,1)S(1)}, bf16[192,96]{1,0:T(8,128)(2,1)}, u32[]{:S(2)}) copy-start(bf16[192,96]{1,0:T(8,128)(2,1)} %param.30) | copy-start | bytes 110596
  7.2 12.8 %copy-start.20 = (s32[1,2]{1,0:T(1,128)S(1)}, s32[1,2]{1,0:T(1,128)}, u32[]{:S(2)}) copy-start(s32[1,2]{1,0:T(1,128)} %param.25) | copy-start | bytes 28
  7.2 15.8 %copy-start.3 = (bf16[1,2,522,768]{3,1,2,0:T(2,128)(2,1)S(1)}, bf16[1,2,522,768]{3,1,2,0:T(2,128)(2,1)}, u32[]{:S(2)}) copy-start(bf16[1,2,522,768]{3,1,2,0:T(2,128)(2,1)} %param.26) | copy-start | bytes 4810756
  7.2 70.2 %all-gather.10.cloned.1.call-start = ((), (), s32[]{:S(2)}) async-start(), calls=%async_computation.8 | async-start | bytes 4866048 | tf_op jit(solution)/shard_map/all_gather | solution.py:403
  8.0 135.0 %all-gather.6.cloned.1.call-start = ((), (), s32[]{:S(2)}) async-start(), calls=%async_computation.3 | async-start | bytes 4866048 | tf_op jit(solution)/shard_map/all_gather | solution.py:403
  10.2 201.1 %all-gather.8.cloned.1.call-start = ((), (), s32[]{:S(2)}) async-start(), calls=%async_computation.7 | async-start | bytes 5677056 | tf_op jit(solution)/shard_map/all_gather | solution.py:403
  19.2 589.0 %reduce-scatter.6.cloned.1.call-start = ((), (), s32[]{:S(2)}) async-start(), calls=%async_computation.5 | async-start | bytes 4866048 | tf_op jit(solution)/shard_map/reduce_scatter | solution.py:441
  23.3 2.8 copy-start
  23.3 2.8 copy-start.13
  23.3 2.8 copy-start.2
  406.8 17.0 %copy-start.4 = (bf16[528,768]{1,0:T(8,128)(2,1)S(1)}, bf16[528,768]{1,0:T(8,128)(2,1)}, u32[]{:S(2)}) copy-start(bf16[528,768]{1,0:T(8,128)(2,1)} %convert_element_type.128) | copy-start | bytes 2433028
  406.8 17.1 %copy-start.5 = (bf16[528,768]{1,0:T(8,128)(2,1)S(1)}, bf16[528,768]{1,0:T(8,128)(2,1)}, u32[]{:S(2)}) copy-start(bf16[528,768]{1,0:T(8,128)(2,1)} %convert_element_type.129) | copy-start | bytes 2433028
  469.3 218.7 %reduce-scatter.8.cloned.1.call-start = ((), (), s32[]{:S(2)}) async-start(), calls=%async_computation.6 | async-start | bytes 4866048 | tf_op jit(solution)/shard_map/reduce_scatter | solution.py:441
  494.9 0.7 copy-start.16
  494.9 0.7 copy-start.17
  494.9 308.3 %reduce-scatter.4.cloned.1.call-start = ((), (), s32[]{:S(2)}) async-start(), calls=%async_computation.4 | async-start | bytes 5677056 | tf_op jit(solution)/shard_map/reduce_scatter | solution.py:441
  495.7 18.6 %copy-start.19 = (f32[1,768]{1,0:T(1,128)S(1)}, f32[1,768]{1,0:T(1,128)}, u32[]{:S(2)}) copy-start(f32[1,768]{1,0:T(1,128)} %get-tuple-element.127) | copy-start | bytes 9220
  495.7 19.4 %copy-start.18 = (f32[1,768]{1,0:T(1,128)S(1)}, f32[1,768]{1,0:T(1,128)}, u32[]{:S(2)}) copy-start(f32[1,768]{1,0:T(1,128)} %get-tuple-element.125) | copy-start | bytes 9220
  495.7 20.1 %copy-start.14 = (f32[8,768]{1,0:T(8,128)S(1)}, f32[8,768]{1,0:T(8,128)}, u32[]{:S(2)}) copy-start(f32[8,768]{1,0:T(8,128)} %get-tuple-element.129) | copy-start | bytes 73732
  495.7 20.1 %copy-start.15 = (f32[8,768]{1,0:T(8,128)S(1)}, f32[8,768]{1,0:T(8,128)}, u32[]{:S(2)}) copy-start(f32[8,768]{1,0:T(8,128)} %get-tuple-element.128) | copy-start | bytes 73732
  516.6 1.6 copy-start.21
  516.6 2.2 copy-start.22
  517.1 0.9 copy-start.6
  517.1 1.1 copy-start.7
  548.5 4.9 copy-start.1
  597.9 1.5 copy-start.9
  599.3 1.5 copy-start.10
  601.0 4.0 copy-start.8
Sparse Core Ops, SparseCore 0:
  11.1 66.3 all-gather.9
  81.0 61.9 all-gather.5
  146.6 64.6 all-gather.7
  469.4 106.5 reduce-scatter.5
  581.3 106.5 reduce-scatter.7
  693.3 109.8 reduce-scatter.3

commit v2 on v1

--- a/solution.py
+++ b/solution.py
@@ -16,6 +16,7 @@
 ROWS = 528
 KEYS = 640
 QUAD = 256
+UNITS = 512
 F32 = jnp.float32
 BF16 = jnp.bfloat16
 
@@ -70,7 +71,7 @@
 def attention_forward_kernel(
     info, x, wq, wk, wv, wo, vq, vv, vo, gain, shift,
     q_out, k_out, v_out, e_out, total_out, mixed_out, hidden_out, normed_out, inverse_out,
-    narrow, bias, k_pad, v_pad, branch,
+    narrow, narrow_hidden, bias, k_pad, v_pad, branch,
 ):
     step = pl.program_id(0)
 
@@ -124,6 +125,7 @@
             x[...] + (branch[...] + vo[...]), gain[...], shift[...]
         )
         hidden_out[...] = hidden
+        narrow_hidden[...] = hidden.astype(BF16)
         normed_out[...] = normed
         inverse_out[...] = jnp.broadcast_to(inverse, inverse_out.shape)
 
@@ -160,16 +162,16 @@
         out_specs=[
             rows_block, rows_block, rows_block,
             pl.BlockSpec((4, ROWS, KEYS), lambda i: (i, 0, 0)),
-            stats, rows_block, full, full, stats,
+            stats, rows_block, full, full, stats, full, full,
         ],
         out_shape=[
             shape((ROWS, width), BF16), shape((ROWS, width), BF16), shape((ROWS, width), BF16),
             shape((HEADS, ROWS, KEYS), BF16),
             shape((ROWS, 128), F32), shape((ROWS, width), BF16),
             shape((ROWS, width), F32), shape((ROWS, width), F32), shape((ROWS, 128), F32),
+            shape((ROWS, width), BF16), shape((ROWS, width), BF16),
         ],
         scratch_shapes=[
-            pltpu.VMEM((ROWS, width), BF16),
             pltpu.VMEM((ROWS, KEYS), F32),
             pltpu.VMEM((KEYS, QUAD), BF16),
             pltpu.VMEM((KEYS, QUAD), BF16),
@@ -184,17 +186,16 @@
 
 
 def feed_forward_kernel(
-    hidden, wu, wd, vu, vd, gain, shift, act_out, slope_out, y_out, normed_out, inverse_out,
-    narrow, total,
+    hidden, narrow, wu, wd, vu, vd, gain, shift, act_out, slope_out, y_out, normed_out, inverse_out,
+    total,
 ):
     step = pl.program_id(0)
 
     @pl.when(step == 0)
     def _():
-        narrow[...] = hidden[...].astype(BF16)
         total[...] = jnp.zeros_like(total)
 
-    upward = nt(narrow[...], wu[...]) + vu[...]
+    upward = nn(narrow[...], wu[...]) + vu[...]
     act, slope = gelu_pair(upward)
     act_out[...] = act.astype(BF16)
     slope_out[...] = slope.astype(BF16)
@@ -210,12 +211,9 @@
         inverse_out[...] = jnp.broadcast_to(inverse, inverse_out.shape)
 
 
-UNITS = 512
-
-
-def feed_forward(hidden, weights):
+def feed_forward(hidden, narrow, weights):
     width = hidden.shape[1]
-    units = weights["u"].shape[0]
+    units = weights["u"].shape[1]
     vector = whole((1, width))
     full = whole((ROWS, width))
     block = pl.BlockSpec((ROWS, UNITS), lambda i: (0, i))
@@ -224,8 +222,8 @@
         feed_forward_kernel,
         grid=(units // UNITS,),
         in_specs=[
-            full,
-            pl.BlockSpec((UNITS, width), lambda i: (i, 0)),
+            full, full,
+            pl.BlockSpec((width, UNITS), lambda i: (0, i)),
             pl.BlockSpec((width, UNITS), lambda i: (0, i)),
             pl.BlockSpec((1, UNITS), lambda i: (0, i)),
             vector, vector, vector,
@@ -235,11 +233,11 @@
             shape((ROWS, units), BF16), shape((ROWS, units), BF16),
             shape((ROWS, width), F32), shape((ROWS, width), F32), shape((ROWS, 128), F32),
         ],
-        scratch_shapes=[pltpu.VMEM((ROWS, width), BF16), pltpu.VMEM((ROWS, width), F32)],
+        scratch_shapes=[pltpu.VMEM((ROWS, width), F32)],
         compiler_params=params(),
         name="feed_forward",
     )(
-        hidden, weights["u"], weights["d"], weights["vu"], weights["vd"],
+        hidden, narrow, weights["u"], weights["d"], weights["vu"], weights["vd"],
         weights["og"], weights["os"],
     )
 
@@ -266,7 +264,7 @@
     up = (nn(gd_out[...], wd[...]) * slope[...].astype(F32)).astype(BF16)
     gu_out[...] = up
     vu_out[...] = column_sum(up.astype(F32))
-    dhidden[...] += nn(up, wu[...])
+    dhidden[...] += nt(up, wu[...])
 
     @pl.when(step == pl.num_programs(0) - 1)
     def _():
@@ -284,7 +282,7 @@
 
 def feed_backward(dy, saved, weights):
     width = dy.shape[1]
-    units = weights["u"].shape[0]
+    units = weights["u"].shape[1]
     vector = whole((1, width))
     full = whole((ROWS, width))
     stats = whole((ROWS, 128))
@@ -296,7 +294,7 @@
         in_specs=[
             full, full, stats, full, stats, block,
             pl.BlockSpec((width, UNITS), lambda i: (0, i)),
-            pl.BlockSpec((UNITS, width), lambda i: (i, 0)),
+            pl.BlockSpec((width, UNITS), lambda i: (0, i)),
             whole((width, width)), vector, vector,
         ],
         out_specs=[
@@ -399,6 +397,551 @@
     )
 
 
+ROWS_MESH = 4
+LINES = 16
+MESH_IDS = pl.DeviceIdType.MESH
+Z_UP, Z_DOWN, ACROSS, ALONG, HALF_ACROSS, HALF_ALONG = range(6)
+SHARE = 6
+
+
+class Place:
+    def __init__(self, cols):
+        self.row, self.col = lax.axis_index("row"), lax.axis_index("col")
+        self.length = cols // 2
+        self.core = lax.rem(self.col, 2)
+        self.line = lax.div(self.col, 2)
+        self.across_row = self.row + 1 - 2 * lax.rem(self.row, 2)
+        self.along_row = self.row + 2 - 4 * lax.div(self.row, 2)
+        self.corner_row = 3 - self.row
+        self.across = (self.across_row, self.col)
+        self.along = (self.along_row, self.col)
+        self.up = (self.row, self.col + 2)
+        self.down = (self.row, self.col - 2)
+        self.other_core = 1 - self.core
+        self.partner = (self.row, self.col + 1 - 2 * self.core)
+
+    def greet(self):
+        barrier = pltpu.get_barrier_semaphore()
+
+        def signal(device):
+            pl.semaphore_signal(barrier, inc=1, device_id=device, device_id_type=MESH_IDS)
+
+        signal(self.across)
+        signal(self.along)
+        signal(self.partner)
+        pl.when(self.line > 0)(lambda: signal(self.down))
+        pl.when(self.line < self.length - 1)(lambda: signal(self.up))
+        has_down = lax.div(self.line + self.length - 1, self.length)
+        has_up = lax.div(2 * self.length - 2 - self.line, self.length)
+        pl.semaphore_wait(barrier, 3 + has_down + has_up)
+
+    def at_distance(self, distance, visit):
+        if distance == 0:
+            visit(self.line, None)
+        else:
+            below, above = self.line - distance, self.line + distance
+            pl.when(below >= 0)(lambda: visit(below, True))
+            pl.when(above < self.length)(lambda: visit(above, False))
+
+
+def splits(count):
+    first = count // 32 * 16
+    return ((0, first), (first, count - first))
+
+
+def gather_kernel(
+    square, upper, lower, wq, wk, wv, wo, lines, whole_upper, whole_lower, gathered, send, recv, own
+):
+    rows, cols = ROWS_MESH, lines.shape[0]
+    place = Place(cols)
+    depth, across = upper.shape[0], lower.shape[0]
+    sources = (square, upper, lower)
+
+    def target(which, row, col, part=None):
+        if which == 0:
+            view, count = gathered.at[row * cols + col], square.shape[0]
+            begin, size = part if part else (0, count)
+            return view.at[pl.ds(begin, size)]
+        count, wide = sources[which].shape
+        array, high, side = (whole_upper, row, col) if which == 1 else (whole_lower, col, row)
+        begin, size = part if part else (0, count)
+        return array.at[
+            pl.ds(pl.multiple_of(high * count + begin, 16), size),
+            pl.ds(pl.multiple_of(side * wide, 128), wide),
+        ]
+
+    def copy(which, kind, row, line, device, part=None, mine=None, arrival=None):
+        col = 2 * line + (place.core if mine is None else mine)
+        there = target(which, row, col, part)
+        here = there if arrival is None else sources[which]
+        return pltpu.make_async_remote_copy(
+            src_ref=here, dst_ref=there,
+            send_sem=send.at[which, kind, line], recv_sem=recv.at[which, kind, line],
+            device_id=device, device_id_type=MESH_IDS,
+        )
+
+    place.greet()
+    keeps = []
+    for which in range(3):
+        keep = pltpu.make_async_copy(
+            sources[which], target(which, place.row, place.col), own.at[which]
+        )
+        keep.start()
+        keeps.append(keep)
+
+    def both(which):
+        return splits(sources[which].shape[0])
+
+    def by_line(which, distance):
+        def visit(line, upward):
+            first = True if upward is None else None
+            args = (place.row, line)
+            if upward is not None:
+                kind = Z_UP if upward else Z_DOWN
+                copy(which, kind, *args, place.down).wait_recv()
+            if upward is None or upward:
+                pl.when(place.line < place.length - 1)(
+                    lambda: copy(which, Z_UP, *args, place.up, arrival=first).start()
+                )
+            if upward is None or not upward:
+                pl.when(place.line > 0)(
+                    lambda: copy(which, Z_DOWN, *args, place.down, arrival=first).start()
+                )
+            copy(which, ACROSS, *args, place.across, arrival=first).start()
+            copy(which, ALONG, *args, place.along, arrival=first).start()
+            copy(which, SHARE, *args, place.partner, arrival=first).start()
+
+        place.at_distance(distance, visit)
+
+    def by_side(which, distance):
+        halves = both(which)
+
+        def visit(line, upward):
+            copy(which, ACROSS, place.across_row, line, place.across).wait_recv()
+            copy(which, HALF_ALONG, place.across_row, line, place.along, halves[1]).start()
+            copy(which, SHARE + 1, place.across_row, line, place.partner).start()
+            copy(which, ALONG, place.along_row, line, place.along).wait_recv()
+            copy(which, HALF_ACROSS, place.along_row, line, place.across, halves[0]).start()
+            copy(which, SHARE + 2, place.along_row, line, place.partner).start()
+
+        place.at_distance(distance, visit)
+
+    def by_corner(which, distance):
+        halves = both(which)
+
+        def visit(line, upward):
+            copy(which, HALF_ACROSS, place.corner_row, line, place.across, halves[0]).wait_recv()
+            copy(which, SHARE + 3, place.corner_row, line, place.partner, halves[0]).start()
+            copy(which, HALF_ALONG, place.corner_row, line, place.along, halves[1]).wait_recv()
+            copy(which, SHARE + 4, place.corner_row, line, place.partner, halves[1]).start()
+
+        place.at_distance(distance, visit)
+
+    def from_partner(which):
+        halves = both(which)
+        for distance in range(place.length):
+
+            def visit(line, upward):
+                mine = place.other_core
+                for kind, row, part in (
+                    (0, place.row, None), (1, place.across_row, None), (2, place.along_row, None),
+                    (3, place.corner_row, halves[0]), (4, place.corner_row, halves[1]),
+                ):
+                    copy(which, SHARE + kind, row, line, place.partner, part, mine=mine).wait_recv()
+
+            place.at_distance(distance, visit)
+
+    def drain(which):
+        halves = both(which)
+        for distance in range(place.length):
+
+            def visit(line, upward):
+                args = (place.row, line)
+                first = True if upward is None else None
+                if upward is None or upward:
+                    pl.when(place.line < place.length - 1)(
+                        lambda: copy(which, Z_UP, *args, place.up, arrival=first).wait_send()
+                    )
+                if upward is None or not upward:
+                    pl.when(place.line > 0)(
+                        lambda: copy(which, Z_DOWN, *args, place.down, arrival=first).wait_send()
+                    )
+                copy(which, ACROSS, *args, place.across, arrival=first).wait_send()
+                copy(which, ALONG, *args, place.along, arrival=first).wait_send()
+                copy(which, SHARE, *args, place.partner, arrival=first).wait_send()
+                copy(which, HALF_ALONG, place.across_row, line, place.along, halves[1]).wait_send()
+                copy(which, HALF_ACROSS, place.along_row, line, place.across, halves[0]).wait_send()
+                copy(which, SHARE + 1, place.across_row, line, place.partner).wait_send()
+                copy(which, SHARE + 2, place.along_row, line, place.partner).wait_send()
+                copy(which, SHARE + 3, place.corner_row, line, place.partner, halves[0]).wait_send()
+                copy(which, SHARE + 4, place.corner_row, line, place.partner, halves[1]).wait_send()
+
+            place.at_distance(distance, visit)
+
+    length = place.length
+    finish = length + 2
+    for step in range(finish + 4):
+        for which in range(3):
+            distance = step - 2 * which
+            if 0 <= distance < length:
+                by_line(which, distance)
+            if 1 <= distance < length + 1:
+                by_side(which, distance - 1)
+            if 2 <= distance < length + 2:
+                by_corner(which, distance - 2)
+        if step == finish:
+            from_partner(0)
+            keeps[0].wait()
+            outs = (wq, wk, wv, wo)
+            for col in range(cols):
+                for at, out in enumerate(outs):
+                    out[across * col : across * col + across, :] = jnp.concatenate(
+                        [
+                            gathered[row * cols + col, :across, depth * at : depth * at + depth]
+                            for row in range(rows)
+                        ],
+                        axis=1,
+                    )
+                lines[col] = gathered[col, across:, :128].astype(F32)
+    for which in range(1, 3):
+        from_partner(which)
+        keeps[which].wait()
+    for which in range(3):
+        drain(which)
+
+
+def pack_kernel(wq, wk, wv, wo, wd, vectors, square, lower):
+    across, depth = wq.shape[1], wq.shape[0]
+    square[:across, :] = jnp.concatenate(
+        [item[...].astype(F32).T for item in (wq, wk, wv, wo)], axis=1
+    ).astype(BF16)
+    square[across:, :] = jnp.zeros((LINES, square.shape[1]), BF16)
+    square[across : across + LINES, :128] = vectors[...]
+    lower[...] = wd[...].astype(F32).T.astype(BF16)
+
+
+def fetch_by_kernel(arguments):
+    matrices, vectors = arguments[:6], arguments[6:]
+    rows, cols = lax.axis_size("row"), lax.axis_size("col")
+    depth, across = matrices[0].shape
+    width = depth * rows
+    units = matrices[4].shape[1] * cols
+    table = jnp.stack([*vectors[:5], *vectors[6:]])
+    table = jnp.concatenate([table, vectors[5].reshape(-1, across)], axis=0)
+    table = jnp.pad(table, ((0, LINES - table.shape[0]), (0, 128 - across)))
+    shape = jax.ShapeDtypeStruct
+    square, lower = pl.pallas_call(
+        pack_kernel,
+        out_shape=[shape((across + LINES, 4 * depth), BF16), shape((across, matrices[5].shape[0]), BF16)],
+        in_specs=[pl.BlockSpec(memory_space=pltpu.VMEM)] * 6,
+        out_specs=[pl.BlockSpec(memory_space=pltpu.VMEM)] * 2,
+        name="pack",
+    )(*matrices[:4], matrices[5], table)
+    anywhere, local = pl.BlockSpec(memory_space=pl.ANY), pl.BlockSpec(memory_space=pltpu.VMEM)
+    kinds = (3, SHARE + 5, cols // 2)
+    wq, wk, wv, wo, lines, upper, lower = pl.pallas_call(
+        gather_kernel,
+        out_shape=[shape((width, width), BF16)] * 4
+        + [shape((cols, LINES, 128), F32), shape((width, units), BF16), shape((width, units), BF16)],
+        in_specs=[anywhere] * 3,
+        out_specs=[local] * 5 + [anywhere] * 2,
+        scratch_shapes=[
+            pltpu.VMEM((rows * cols, across + LINES, 4 * depth), BF16),
+            pltpu.SemaphoreType.DMA(kinds), pltpu.SemaphoreType.DMA(kinds), pltpu.SemaphoreType.DMA((3,)),
+        ],
+        compiler_params=pltpu.CompilerParams(
+            collective_id=0, has_side_effects=True, vmem_limit_bytes=40 * 1024 * 1024
+        ),
+        name="gather",
+    )(square, matrices[4], lower)
+    names = ("vq", "vv", "vo", "ag", "as", "vd", "og", "os")
+    table = lines[:, :, :across]
+    weights = dict(q=wq, k=wk, v=wv, o=wo, u=upper, d=lower)
+    for at, name in enumerate(names):
+        weights[name] = table[:, at].reshape(1, -1)
+    weights["vu"] = table[:, len(names) : len(names) + units // cols // across].reshape(1, -1)
+    return weights
+
+
+def scatter_kernel(square, upper, lower, square_out, upper_out, lower_out, *scratch):
+    mine, theirs, corner, side, lined = (scratch[3 * at : 3 * at + 3] for at in range(5))
+    send, recv, own = scratch[15:]
+    rows, cols = ROWS_MESH, square.shape[0] // ROWS_MESH
+    place = Place(cols)
+    outs = (square_out, upper_out, lower_out)
+    length = place.length
+
+    def source(which, row, col):
+        count, wide = outs[which].shape
+        if which == 0:
+            return square.at[row * cols + col]
+        array, high, level = (upper, row, col) if which == 1 else (lower, col, row)
+        return array.at[
+            pl.ds(pl.multiple_of(high * count, 16), count),
+            pl.ds(pl.multiple_of(level * wide, 128), wide),
+        ]
+
+    def load(which, row, line):
+        return pltpu.make_async_copy(
+            source(which, row, 2 * line + place.core),
+            mine[which].at[row * length + line], own.at[which, row * length + line],
+        )
+
+    def share(which, row, line, core):
+        at = row * length + line
+        return pltpu.make_async_remote_copy(
+            src_ref=source(which, row, 2 * line + core), dst_ref=theirs[which].at[at],
+            send_sem=send.at[which, SHARE + row, line], recv_sem=recv.at[which, SHARE + row, line],
+            device_id=place.partner, device_id_type=MESH_IDS,
+        )
+
+    def remote(which, kind, line, here, there, device):
+        return pltpu.make_async_remote_copy(
+            src_ref=here, dst_ref=there,
+            send_sem=send.at[which, kind, line], recv_sem=recv.at[which, kind, line],
+            device_id=device, device_id_type=MESH_IDS,
+        )
+
+    def corner_copy(which, kind, line):
+        begin, size = splits(outs[which].shape[0])[kind - HALF_ACROSS]
+        part = pl.ds(begin, size)
+        here = mine[which].at[place.corner_row * length + line, part]
+        there = corner[which].at[line, part]
+        return remote(which, kind, line, here, there, place.across if kind == HALF_ACROSS else place.along)
+
+    def side_copy(which, kind, line):
+        row, device = (place.across_row, place.across) if kind == ACROSS else (place.along_row, place.along)
+        here = mine[which].at[row * length + line]
+        return remote(which, kind, line, here, side[which].at[kind - ACROSS, line], device)
+
+    def line_copy(which, kind, line):
+        here = mine[which].at[place.row * length + line]
+        return remote(which, kind, line, here, lined[which].at[kind, line], place.up if kind == Z_UP else place.down)
+
+    def add(which, at, arrived, part=None):
+        block = mine[which].at[at] if part is None else mine[which].at[at, pl.ds(*part)]
+        block[...] = (block[...].astype(F32) + arrived[...].astype(F32)).astype(BF16)
+
+    place.greet()
+
+    def spread(distance, visit):
+        place.at_distance(distance, lambda line, upward: visit(line))
+
+    farthest = range(length - 1, -1, -1)
+    order = ("corner_row", "across_row", "along_row", "row")
+    for which in range(3):
+        for distance in farthest:
+
+            def begin(line):
+                for name in order:
+                    row = getattr(place, name)
+                    load(which, row, line).start()
+                    share(which, row, line, place.other_core).start()
+
+            spread(distance, begin)
+
+    def merge(which, row, line):
+        load(which, row, line).wait()
+        share(which, row, line, place.core).wait_recv()
+        at = row * length + line
+        add(which, at, theirs[which].at[at])
+
+    def cores(which, distance):
+        def visit(line):
+            merge(which, place.corner_row, line)
+            merge(which, place.across_row, line)
+            corner_copy(which, HALF_ACROSS, line).start()
+            corner_copy(which, HALF_ALONG, line).start()
+            merge(which, place.along_row, line)
+            merge(which, place.row, line)
+
+        spread(distance, visit)
+
+    def corners(which, distance):
+        first, second = splits(outs[which].shape[0])
+
+        def visit(line):
+            corner_copy(which, HALF_ACROSS, line).wait_recv()
+            add(which, place.along_row * length + line, corner[which].at[line, pl.ds(*first)], first)
+            corner_copy(which, HALF_ALONG, line).wait_recv()
+            add(which, place.across_row * length + line, corner[which].at[line, pl.ds(*second)], second)
+            side_copy(which, ALONG, line).start()
+            side_copy(which, ACROSS, line).start()
+
+        spread(distance, visit)
+
+    def sides(which, distance):
+        def visit(line):
+            at = place.row * length + line
+            side_copy(which, ACROSS, line).wait_recv()
+            add(which, at, side[which].at[0, line])
+            side_copy(which, ALONG, line).wait_recv()
+            add(which, at, side[which].at[1, line])
+
+        spread(distance, visit)
+
+    def lines(which, distance):
+        def visit(line, downward):
+            at = place.row * length + line
+            kind = Z_DOWN if downward else Z_UP
+            onward = place.line < length - 1 if downward else place.line > 0
+
+            @pl.when(onward)
+            def _():
+                line_copy(which, kind, line).wait_recv()
+                add(which, at, lined[which].at[kind, line])
+
+            line_copy(which, kind, line).start()
+
+        place.at_distance(distance, visit)
+
+    def result(which):
+        at = place.row * length + place.line
+        for kind, there in ((Z_UP, place.line > 0), (Z_DOWN, place.line < length - 1)):
+
+            @pl.when(there)
+            def _():
+                line_copy(which, kind, place.line).wait_recv()
+                add(which, at, lined[which].at[kind, place.line])
+
+        outs[which][...] = mine[which][at].astype(F32)
+
+    def drain(which):
+        for distance in farthest:
+
+            def visit(line, downward):
+                for row in range(rows):
+                    share(which, row, line, place.other_core).wait_send()
+                for kind in (HALF_ACROSS, HALF_ALONG):
+                    corner_copy(which, kind, line).wait_send()
+                for kind in (ACROSS, ALONG):
+                    side_copy(which, kind, line).wait_send()
+                if downward is not None:
+                    line_copy(which, Z_DOWN if downward else Z_UP, line).wait_send()
+
+            place.at_distance(distance, visit)
+
+    for step in range(length + 3 + 4):
+        for which in range(3):
+            stage = step - 2 * which
+            if 0 <= stage < length:
+                cores(which, length - 1 - stage)
+            if 1 <= stage < length + 1:
+                corners(which, length - stage)
+            if 2 <= stage < length + 2:
+                sides(which, length + 1 - stage)
+            if 3 <= stage < length + 2:
+                lines(which, length + 2 - stage)
+            if stage == length + 2:
+                result(which)
+    for which in range(3):
+        drain(which)
+
+
+def scatter_by_kernel(square, upper, lower):
+    cols = square.shape[0] // ROWS_MESH
+    length = cols // 2
+    count, wide = square.shape[1:]
+    blocks = (
+        (count, wide),
+        (upper.shape[0] // ROWS_MESH, upper.shape[1] // cols),
+        (lower.shape[0] // cols, lower.shape[1] // ROWS_MESH),
+    )
+    kinds = (3, SHARE + ROWS_MESH, length)
+    anywhere, local = pl.BlockSpec(memory_space=pl.ANY), pl.BlockSpec(memory_space=pltpu.VMEM)
+    buffers = [
+        pltpu.VMEM((*lead, *block), BF16)
+        for lead in ((ROWS_MESH * length,), (ROWS_MESH * length,), (length,), (2, length), (2, length))
+        for block in blocks
+    ]
+    return pl.pallas_call(
+        scatter_kernel,
+        out_shape=[jax.ShapeDtypeStruct(block, F32) for block in blocks],
+        in_specs=[anywhere] * 3,
+        out_specs=[local] * 3,
+        scratch_shapes=[
+            *buffers,
+            pltpu.SemaphoreType.DMA(kinds), pltpu.SemaphoreType.DMA(kinds),
+            pltpu.SemaphoreType.DMA((3, ROWS_MESH * length)),
+        ],
+        compiler_params=pltpu.CompilerParams(
+            collective_id=1, has_side_effects=True, vmem_limit_bytes=50 * 1024 * 1024
+        ),
+        name="scatter",
+    )(square, upper, lower)
+
+
+def product_kernel(left1, left2, right1, right2, out, turned):
+    @pl.when(pl.program_id(0) == 0)
+    def _():
+        turned[0] = left1[...].T
+        turned[1] = left2[...].T
+
+    out[...] = (nn(turned[0], right1[...]) + nn(turned[1], right2[...])).astype(BF16)
+
+
+def product_t(left1, left2, right1, right2):
+    width, units = left1.shape[1], right1.shape[1]
+    block = pl.BlockSpec((ROWS, UNITS), lambda i: (0, i))
+    return pl.pallas_call(
+        product_kernel,
+        grid=(units // UNITS,),
+        in_specs=[whole((ROWS, width))] * 2 + [block] * 2,
+        out_specs=pl.BlockSpec((width, UNITS), lambda i: (0, i)),
+        out_shape=jax.ShapeDtypeStruct((width, units), BF16),
+        scratch_shapes=[pltpu.VMEM((2, width, ROWS), BF16)],
+        compiler_params=params(),
+        name="weight_gradient",
+    )(left1, left2, right1, right2)
+
+
+def square_kernel(
+    gq1, gq2, gk1, gk2, gv1, gv2, gb1, gb2, x1, x2, mixed1, mixed2, vectors, wide, out, total
+):
+    rows = ROWS_MESH
+    cols = out.shape[0] // rows
+    across, depth = vectors.shape[1] // cols, vectors.shape[1] // rows
+    lefts = ((gq1, gq2), (gk1, gk2), (gv1, gv2), (gb1, gb2))
+    for at, (left1, left2) in enumerate(lefts):
+        right1, right2 = (x1, x2) if at < 3 else (mixed1, mixed2)
+        total[at] = (nn(left1[...].T, right1[...]) + nn(left2[...].T, right2[...])).astype(BF16)
+    share = wide.shape[1] // cols // across
+    for col in range(cols):
+        begin = across * col
+        narrow = jnp.concatenate(
+            [vectors[:, begin : begin + across]]
+            + [wide[:, across * (col * share + at) : across * (col * share + at + 1)] for at in range(share)]
+            + [jnp.zeros((LINES - 8 - share, across), F32)],
+            axis=0,
+        )
+        narrow = jnp.pad(narrow, ((0, 0), (0, out.shape[2] - across))).astype(BF16)
+        for row in range(rows):
+            block = row * cols + col
+            out[block, :across, :] = jnp.concatenate(
+                [total[at, begin : begin + across, depth * row : depth * row + depth] for at in range(4)],
+                axis=1,
+            )
+            out[block, across:, :] = narrow
+
+
+def square_gradients(grads1, grads2, saved1, saved2, vectors, wide, cols):
+    width = vectors.shape[1]
+    operands = []
+    for name in ("gq", "gk", "gv", "gb"):
+        operands += [grads1[name], grads2[name]]
+    operands += [saved1["x"], saved2["x"], saved1["mixed"], saved2["mixed"], vectors, wide]
+    local = pl.BlockSpec(memory_space=pltpu.VMEM)
+    return pl.pallas_call(
+        square_kernel,
+        in_specs=[local] * len(operands),
+        out_specs=local,
+        out_shape=jax.ShapeDtypeStruct((ROWS_MESH * cols, width // cols + LINES, width), BF16),
+        scratch_shapes=[pltpu.VMEM((4, width, width), BF16)],
+        compiler_params=pltpu.CompilerParams(vmem_limit_bytes=58 * 1024 * 1024),
+        name="square_gradients",
+    )(*operands)
+
+
 def gather_all(part):
     return lax.all_gather(part, ("row", "col"), axis=0, tiled=False)
 
@@ -426,7 +969,7 @@
     weights = {name: whole_square[at] for at, name in enumerate(names)}
     weights["u"] = (
         second.reshape(rows, cols, across, 4, depth)
-        .transpose(1, 3, 2, 0, 4).reshape(4 * width, width)
+        .transpose(0, 4, 1, 3, 2).reshape(width, 4 * width)
     )
     weights["d"] = third.reshape(rows, cols, across, 4 * depth).transpose(1, 2, 0, 3).reshape(width, 4 * width)
     lines = first[:cols, across:].reshape(cols, -1).astype(F32)
@@ -441,8 +984,24 @@
     return lax.psum_scatter(terms, ("row", "col"), scatter_dimension=0, tiled=False)
 
 
-def product_t(left, right):
-    return jnp.einsum("rd,re->de", left, right, preferred_element_type=F32).astype(BF16)
+def scatter(square, upper, lower, lines):
+    rows, cols = lax.axis_size("row"), lax.axis_size("col")
+    width = square.shape[1]
+    depth, across = width // rows, width // cols
+    square = square.reshape(4, cols, across, rows, depth).transpose(3, 1, 2, 0, 4)
+    square = square.reshape(rows, cols, across, 4 * depth)
+    count = lines.shape[1]
+    extra = -(-count // (4 * depth))
+    extra += -(across + extra) % 16
+    lines = jnp.pad(lines, ((0, 0), (0, extra * 4 * depth - count))).astype(BF16)
+    lines = jnp.broadcast_to(lines.reshape(1, cols, extra, 4 * depth), (rows, cols, extra, 4 * depth))
+    square = jnp.concatenate([square, lines], axis=2)
+    square = scatter_all(square.reshape(rows * cols, across + extra, 4 * depth)).astype(F32)
+    upper = upper.reshape(rows, depth, cols, 4 * across).transpose(0, 2, 1, 3)
+    upper = scatter_all(upper.reshape(rows * cols, depth, 4 * across)).astype(F32)
+    lower = lower.reshape(cols, across, rows, 4 * depth).transpose(2, 0, 1, 3)
+    lower = scatter_all(lower.reshape(rows * cols, across, 4 * depth)).astype(F32)
+    return square[:across], upper, lower, square[across:].reshape(-1)[:count]
 
 
 def solution_body(
@@ -451,17 +1010,19 @@
     rows, cols = lax.axis_size("row"), lax.axis_size("col")
     depth, across = parameters[0].shape
     width = depth * rows
-    weights = fetch(parameters)
+    by_kernel = rows == ROWS_MESH and cols % 2 == 0 and depth % 32 == 0 and across % 32 == 0
+    by_kernel = by_kernel and 4 * across % 128 == 0
+    weights = fetch_by_kernel(parameters) if by_kernel else fetch(parameters)
     full_length = jnp.full((1,), TEXT, jnp.int32)
     pad = jnp.zeros((ROWS - SEG_ROWS, width), F32)
 
     def forward(edge, words, length, start):
         info = jnp.concatenate([length, start])
         x = jnp.concatenate([edge, words.astype(F32), edge, pad], axis=0)
-        q, k, v, e, total, mixed, hidden, normed1, inverse1 = attention_forward(info, x, weights)
-        act, slope, y, normed2, inverse2 = feed_forward(hidden, weights)
+        q, k, v, e, total, mixed, hidden, normed1, inverse1, xb, hb = attention_forward(info, x, weights)
+        act, slope, y, normed2, inverse2 = feed_forward(hidden, hb, weights)
         saved = dict(
-            x=x.astype(BF16), q=q, k=k, v=v, e=e, total=total, mixed=mixed, hidden=hidden.astype(BF16),
+            x=xb, q=q, k=k, v=v, e=e, total=total, mixed=mixed, hidden=hb,
             normed1=normed1, inverse1=inverse1, act=act, slope=slope, normed2=normed2, inverse2=inverse2,
         )
         return y, saved
@@ -485,50 +1046,39 @@
         [dx1[MEMORY : MEMORY + TEXT], dx2[MEMORY : MEMORY + TEXT]]
     ).astype(BF16)[None]
 
-    def both(name):
-        return jnp.concatenate([grads1[name], grads2[name]], axis=0)
-
-    def kept(name):
-        return jnp.concatenate([saved1[name], saved2[name]], axis=0)
-
-    lower = product_t(both("gd"), kept("act"))
-    lower = lower.reshape(cols, across, rows, 4 * depth).transpose(2, 0, 1, 3)
-    lower = scatter_all(lower.reshape(rows * cols, across, 4 * depth))
-    upper = product_t(both("gu"), kept("hidden"))
-    upper = upper.reshape(cols, 4, across, rows, depth).transpose(3, 0, 2, 1, 4)
-    upper = scatter_all(upper.reshape(rows * cols, across, 4 * depth))
-    xb = kept("x")
-    square = jnp.stack(
-        [
-            product_t(both("gq"), xb), product_t(both("gk"), xb), product_t(both("gv"), xb),
-            product_t(both("gb"), kept("mixed")),
-        ]
-    )
-    square = square.reshape(4, cols, across, rows, depth).transpose(3, 1, 2, 0, 4)
+    upper = product_t(saved1["hidden"], saved2["hidden"], grads1["gu"], grads2["gu"])
+    lower = product_t(grads1["gd"], grads2["gd"], saved1["act"], saved2["act"])
     sums = grads1["sums"] + grads2["sums"]
-    vectors = (
-        grads1["vq"] + grads2["vq"], grads1["vv"] + grads2["vv"], sums[5], sums[3], sums[4],
-        grads1["vu"] + grads2["vu"], sums[2], sums[0], sums[1],
-    )
-    lines = jnp.concatenate([item.reshape(cols, -1) for item in vectors], axis=1)
-    count = lines.shape[1]
-    extra = -(-count // (4 * depth))
-    extra += -(across + extra) % 16
-    lines = jnp.pad(lines, ((0, 0), (0, extra * 4 * depth - count))).astype(BF16)
-    lines = jnp.broadcast_to(lines.reshape(1, cols, extra, 4 * depth), (rows, cols, extra, 4 * depth))
-    square = jnp.concatenate([square.reshape(rows, cols, across, 4 * depth), lines], axis=2)
-    square = scatter_all(square.reshape(rows * cols, across + extra, 4 * depth))
-    own = square[:across].astype(F32).reshape(across, 4, depth)
-    line = square[across:].astype(F32).reshape(-1)
-    result = [own[:, at].T for at in range(4)]
-    upper = upper.astype(F32).reshape(across, 4, depth).transpose(2, 1, 0).reshape(depth, 4 * across)
-    result += [upper, lower.astype(F32).T]
-    at = 0
-    for item in vectors:
-        size = item.size // cols
-        result.append(line[at : at + size])
-        at += size
-    return (layer_output, text_grad, memory_grad, *result)
+    wide = grads1["vu"] + grads2["vu"]
+    parts = (grads1["vq"] + grads2["vq"], grads1["vv"] + grads2["vv"])
+    names = (0, 1, 5, 3, 4, 2, 0, 1)
+    vectors = jnp.concatenate([*parts, *(sums[at : at + 1] for at in names[2:])], axis=0)
+    if by_kernel:
+        square = square_gradients(grads1, grads2, saved1, saved2, vectors, wide, cols)
+        square, upper, lower = scatter_by_kernel(square, upper, lower)
+        table = square[across : across + LINES, :across]
+        square = square[:across]
+        lines = [table[at] for at in range(8)]
+        lines.insert(5, table[8 : 8 + wide.size // cols // across].reshape(-1))
+    else:
+        square = jnp.stack(
+            [
+                product_t(grads1["gq"], grads2["gq"], saved1["x"], saved2["x"]),
+                product_t(grads1["gk"], grads2["gk"], saved1["x"], saved2["x"]),
+                product_t(grads1["gv"], grads2["gv"], saved1["x"], saved2["x"]),
+                product_t(grads1["gb"], grads2["gb"], saved1["mixed"], saved2["mixed"]),
+            ]
+        )
+        table = jnp.concatenate(
+            [vectors.reshape(8, cols, across).transpose(1, 0, 2).reshape(cols, -1), wide.reshape(cols, -1)],
+            axis=1,
+        )
+        square, upper, lower, line = scatter(square, upper, lower, table)
+        lines = [line[at * across : at * across + across] for at in range(8)]
+        lines.insert(5, line[8 * across :])
+    own = square.reshape(across, 4, depth)
+    result = [own[:, at].T for at in range(4)] + [upper, lower.T]
+    return (layer_output, text_grad, memory_grad, *result, *lines)
 
 
 def solution(mesh):

time: 825 us -> 391 us (0.47)
  waiting for transfers between devices: 328 us -> 0 us
  local copies, waits for them, and re-layouts: 250 us -> 40.4 us
  Pallas kernels: 143 us -> 332 us
  matrix products: 36.1 us -> 0 us
  other arithmetic: 42.1 us -> 11.4 us
  between operations: 15.5 us -> 1.8 us
    reduce_scatter x3 -> x0, waiting for transfers between devices: 191 us -> none  [scatter_all(): lax.psum_scatter(terms, ('row', 'col'), scatter_dimension=0, tiled=False)]
    pallas_call x0 -> x6, Pallas kernels: none -> 189 us  [the longest x1 74.9 us: scatter_by_kernel(): pl.pallas_call(scatter_kernel, out_shape=[jax.ShapeDtypeStruct(block, F32...]
    all_gather x3 -> x0, waiting for transfers between devices: 136 us -> none  [gather_all(): return lax.all_gather(part, ('row', 'col'), axis=0, tiled=False)]
    reshape x25 -> x4, local copies, waits for them, and re-layouts: 97.9 us -> 2.28 us  [the longest x1 0.76 us: fetch_by_kernel(): table = jnp.concatenate([table, vectors[5].reshape(-1, across)], axis=0)]
    slice x10 -> x6, local copies, waits for them, and re-layouts: 44.2 us -> 0.13 us  [the longest x1 0.09 us: fetch_by_kernel(): weights[name] = table[:, at].reshape(1, -1)]
    dot_general x6 -> x0, matrix products: 36.1 us -> none  [product_t(): jnp.einsum('rd,re->de', left, right, preferred_element_type=F32)]
    another operation x15 -> x8, local copies, waits for them, and re-layouts: 30.1 us -> 5.26 us  [fetch_by_kernel(): weights[name] = table[:, at].reshape(1, -1)]
    transpose x2 -> x0, other arithmetic: 19.2 us -> none  [the longest x1 17.6 us: solution_body(): square.reshape(4, cols, across, rows, depth).transpose(3, 1, 2, 0, 4)]
  transfers between devices with their start and end apart: 6 -> 0, of which waited for: 5 -> 0; matrix products, arithmetic and copies ran while one was open for 23% -> 0% of each run, Pallas kernels for 2% -> 0%
where the time goes in v2:
time: 391 us; the launch traced here: 385 us
  Pallas kernels  332 us (85%)
  local copies, waits for them, and re-layouts  40.4 us (10%)
  other arithmetic  11.4 us (3%)
    pallas_call x1, Pallas kernels, scatter_by_kernel(): pl.pallas_call(scatter_kernel, out_shape=[jax.ShapeDtypeStruct(block, F32...  74.9 us
    pallas_call x1, Pallas kernels, fetch_by_kernel(): pl.pallas_call(gather_kernel, out_shape=[shape((width, width), BF16)] * 4...  73.8 us
    pallas_call x2, Pallas kernels, attention_forward(): pl.pallas_call(attention_forward_kernel, grid=(steps,), in_specs=[pl.Bloc...  37.3 us
    pallas_call x2, Pallas kernels, feed_forward(): pl.pallas_call(feed_forward_kernel, grid=(units // UNITS,), in_specs=[ful...  35.7 us
    pallas_call x2, Pallas kernels, attention_backward(): pl.pallas_call(attention_backward_kernel, grid=(width // QUAD,), in_specs...  35.7 us
    pallas_call x2, Pallas kernels, feed_backward(): pl.pallas_call(feed_backward_kernel, grid=(units // UNITS,), in_specs=[fu...  34.4 us
    pallas_call x2, Pallas kernels, product_t(): pl.pallas_call(product_kernel, grid=(units // UNITS,), in_specs=[whole((R...  23.9 us
    unnamed x39, local copies, waits for them, and re-layouts  14.7 us

profile of v2, /device:TPU:0, one launch (start us, length us, event | category | flops | bytes accessed | tf_op | source)
XLA Modules:
  0.0 385.4 jit_solution(18009291359045812363)
XLA Ops:
  1.3 0.8 reshape.151
  2.1 1.3 fusion.13
  3.4 1.2 pad_add_fusion.info
  4.6 1.2 pad_add_fusion.1.info
  5.8 0.8 concatenate.38
  6.7 0.6 pad.10.vectors
  7.3 0.7 bitcast_convert_fusion.1
  8.1 1.7 copy.39.wd
  9.8 2.0 pack.1
  11.8 4.3 %fusion.10 = (bf16[1,1,502,768]{3,1,2,0:T(2,128)(2,1)S(1)}, bf16[1,1,502,768]{3,1,2,0:T(2,128)(2,1)S(1)}) fusion(bf16[1,2,502,768]{3,1,2,0:T(2,128)(2,1)} %param.22), kind=kLoop, calls=%fused_computation.48 | loop fusion | bytes 3084288 | tf_op jit(solution)/shard_map/slice | solution.py:1031
  16.1 1.4 fusion.6
  17.5 1.4 maximum_maximum_fusion.x
  18.9 0.5 copy-done.9
  19.4 0.2 bitcast_convert_fusion
  19.7 1.9 fusion
  21.6 73.8 %gather.1 = (bf16[768,768]{1,0:T(8,128)(2,1)S(1)}, bf16[768,768]{1,0:T(8,128)(2,1)S(1)}, bf16[768,768]{1,0:T(8,128)(2,1)S(1)}, bf16[768,768]{1,0:T(8,128)(2,1)S(...) custom-call(bf16[112,768]{1,0:T(8,128)(2,1)S(1)} %copy-done.5, ...), custom_call_target="tpu_custom_call" | custom-call | tf_op jit(solution)/shard_map/gather/pallas_call | solution.py:642
  95.5 2.2 copy-done
  97.7 1.0 copy-done.1
  98.7 1.0 copy-done.2
  99.7 1.0 copy-done.3
  100.7 1.0 copy-done.4
  101.9 0.7 reshape.152.vu
  102.6 0.7 reshape_squeeze.31.shift
  103.2 0.7 reshape_squeeze.30.gain.gain2
  103.9 0.7 reshape_squeeze.27.gain.gain1
  104.5 0.7 reshape_squeeze.29.vd
  105.2 0.7 reshape_squeeze.28.shift
  105.9 0.7 reshape_squeeze.26.vo
  106.5 0.7 reshape_squeeze.25.vv
  107.2 0.7 reshape_squeeze.24.vq
  107.8 18.5 %attention_forward.2 = (bf16[528,768]{1,0:T(8,128)(2,1)}, bf16[528,768]{1,0:T(8,128)(2,1)}, bf16[528,768]{1,0:T(8,128)(2,1)}, bf16[12,528,640]{2,1,0:T(8,128)(2,...) custom-call(s32[2]{0:T(128)} %pad_add_fusion.info, ...), custom_call_target="tpu_custom_call" | custom-call | tf_op jit(solution)/shard_map/attention_forward/pallas_call | solution.py:154
  126.3 17.8 %feed_forward.2 = (bf16[528,3072]{1,0:T(8,128)(2,1)}, bf16[528,3072]{1,0:T(8,128)(2,1)}, f32[528,768]{1,0:T(8,128)}, f32[528,768]{1,0:T(8,128)}, f32[528,128]{1,0:T(8,128)}) custom-call(f32[528,768]{1,0:T(8,128)} %get-tuple-element.107.hidden, bf16[528,768]{1,0:T(8,128)(2,1)} %get-tuple-element.108.narrow.left1, bf16[768,3072]{1,0:T(8,128)(2,1)} %copy-done, ...), custom_call_target="tpu_custom_call" | custom-call | tf_op jit(solution)/shard_map/feed_forward/pallas_call | solution.py:221
  144.2 0.9 slice.188
  145.1 1.5 fusion.2
  146.6 1.4 maximum_maximum_fusion.1.x
  148.0 18.8 %attention_forward.3 = (bf16[528,768]{1,0:T(8,128)(2,1)}, bf16[528,768]{1,0:T(8,128)(2,1)}, bf16[528,768]{1,0:T(8,128)(2,1)}, bf16[12,528,640]{2,1,0:T(8,128)(2,...) custom-call(s32[2]{0:T(128)} %pad_add_fusion.1.info, ...), custom_call_target="tpu_custom_call" | custom-call | tf_op jit(solution)/shard_map/attention_forward/pallas_call | solution.py:154
  166.9 17.9 %feed_forward.3 = (bf16[528,3072]{1,0:T(8,128)(2,1)}, bf16[528,3072]{1,0:T(8,128)(2,1)}, f32[528,768]{1,0:T(8,128)}, f32[528,768]{1,0:T(8,128)}, f32[528,128]{1,0:T(8,128)}) custom-call(f32[528,768]{1,0:T(8,128)} %get-tuple-element.112.hidden, bf16[528,768]{1,0:T(8,128)(2,1)} %get-tuple-element.113.narrow.left2, bf16[768,3072]{1,0:T(8,128)(2,1)} %copy-done, ...), custom_call_target="tpu_custom_call" | custom-call | tf_op jit(solution)/shard_map/feed_forward/pallas_call | solution.py:221
  184.8 1.5 fusion.3
  186.3 0.1 pad_maximum_fusion
  186.5 2.4 copy.46
  188.9 17.4 %feed_backward.2 = (bf16[528,768]{1,0:T(8,128)(2,1)}, bf16[528,3072]{1,0:T(8,128)(2,1)}, bf16[528,768]{1,0:T(8,128)(2,1)}, f32[528,768]{1,0:T(8,128)}, bf16[528,...) custom-call(f32[528,768]{1,0:T(8,128)} %get-tuple-element.197.dy, f32[528,768]{1,0:T(8,128)} %get-tuple-element.127.normed2, ...), custom_call_target="tpu_custom_call" | custom-call | tf_op jit(solution)/shard_map/feed_backward/pallas_call | solution.py:291
  206.3 17.8 %attention_backward.2 = (bf16[528,768]{1,0:T(8,128)(2,1)}, bf16[528,768]{1,0:T(8,128)(2,1)}, bf16[528,768]{1,0:T(8,128)(2,1)}, f32[528,768]{1,0:T(8,128)}, f32[1,768]{1,0:T(1,128)}, /*index=5*/f32[1,768]{1,0:T(1,128)}) custom-call(bf16[528,768]{1,0:T(8,128)(2,1)} %get-tuple-element.121.q, bf16[528,768]{1,0:T(8,128)(2,1)} %get-tuple-element.122.k, ...), custom_call_target="tpu_custom_call" | custom-call | tf_op jit(solution)/shard_map/attention_backward/pallas_call | solution.py:378
  224.1 0.8 fusion.8
  224.9 1.4 scatter-add.4.dy
  226.4 17.0 %feed_backward.3 = (bf16[528,768]{1,0:T(8,128)(2,1)}, bf16[528,3072]{1,0:T(8,128)(2,1)}, bf16[528,768]{1,0:T(8,128)(2,1)}, f32[528,768]{1,0:T(8,128)}, bf16[528,...) custom-call(f32[528,768]{1,0:T(8,128)} %scatter-add.4.dy, f32[528,768]{1,0:T(8,128)} %get-tuple-element.135.normed2, ...), custom_call_target="tpu_custom_call" | custom-call | tf_op jit(solution)/shard_map/feed_backward/pallas_call | solution.py:291
  243.4 12.0 %weight_gradient.3.lower = bf16[768,3072]{1,0:T(8,128)(2,1)} custom-call(bf16[528,768]{1,0:T(8,128)(2,1)} %get-tuple-element.163.left1, bf16[528,768]{1,0:T(8,128)(2,1)} %get-tuple-element.164.left2, bf16[528,3072]{1,0:T(8,128)(2,1)} %get-tuple-element.165.right1, bf16[528,3072]{1,0:T(8,128)(2,1)} %get-tuple-element.166.right2), custom_call_target="tpu_custom_call" | custom-call | tf_op jit(solution)/shard_map/weight_gradient/pallas_call | solution.py:886
  255.4 11.9 %weight_gradient.2.upper = bf16[768,3072]{1,0:T(8,128)(2,1)} custom-call(bf16[528,768]{1,0:T(8,128)(2,1)} %get-tuple-element.108.narrow.left1, bf16[528,768]{1,0:T(8,128)(2,1)} %get-tuple-element.113.narrow.left2, bf16[528,3072]{1,0:T(8,128)(2,1)} %get-tuple-element.161.right1, bf16[528,3072]{1,0:T(8,128)(2,1)} %get-tuple-element.162.right2), custom_call_target="tpu_custom_call" | custom-call | tf_op jit(solution)/shard_map/weight_gradient/pallas_call | solution.py:886
  267.3 0.6 add.35.wide
  268.0 17.8 %attention_backward.3 = (bf16[528,768]{1,0:T(8,128)(2,1)}, bf16[528,768]{1,0:T(8,128)(2,1)}, bf16[528,768]{1,0:T(8,128)(2,1)}, f32[528,768]{1,0:T(8,128)}, f32[1,768]{1,0:T(1,128)}, /*index=5*/f32[1,768]{1,0:T(1,128)}) custom-call(bf16[528,768]{1,0:T(8,128)(2,1)} %get-tuple-element.115.q, bf16[528,768]{1,0:T(8,128)(2,1)} %get-tuple-element.116.k, ...), custom_call_target="tpu_custom_call" | custom-call | tf_op jit(solution)/shard_map/attention_backward/pallas_call | solution.py:378
  285.8 0.7 add.33
  286.5 0.7 add.32
  287.2 0.6 concatenate.41.vectors
  287.9 14.1 %square_gradients.1.square = bf16[32,112,768]{2,1,0:T(8,128)(2,1)} custom-call(bf16[528,768]{1,0:T(8,128)(2,1)} %get-tuple-element.143.gq1, bf16[528,768]{1,0:T(8,128)(2,1)} %get-tuple-element.144.gq2, bf16[528,768]{1,0:T(8,128)(2,1)} %get-tuple-element.145.gk1, bf16[528,768]{1,0:T(8,128)(2,1)} %get-tuple-element.146.gk2, ...), custom_call_target="tpu_custom_call" | custom-call | tf_op jit(solution)/shard_map/square_gradients/pallas_call | solution.py:934
  302.0 74.9 %scatter.1 = (f32[112,768]{1,0:T(8,128)S(1)}, f32[192,384]{1,0:T(8,128)S(1)}, f32[96,768]{1,0:T(8,128)S(1)}) custom-call(bf16[32,112,768]{2,1,0:T(8,128)(2,1)} %square_gradients.1.square, bf16[768,3072]{1,0:T(8,128)(2,1)} %weight_gradient.2.upper, bf16[768,3072]{1,0:T(8,128)(2,1)} %weight_gradient.3.lower), custom_call_target="tpu_custom_call" | custom-call | tf_op jit(solution)/shard_map/scatter/pallas_call | solution.py:857
  376.9 0.7 reshape.155
  377.5 0.5 slice_bitcast_fusion.5
  378.1 0.6 fusion.9
  378.9 0.2 copy.48
  379.0 0.8 slice_bitcast_fusion
  379.8 1.5 fusion.5
  381.3 0.1 pad_maximum_fusion.1
  381.5 2.3 copy.47
  383.8 0.7 copy.62
  384.5 0.7 copy.63
  (38 shorter events, 0.4 us)
Async XLA Ops:
  17.5 1.9 copy-start.9
  19.6 2.0 copy-start.5
  19.6 2.0 copy-start.6
  19.7 2.0 copy-start.7
  95.5 2.2 copy-start
  97.7 1.0 copy-start.1
  98.7 1.0 copy-start.2
  99.7 1.0 copy-start.3
  100.7 1.0 copy-start.4
  144.1 2.4 copy-start.8
  255.4 11.9 %copy-start.13 = (f32[1,3072]{1,0:T(1,128)S(1)}, f32[1,3072]{1,0:T(1,128)}, u32[]{:S(2)}) copy-start(f32[1,3072]{1,0:T(1,128)} %get-tuple-element.160) | copy-start | bytes 36868
  255.4 11.9 %copy-start.14 = (f32[1,3072]{1,0:T(1,128)S(1)}, f32[1,3072]{1,0:T(1,128)}, u32[]{:S(2)}) copy-start(f32[1,3072]{1,0:T(1,128)} %get-tuple-element.159) | copy-start | bytes 36868
  255.4 12.6 %copy-start.11 = (f32[8,768]{1,0:T(8,128)S(1)}, f32[8,768]{1,0:T(8,128)}, u32[]{:S(2)}) copy-start(f32[8,768]{1,0:T(8,128)} %get-tuple-element.158) | copy-start | bytes 73732
  255.4 12.5 %copy-start.12 = (f32[8,768]{1,0:T(8,128)S(1)}, f32[8,768]{1,0:T(8,128)}, u32[]{:S(2)}) copy-start(f32[8,768]{1,0:T(8,128)} %get-tuple-element.157) | copy-start | bytes 73732
  268.0 17.9 %copy-start.16 = (f32[1,768]{1,0:T(1,128)S(1)}, f32[1,768]{1,0:T(1,128)}, u32[]{:S(2)}) copy-start(f32[1,768]{1,0:T(1,128)} %get-tuple-element.156) | copy-start | bytes 9220
  268.0 18.5 %copy-start.15 = (f32[1,768]{1,0:T(1,128)S(1)}, f32[1,768]{1,0:T(1,128)}, u32[]{:S(2)}) copy-start(f32[1,768]{1,0:T(1,128)} %get-tuple-element.154) | copy-start | bytes 9220
  302.0 76.1 %copy-start.10 = (f32[528,768]{1,0:T(8,128)S(1)}, f32[528,768]{1,0:T(8,128)}, u32[]{:S(2)}) copy-start(f32[528,768]{1,0:T(8,128)} %get-tuple-element.142) | copy-start | bytes 4866052

commit v3 on v2

--- a/solution.py
+++ b/solution.py
@@ -69,20 +69,24 @@
 
 
 def attention_forward_kernel(
-    info, x, wq, wk, wv, wo, vq, vv, vo, gain, shift,
+    segment, tails, starts, words, edge, wq, wk, wv, wo, vq, vv, vo, gain, shift,
     q_out, k_out, v_out, e_out, total_out, mixed_out, hidden_out, normed_out, inverse_out,
-    narrow, narrow_hidden, bias, k_pad, v_pad, branch,
+    narrow, narrow_hidden, x, bias, k_pad, v_pad, branch,
 ):
     step = pl.program_id(0)
 
     @pl.when(step == 0)
     def _():
+        x[...] = words[0]
+        x[:MEMORY, :] = edge[:MEMORY, :].astype(F32)
+        x[MEMORY + TEXT : SEG_ROWS, :] = edge[:MEMORY, :].astype(F32)
         narrow[...] = x[...].astype(BF16)
         branch[...] = jnp.zeros_like(branch)
         total_out[...] = jnp.ones_like(total_out)
         k_pad[...] = jnp.zeros_like(k_pad)
         v_pad[...] = jnp.zeros_like(v_pad)
-        length, start = info[0], info[1]
+        length = TEXT if segment == 0 else tails[0]
+        start = starts[0, segment]
         row = lax.broadcasted_iota(jnp.int32, (ROWS, KEYS), 0)
         col = lax.broadcasted_iota(jnp.int32, (ROWS, KEYS), 1)
         low, high = start + MEMORY, start + MEMORY + PICTURE
@@ -140,8 +144,8 @@
     )
 
 
-def attention_forward(info, x, weights):
-    width = x.shape[1]
+def attention_forward(segment, tails, starts, words, edge, weights):
+    width = words.shape[2]
     steps = width // QUAD
     row_block = pl.BlockSpec((QUAD, width), lambda i: (i, 0))
     col_block = pl.BlockSpec((width, QUAD), lambda i: (0, i))
@@ -152,11 +156,11 @@
     stats = whole((ROWS, 128))
     shape = jax.ShapeDtypeStruct
     return pl.pallas_call(
-        attention_forward_kernel,
+        functools.partial(attention_forward_kernel, segment),
         grid=(steps,),
         in_specs=[
-            pl.BlockSpec(memory_space=pltpu.SMEM),
-            full, row_block, row_block, row_block, col_block,
+            pl.BlockSpec(memory_space=pltpu.SMEM), pl.BlockSpec(memory_space=pltpu.SMEM),
+            pl.BlockSpec((1, ROWS, width), lambda i: (segment, 0, 0)), whole(edge.shape), row_block, row_block, row_block, col_block,
             bias_block, bias_block, vector, vector, vector,
         ],
         out_specs=[
@@ -172,6 +176,7 @@
             shape((ROWS, width), BF16), shape((ROWS, width), BF16),
         ],
         scratch_shapes=[
+            pltpu.VMEM((ROWS, width), F32),
             pltpu.VMEM((ROWS, KEYS), F32),
             pltpu.VMEM((KEYS, QUAD), BF16),
             pltpu.VMEM((KEYS, QUAD), BF16),
@@ -180,13 +185,13 @@
         compiler_params=params(),
         name="attention_forward",
     )(
-        info, x, weights["q"], weights["k"], weights["v"], weights["o"],
+        tails, starts, words, edge, weights["q"], weights["k"], weights["v"], weights["o"],
         weights["vq"], weights["vv"], weights["vo"], weights["ag"], weights["as"],
     )
 
 
 def feed_forward_kernel(
-    hidden, narrow, wu, wd, vu, vd, gain, shift, act_out, slope_out, y_out, normed_out, inverse_out,
+    hidden, narrow, wu, wd, vu, vd, gain, shift, act_out, slope_out, y_out, edge_out, normed_out, inverse_out,
     total,
 ):
     step = pl.program_id(0)
@@ -206,7 +211,8 @@
         y, normed, inverse = norm_forward(
             hidden[...] + (total[...] + vd[...]), gain[...], shift[...]
         )
-        y_out[...] = y
+        y_out[...] = y.astype(BF16)
+        edge_out[...] = y[MEMORY + TEXT :, :]
         normed_out[...] = normed
         inverse_out[...] = jnp.broadcast_to(inverse, inverse_out.shape)
 
@@ -228,10 +234,10 @@
             pl.BlockSpec((1, UNITS), lambda i: (0, i)),
             vector, vector, vector,
         ],
-        out_specs=[block, block, full, full, whole((ROWS, 128))],
+        out_specs=[block, block, full, whole((ROWS - MEMORY - TEXT, width)), full, whole((ROWS, 128))],
         out_shape=[
-            shape((ROWS, units), BF16), shape((ROWS, units), BF16),
-            shape((ROWS, width), F32), shape((ROWS, width), F32), shape((ROWS, 128), F32),
+            shape((ROWS, units), BF16), shape((ROWS, units), BF16), shape((ROWS, width), BF16),
+            shape((ROWS - MEMORY - TEXT, width), F32), shape((ROWS, width), F32), shape((ROWS, 128), F32),
         ],
         scratch_shapes=[pltpu.VMEM((ROWS, width), F32)],
         compiler_params=params(),
@@ -243,7 +249,7 @@
 
 
 def feed_backward_kernel(
-    dy, normed2, inverse2, normed1, inverse1, slope, wd, wu, wo, gain2, gain1,
+    segment, dy, top, bottom, normed2, inverse2, normed1, inverse1, slope, wd, wu, wo, gain2, gain1,
     gd_out, gu_out, gb_out, dfirst_out, gm_out, vu_out, sums_out,
     dsecond, dhidden,
 ):
@@ -251,7 +257,10 @@
 
     @pl.when(step == 0)
     def _():
-        grad, normed = dy[...], normed2[...]
+        dsecond[...] = dy[0]
+        if segment == 0:
+            dsecond[MEMORY + TEXT : SEG_ROWS, :] += top[:MEMORY, :] + bottom[:MEMORY, :]
+        grad, normed = dsecond[...], normed2[...]
         sums_out[0:1, :] = column_sum(grad * normed)
         sums_out[1:2, :] = column_sum(grad)
         second = norm_backward(grad, normed, inverse2[:, 0:1], gain2[...])
@@ -280,8 +289,9 @@
         gm_out[...] = nn(narrow, wo[...]).astype(BF16)
 
 
-def feed_backward(dy, saved, weights):
-    width = dy.shape[1]
+def feed_backward(segment, dy, later, saved, weights):
+    width = dy.shape[2]
+    edges = ROWS - MEMORY - TEXT
     units = weights["u"].shape[1]
     vector = whole((1, width))
     full = whole((ROWS, width))
@@ -289,10 +299,13 @@
     block = pl.BlockSpec((ROWS, UNITS), lambda i: (0, i))
     shape = jax.ShapeDtypeStruct
     return pl.pallas_call(
-        feed_backward_kernel,
+        functools.partial(feed_backward_kernel, segment),
         grid=(units // UNITS,),
         in_specs=[
-            full, full, stats, full, stats, block,
+            pl.BlockSpec((1, ROWS, width), lambda i: (segment, 0, 0)),
+            pl.BlockSpec((edges, width), lambda i: (0, 0)),
+            pl.BlockSpec((edges, width), lambda i: ((MEMORY + TEXT) // edges, 0)),
+            full, stats, full, stats, block,
             pl.BlockSpec((width, UNITS), lambda i: (0, i)),
             pl.BlockSpec((width, UNITS), lambda i: (0, i)),
             whole((width, width)), vector, vector,
@@ -310,7 +323,7 @@
         compiler_params=params(),
         name="feed_backward",
     )(
-        dy, saved["normed2"], saved["inverse2"], saved["normed1"], saved["inverse1"],
+        dy, later, later, saved["normed2"], saved["inverse2"], saved["normed1"], saved["inverse1"],
         saved["slope"], weights["d"], weights["u"], weights["o"], weights["og"], weights["ag"],
     )
 
@@ -450,9 +463,10 @@
 
 
 def gather_kernel(
-    square, upper, lower, wq, wk, wv, wo, lines, whole_upper, whole_lower, gathered, send, recv, own
+    square, upper, lower, wq, wk, wv, wo, *rest
 ):
-    rows, cols = ROWS_MESH, lines.shape[0]
+    vectors, (whole_upper, whole_lower, gathered, send, recv, own) = rest[:9], rest[9:]
+    rows, cols = ROWS_MESH, wq.shape[0] // lower.shape[0]
     place = Place(cols)
     depth, across = upper.shape[0], lower.shape[0]
     sources = (square, upper, lower)
@@ -602,7 +616,13 @@
                         ],
                         axis=1,
                     )
-                lines[col] = gathered[col, across:, :128].astype(F32)
+            lines = [gathered[col, across:, :across].astype(F32) for col in range(cols)]
+            table = jnp.concatenate(lines, axis=1)
+            for at in range(8):
+                vectors[at][...] = table[at : at + 1]
+            vectors[8][...] = jnp.concatenate(
+                [line[8 + at : 9 + at] for line in lines for at in range(upper.shape[1] // across)], axis=1
+            )
     for which in range(1, 3):
         from_partner(which)
         keeps[which].wait()
@@ -639,28 +659,24 @@
     )(*matrices[:4], matrices[5], table)
     anywhere, local = pl.BlockSpec(memory_space=pl.ANY), pl.BlockSpec(memory_space=pltpu.VMEM)
     kinds = (3, SHARE + 5, cols // 2)
-    wq, wk, wv, wo, lines, upper, lower = pl.pallas_call(
+    vector = shape((1, width), F32)
+    names = ("q", "k", "v", "o", "vq", "vv", "vo", "ag", "as", "vd", "og", "os", "vu", "u", "d")
+    whole_arrays = pl.pallas_call(
         gather_kernel,
-        out_shape=[shape((width, width), BF16)] * 4
-        + [shape((cols, LINES, 128), F32), shape((width, units), BF16), shape((width, units), BF16)],
+        out_shape=[shape((width, width), BF16)] * 4 + [vector] * 8 + [shape((1, units), F32)]
+        + [shape((width, units), BF16), shape((width, units), BF16)],
         in_specs=[anywhere] * 3,
-        out_specs=[local] * 5 + [anywhere] * 2,
+        out_specs=[local] * 13 + [anywhere] * 2,
         scratch_shapes=[
             pltpu.VMEM((rows * cols, across + LINES, 4 * depth), BF16),
             pltpu.SemaphoreType.DMA(kinds), pltpu.SemaphoreType.DMA(kinds), pltpu.SemaphoreType.DMA((3,)),
         ],
         compiler_params=pltpu.CompilerParams(
-            collective_id=0, has_side_effects=True, vmem_limit_bytes=40 * 1024 * 1024
+            collective_id=0, has_side_effects=True, vmem_limit_bytes=58 * 1024 * 1024
         ),
         name="gather",
     )(square, matrices[4], lower)
-    names = ("vq", "vv", "vo", "ag", "as", "vd", "og", "os")
-    table = lines[:, :, :across]
-    weights = dict(q=wq, k=wk, v=wv, o=wo, u=upper, d=lower)
-    for at, name in enumerate(names):
-        weights[name] = table[:, at].reshape(1, -1)
-    weights["vu"] = table[:, len(names) : len(names) + units // cols // across].reshape(1, -1)
-    return weights
+    return dict(zip(names, whole_arrays))
 
 
 def scatter_kernel(square, upper, lower, square_out, upper_out, lower_out, *scratch):
@@ -871,13 +887,16 @@
     )(square, upper, lower)
 
 
+def joined(first, second):
+    return jnp.concatenate([first, second], axis=0)
+
+
 def product_kernel(left1, left2, right1, right2, out, turned):
     @pl.when(pl.program_id(0) == 0)
     def _():
-        turned[0] = left1[...].T
-        turned[1] = left2[...].T
-
-    out[...] = (nn(turned[0], right1[...]) + nn(turned[1], right2[...])).astype(BF16)
+        turned[...] = joined(left1[...], left2[...]).T
+
+    out[...] = nn(turned[...], joined(right1[...], right2[...])).astype(BF16)
 
 
 def product_t(left1, left2, right1, right2):
@@ -889,22 +908,33 @@
         in_specs=[whole((ROWS, width))] * 2 + [block] * 2,
         out_specs=pl.BlockSpec((width, UNITS), lambda i: (0, i)),
         out_shape=jax.ShapeDtypeStruct((width, units), BF16),
-        scratch_shapes=[pltpu.VMEM((2, width, ROWS), BF16)],
+        scratch_shapes=[pltpu.VMEM((width, 2 * ROWS), BF16)],
         compiler_params=params(),
         name="weight_gradient",
     )(left1, left2, right1, right2)
 
 
+SUM_ROWS = (5, 3, 4, 2, 0, 1)
+
+
 def square_kernel(
-    gq1, gq2, gk1, gk2, gv1, gv2, gb1, gb2, x1, x2, mixed1, mixed2, vectors, wide, out, total
+    gq1, gq2, gk1, gk2, gv1, gv2, gb1, gb2, x1, x2, mixed1, mixed2,
+    vq1, vq2, vv1, vv2, sums1, sums2, vu1, vu2, out, total
 ):
     rows = ROWS_MESH
     cols = out.shape[0] // rows
-    across, depth = vectors.shape[1] // cols, vectors.shape[1] // rows
+    width = out.shape[2]
+    across, depth = width // cols, width // rows
+    sums = sums1[...] + sums2[...]
+    wide = vu1[...] + vu2[...]
+    vectors = jnp.concatenate(
+        [vq1[...] + vq2[...], vv1[...] + vv2[...]] + [sums[at : at + 1] for at in SUM_ROWS], axis=0
+    )
     lefts = ((gq1, gq2), (gk1, gk2), (gv1, gv2), (gb1, gb2))
     for at, (left1, left2) in enumerate(lefts):
         right1, right2 = (x1, x2) if at < 3 else (mixed1, mixed2)
-        total[at] = (nn(left1[...].T, right1[...]) + nn(left2[...].T, right2[...])).astype(BF16)
+        left, right = joined(left1[...], left2[...]), joined(right1[...], right2[...])
+        total[at] = nn(left.T, right).astype(BF16)
     share = wide.shape[1] // cols // across
     for col in range(cols):
         begin = across * col
@@ -924,12 +954,14 @@
             out[block, across:, :] = narrow
 
 
-def square_gradients(grads1, grads2, saved1, saved2, vectors, wide, cols):
-    width = vectors.shape[1]
+def square_gradients(grads1, grads2, saved1, saved2, cols):
+    width = grads1["gq"].shape[1]
     operands = []
     for name in ("gq", "gk", "gv", "gb"):
         operands += [grads1[name], grads2[name]]
-    operands += [saved1["x"], saved2["x"], saved1["mixed"], saved2["mixed"], vectors, wide]
+    operands += [saved1["x"], saved2["x"], saved1["mixed"], saved2["mixed"]]
+    for name in ("vq", "vv", "sums", "vu"):
+        operands += [grads1[name], grads2[name]]
     local = pl.BlockSpec(memory_space=pltpu.VMEM)
     return pl.pallas_call(
         square_kernel,
@@ -1013,53 +1045,48 @@
     by_kernel = rows == ROWS_MESH and cols % 2 == 0 and depth % 32 == 0 and across % 32 == 0
     by_kernel = by_kernel and 4 * across % 128 == 0
     weights = fetch_by_kernel(parameters) if by_kernel else fetch(parameters)
-    full_length = jnp.full((1,), TEXT, jnp.int32)
-    pad = jnp.zeros((ROWS - SEG_ROWS, width), F32)
-
-    def forward(edge, words, length, start):
-        info = jnp.concatenate([length, start])
-        x = jnp.concatenate([edge, words.astype(F32), edge, pad], axis=0)
-        q, k, v, e, total, mixed, hidden, normed1, inverse1, xb, hb = attention_forward(info, x, weights)
-        act, slope, y, normed2, inverse2 = feed_forward(hidden, hb, weights)
+    words = jnp.pad(text[0].astype(F32), ((0, 0), (MEMORY, ROWS - MEMORY - TEXT), (0, 0)))
+
+    def forward(segment, edge):
+        q, k, v, e, total, mixed, hidden, normed1, inverse1, xb, hb = attention_forward(
+            segment, tail_lengths, picture_starts, words, edge, weights
+        )
+        act, slope, y, edge, normed2, inverse2 = feed_forward(hidden, hb, weights)
         saved = dict(
             x=xb, q=q, k=k, v=v, e=e, total=total, mixed=mixed, hidden=hb,
             normed1=normed1, inverse1=inverse1, act=act, slope=slope, normed2=normed2, inverse2=inverse2,
         )
-        return y, saved
-
-    y1, saved1 = forward(memory[0].astype(F32), text[0, 0], full_length, picture_starts[:, 0])
-    y2, saved2 = forward(y1[MEMORY + TEXT : SEG_ROWS], text[0, 1], tail_lengths, picture_starts[:, 1])
-    layer_output = jnp.stack([y1[:SEG_ROWS], y2[:SEG_ROWS]]).astype(BF16)[None]
-
-    def backward(dy, saved):
-        gd, gu, gb, dfirst, gm, vu, sums = feed_backward(dy, saved, weights)
+        return y, edge, saved
+
+    def paired(first, second, begin, count):
+        which = lax.broadcasted_iota(jnp.int32, (count, 2, width), 1)
+        first, second = (item[begin : begin + count, None, :] for item in (first, second))
+        return jnp.where(which == 0, first, second).astype(BF16).transpose(1, 0, 2)[None]
+
+    y1, edge1, saved1 = forward(0, memory[0])
+    y2, edge2, saved2 = forward(1, edge1)
+    layer_output = paired(y1, y2, 0, SEG_ROWS)
+
+    def backward(segment, later, saved):
+        gd, gu, gb, dfirst, gm, vu, sums = feed_backward(segment, cotangent, later, saved, weights)
         gq, gk, gv, dx, vq, vv = attention_backward(saved, gm, dfirst, weights)
         return dx, dict(gd=gd, gu=gu, gb=gb, gq=gq, gk=gk, gv=gv, vu=vu, sums=sums, vq=vq, vv=vv)
 
     cotangent = jnp.pad(grad_out[0].astype(F32), ((0, 0), (0, ROWS - SEG_ROWS), (0, 0)))
-    dx2, grads2 = backward(cotangent[1], saved2)
-    edge = dx2[:MEMORY] + dx2[MEMORY + TEXT : SEG_ROWS]
-    dy1 = cotangent[0].at[MEMORY + TEXT : SEG_ROWS].add(edge)
-    dx1, grads1 = backward(dy1, saved1)
+    dx2, grads2 = backward(1, saved2["normed2"], saved2)
+    dx1, grads1 = backward(0, dx2, saved1)
     memory_grad = (dx1[:MEMORY] + dx1[MEMORY + TEXT : SEG_ROWS]).astype(BF16)[None]
-    text_grad = jnp.stack(
-        [dx1[MEMORY : MEMORY + TEXT], dx2[MEMORY : MEMORY + TEXT]]
-    ).astype(BF16)[None]
+    text_grad = paired(dx1, dx2, MEMORY, TEXT)
 
     upper = product_t(saved1["hidden"], saved2["hidden"], grads1["gu"], grads2["gu"])
     lower = product_t(grads1["gd"], grads2["gd"], saved1["act"], saved2["act"])
-    sums = grads1["sums"] + grads2["sums"]
-    wide = grads1["vu"] + grads2["vu"]
-    parts = (grads1["vq"] + grads2["vq"], grads1["vv"] + grads2["vv"])
-    names = (0, 1, 5, 3, 4, 2, 0, 1)
-    vectors = jnp.concatenate([*parts, *(sums[at : at + 1] for at in names[2:])], axis=0)
     if by_kernel:
-        square = square_gradients(grads1, grads2, saved1, saved2, vectors, wide, cols)
+        square = square_gradients(grads1, grads2, saved1, saved2, cols)
         square, upper, lower = scatter_by_kernel(square, upper, lower)
         table = square[across : across + LINES, :across]
         square = square[:across]
         lines = [table[at] for at in range(8)]
-        lines.insert(5, table[8 : 8 + wide.size // cols // across].reshape(-1))
+        lines.insert(5, table[8 : 8 + upper.shape[1] // across].reshape(-1))
     else:
         square = jnp.stack(
             [
@@ -1069,6 +1096,10 @@
                 product_t(grads1["gb"], grads2["gb"], saved1["mixed"], saved2["mixed"]),
             ]
         )
+        sums = grads1["sums"] + grads2["sums"]
+        wide = grads1["vu"] + grads2["vu"]
+        parts = (grads1["vq"] + grads2["vq"], grads1["vv"] + grads2["vv"])
+        vectors = jnp.concatenate([*parts, *(sums[at : at + 1] for at in SUM_ROWS)], axis=0)
         table = jnp.concatenate(
             [vectors.reshape(8, cols, across).transpose(1, 0, 2).reshape(cols, -1), wide.reshape(cols, -1)],
             axis=1,

time: 391 us -> 360 us (0.921)
  local copies, waits for them, and re-layouts: 40.4 us -> 11.2 us
    another operation x12 -> x0, local copies, waits for them, and re-layouts: 9.94 us -> none  [the longest x8 5.26 us: fetch_by_kernel(): weights[name] = table[:, at].reshape(1, -1)]
    unnamed x39 -> x11, local copies, waits for them, and re-layouts: 14.7 us -> 5.24 us
    concatenate x4 -> x0, other arithmetic: 5.32 us -> none  [the longest x2 2.86 us: forward(): x = jnp.concatenate([edge, words.astype(F32), edge, pad], axis=0)]
    slice x8 -> x3, local copies, waits for them, and re-layouts: 6.62 us -> 1.67 us  [the longest x2 1.67 us: paired(): item[begin:begin + count, None, :]]
    select_n x0 -> x1, other arithmetic: none -> 4.47 us  [paired(): jnp.where(which == 0, first, second).astype(BF16).transpose(1, 0, 2)[None]]
    pad x0 -> x2, other arithmetic: none -> 3.91 us  [the longest x1 2.03 us: solution_body(): jnp.pad(text[0].astype(F32), ((0, 0), (MEMORY, ROWS - MEMORY - TEXT), (0,...]
where the time goes in v3:
time: 360 us; the launch traced here: 356 us
  Pallas kernels  331 us (92%)
  other arithmetic  12.1 us (3%)
  local copies, waits for them, and re-layouts  11.2 us (3%)
    pallas_call x1, Pallas kernels, fetch_by_kernel(): pl.pallas_call(gather_kernel, out_shape=[shape((width, width), BF16)] * 4...  76 us
    pallas_call x1, Pallas kernels, scatter_by_kernel(): pl.pallas_call(scatter_kernel, out_shape=[jax.ShapeDtypeStruct(block, F32...  74.9 us
    pallas_call x2, Pallas kernels, attention_forward(): pl.pallas_call(functools.partial(attention_forward_kernel, segment), grid...  37.4 us
    pallas_call x2, Pallas kernels, attention_backward(): pl.pallas_call(attention_backward_kernel, grid=(width // QUAD,), in_specs...  35.7 us
    pallas_call x2, Pallas kernels, feed_forward(): pl.pallas_call(feed_forward_kernel, grid=(units // UNITS,), in_specs=[ful...  35.3 us
    pallas_call x2, Pallas kernels, feed_backward(): pl.pallas_call(functools.partial(feed_backward_kernel, segment), grid=(un...  34.3 us
    pallas_call x2, Pallas kernels, product_t(): pl.pallas_call(product_kernel, grid=(units // UNITS,), in_specs=[whole((R...  22.4 us
    pallas_call x1, Pallas kernels, square_gradients(): pl.pallas_call(square_kernel, in_specs=[local] * len(operands), out_specs...  12.9 us

profile of v3, /device:TPU:0, one launch (start us, length us, event | category | flops | bytes accessed | tf_op | source)
XLA Modules:
  0.0 355.8 jit_solution(13631229291761113717)
XLA Ops:
  1.3 0.8 reshape.62
  2.1 0.8 concatenate.3
  2.9 0.6 pad.18.vectors
  3.5 1.7 copy.39.wd
  5.2 2.0 pack.1
  7.2 0.0 copy-start
  7.2 1.7 copy.49
  8.9 0.2 copy-done
  9.1 0.2 copy.48
  9.3 1.9 pad_convert_fusion.dy
  11.2 2.0 pad_convert_fusion.1.words
  13.2 76.0 %gather.1 = (bf16[768,768]{1,0:T(8,128)(2,1)}, bf16[768,768]{1,0:T(8,128)(2,1)}, bf16[768,768]{1,0:T(8,128)(2,1)}, bf16[768,768]{1,0:T(8,128)(2,1)}, f32[1,768]{...) custom-call(bf16[112,768]{1,0:T(8,128)(2,1)} %get-tuple-element.97.s, ...), custom_call_target="tpu_custom_call" | custom-call | tf_op jit(solution)/shard_map/gather/pallas_call | solution.py:664
  89.2 18.7 %attention_forward.2 = (bf16[528,768]{1,0:T(8,128)(2,1)}, bf16[528,768]{1,0:T(8,128)(2,1)}, bf16[528,768]{1,0:T(8,128)(2,1)}, bf16[12,528,640]{2,1,0:T(8,128)(2,...) custom-call(s32[1]{0:T(128)S(6)} %copy.52.tails, ...), custom_call_target="tpu_custom_call" | custom-call | tf_op jit(solution)/shard_map/attention_forward/pallas_call | solution.py:158
  107.8 17.6 %feed_forward.2 = (bf16[528,3072]{1,0:T(8,128)(2,1)}, bf16[528,3072]{1,0:T(8,128)(2,1)}, bf16[528,768]{1,0:T(8,128)(2,1)}, f32[16,768]{1,0:T(8,128)}, f32[528,768]{1,0:T(8,128)}, /*index=5*/f32[528,128]{1,0:T(8,128)}) custom-call(f32[528,768]{1,0:T(8,128)} %get-tuple-element.108.hidden, bf16[528,768]{1,0:T(8,128)(2,1)} %get-tuple-element.109.narrow.left1, ...), custom_call_target="tpu_custom_call" | custom-call | tf_op jit(solution)/shard_map/feed_forward/pallas_call | solution.py:227
  125.5 18.8 %attention_forward.3 = (bf16[528,768]{1,0:T(8,128)(2,1)}, bf16[528,768]{1,0:T(8,128)(2,1)}, bf16[528,768]{1,0:T(8,128)(2,1)}, bf16[12,528,640]{2,1,0:T(8,128)(2,...) custom-call(s32[1]{0:T(128)S(6)} %copy.52.tails, ...), custom_call_target="tpu_custom_call" | custom-call | tf_op jit(solution)/shard_map/attention_forward/pallas_call | solution.py:158
  144.2 0.0 copy-start.1
  144.3 17.7 %feed_forward.3 = (bf16[528,3072]{1,0:T(8,128)(2,1)}, bf16[528,3072]{1,0:T(8,128)(2,1)}, bf16[528,768]{1,0:T(8,128)(2,1)}, f32[16,768]{1,0:T(8,128)}, f32[528,768]{1,0:T(8,128)}, /*index=5*/f32[528,128]{1,0:T(8,128)}) custom-call(f32[528,768]{1,0:T(8,128)} %get-tuple-element.118.hidden, bf16[528,768]{1,0:T(8,128)(2,1)} %get-tuple-element.119.narrow.left2, ...), custom_call_target="tpu_custom_call" | custom-call | tf_op jit(solution)/shard_map/feed_forward/pallas_call | solution.py:227
  162.0 0.0 copy-done.1
  162.0 4.5 %broadcast_select_fusion = bf16[1,2,522,768]{3,1,2,0:T(2,128)(2,1)} fusion(pred[2]{0:T(512)(128)(4,1)S(1)} %iota_compare_fusion, bf16[522,768]{1,0:T(8,128)(2,1)} %bitcast.58, bf16[522,768]{1,0:T(8,128)(2,1)S(1)} %bitcast.57), kind=kLoop, calls=%fused_computation | loop fusion | flops 801792 | bytes 3207170 | tf_op jit(solution)/shard_map/jit(_where)/select_n | solution.py:1064
  166.5 17.4 %feed_backward.2 = (bf16[528,768]{1,0:T(8,128)(2,1)}, bf16[528,3072]{1,0:T(8,128)(2,1)}, bf16[528,768]{1,0:T(8,128)(2,1)}, f32[528,768]{1,0:T(8,128)}, bf16[528,...) custom-call(f32[2,528,768]{2,1,0:T(8,128)} %pad_convert_fusion.dy, ...), custom_call_target="tpu_custom_call" | custom-call | tf_op jit(solution)/shard_map/feed_backward/pallas_call | solution.py:301
  183.8 17.8 %attention_backward.2 = (bf16[528,768]{1,0:T(8,128)(2,1)}, bf16[528,768]{1,0:T(8,128)(2,1)}, bf16[528,768]{1,0:T(8,128)(2,1)}, f32[528,768]{1,0:T(8,128)}, f32[1,768]{1,0:T(1,128)}, /*index=5*/f32[1,768]{1,0:T(1,128)}) custom-call(bf16[528,768]{1,0:T(8,128)(2,1)} %get-tuple-element.127.q, bf16[528,768]{1,0:T(8,128)(2,1)} %get-tuple-element.128.k, ...), custom_call_target="tpu_custom_call" | custom-call | tf_op jit(solution)/shard_map/attention_backward/pallas_call | solution.py:391
  201.6 16.9 %feed_backward.3 = (bf16[528,768]{1,0:T(8,128)(2,1)}, bf16[528,3072]{1,0:T(8,128)(2,1)}, bf16[528,768]{1,0:T(8,128)(2,1)}, f32[528,768]{1,0:T(8,128)}, bf16[528,...) custom-call(f32[2,528,768]{2,1,0:T(8,128)} %pad_convert_fusion.dy, ...), custom_call_target="tpu_custom_call" | custom-call | tf_op jit(solution)/shard_map/feed_backward/pallas_call | solution.py:301
  218.6 11.3 %weight_gradient.3.lower = bf16[768,3072]{1,0:T(8,128)(2,1)} custom-call(bf16[528,768]{1,0:T(8,128)(2,1)} %get-tuple-element.169.left1, bf16[528,768]{1,0:T(8,128)(2,1)} %get-tuple-element.170.left2, bf16[528,3072]{1,0:T(8,128)(2,1)} %get-tuple-element.171.right1, bf16[528,3072]{1,0:T(8,128)(2,1)} %get-tuple-element.172.right2), custom_call_target="tpu_custom_call" | custom-call | tf_op jit(solution)/shard_map/weight_gradient/pallas_call | solution.py:905
  229.9 11.1 %weight_gradient.2.upper = bf16[768,3072]{1,0:T(8,128)(2,1)} custom-call(bf16[528,768]{1,0:T(8,128)(2,1)} %get-tuple-element.109.narrow.left1, bf16[528,768]{1,0:T(8,128)(2,1)} %get-tuple-element.119.narrow.left2, bf16[528,3072]{1,0:T(8,128)(2,1)} %get-tuple-element.167.right1, bf16[528,3072]{1,0:T(8,128)(2,1)} %get-tuple-element.168.right2), custom_call_target="tpu_custom_call" | custom-call | tf_op jit(solution)/shard_map/weight_gradient/pallas_call | solution.py:905
  240.9 17.8 %attention_backward.3 = (bf16[528,768]{1,0:T(8,128)(2,1)}, bf16[528,768]{1,0:T(8,128)(2,1)}, bf16[528,768]{1,0:T(8,128)(2,1)}, f32[528,768]{1,0:T(8,128)}, f32[1,768]{1,0:T(1,128)}, /*index=5*/f32[1,768]{1,0:T(1,128)}) custom-call(bf16[528,768]{1,0:T(8,128)(2,1)} %get-tuple-element.121.q, bf16[528,768]{1,0:T(8,128)(2,1)} %get-tuple-element.122.k, ...), custom_call_target="tpu_custom_call" | custom-call | tf_op jit(solution)/shard_map/attention_backward/pallas_call | solution.py:391
  258.8 12.9 %square_gradients.1.square = bf16[32,112,768]{2,1,0:T(8,128)(2,1)} custom-call(bf16[528,768]{1,0:T(8,128)(2,1)} %get-tuple-element.149.gq1, bf16[528,768]{1,0:T(8,128)(2,1)} %get-tuple-element.150.gq2, bf16[528,768]{1,0:T(8,128)(2,1)} %get-tuple-element.151.gk1, bf16[528,768]{1,0:T(8,128)(2,1)} %get-tuple-element.152.gk2, ...), custom_call_target="tpu_custom_call" | custom-call | tf_op jit(solution)/shard_map/square_gradients/pallas_call | solution.py:966
  271.7 0.0 copy-start.2
  271.7 74.9 %scatter.1 = (f32[112,768]{1,0:T(8,128)S(1)}, f32[192,384]{1,0:T(8,128)S(1)}, f32[96,768]{1,0:T(8,128)S(1)}) custom-call(bf16[32,112,768]{2,1,0:T(8,128)(2,1)} %square_gradients.1.square, bf16[768,3072]{1,0:T(8,128)(2,1)} %weight_gradient.2.upper, bf16[768,3072]{1,0:T(8,128)(2,1)} %weight_gradient.3.lower), custom_call_target="tpu_custom_call" | custom-call | tf_op jit(solution)/shard_map/scatter/pallas_call | solution.py:873
  346.6 0.7 reshape.64
  347.3 0.5 slice_bitcast_fusion.4
  347.8 0.0 copy-done.2
  347.9 0.6 fusion
  348.5 0.1 slice.72
  348.6 0.2 copy.45
  348.8 0.8 slice_bitcast_fusion
  349.5 1.5 slice.73
  351.1 3.1 select_convert_fusion
  354.1 0.7 copy.53
  354.9 0.7 copy.54
  (3 shorter events, 0.0 us)
Async XLA Ops:
  7.2 1.9 copy-start
  144.2 17.7 %copy-start.1 = (bf16[528,768]{1,0:T(8,128)(2,1)S(1)}, bf16[528,768]{1,0:T(8,128)(2,1)}, u32[]{:S(2)}) copy-start(bf16[528,768]{1,0:T(8,128)(2,1)} %get-tuple-element.116) | copy-start | bytes 2433028
  271.7 76.1 %copy-start.2 = (f32[528,768]{1,0:T(8,128)S(1)}, f32[528,768]{1,0:T(8,128)}, u32[]{:S(2)}) copy-start(f32[528,768]{1,0:T(8,128)} %get-tuple-element.148) | copy-start | bytes 4866052

commit v4 on v3

--- a/solution.py
+++ b/solution.py
@@ -14,7 +14,9 @@
 PICTURE = 256
 SEG_ROWS = 522
 ROWS = 528
-KEYS = 640
+MAIN = 512
+LAST = 128
+KEYS = MAIN + LAST
 QUAD = 256
 UNITS = 512
 F32 = jnp.float32
@@ -68,10 +70,14 @@
     return upward * phi, phi + upward * (bell * 0.3989422804014327)
 
 
+def plus_last(values, last):
+    return jnp.concatenate([values[:MAIN], values[MAIN:] + last], axis=0)
+
+
 def attention_forward_kernel(
     segment, tails, starts, words, edge, wq, wk, wv, wo, vq, vv, vo, gain, shift,
-    q_out, k_out, v_out, e_out, total_out, mixed_out, hidden_out, normed_out, inverse_out,
-    narrow, narrow_hidden, x, bias, k_pad, v_pad, branch,
+    q_out, k_out, v_out, e_out, last_out, total_out, mixed_out, hidden_out, normed_out, inverse_out,
+    narrow, narrow_hidden, x, bias, last_bias, k_pad, v_pad, branch,
 ):
     step = pl.program_id(0)
 
@@ -87,14 +93,15 @@
         v_pad[...] = jnp.zeros_like(v_pad)
         length = TEXT if segment == 0 else tails[0]
         start = starts[0, segment]
-        row = lax.broadcasted_iota(jnp.int32, (ROWS, KEYS), 0)
-        col = lax.broadcasted_iota(jnp.int32, (ROWS, KEYS), 1)
         low, high = start + MEMORY, start + MEMORY + PICTURE
-        text = (col >= MEMORY) & (col < MEMORY + TEXT)
-        usable = jnp.logical_not(text & (col >= MEMORY + length)) & (col < SEG_ROWS)
+        row = lax.broadcasted_iota(jnp.int32, (ROWS, MAIN), 0)
+        col = lax.broadcasted_iota(jnp.int32, (ROWS, MAIN), 1)
+        usable = (col < MEMORY) | (col < MEMORY + length)
         inside = (row >= low) & (row < high) & (col >= low) & (col < high)
-        allowed = usable & ((col <= row) | inside)
-        bias[...] = jnp.where(allowed, 0.0, MASKED)
+        bias[...] = jnp.where(usable & ((col <= row) | inside), 0.0, MASKED)
+        row = lax.broadcasted_iota(jnp.int32, (ROWS - MAIN, LAST), 0)
+        col = lax.broadcasted_iota(jnp.int32, (ROWS - MAIN, LAST), 1)
+        last_bias[...] = jnp.where((col < SEG_ROWS - MAIN) & (col <= row), 0.0, MASKED)
 
     xb = narrow[...]
     q = ((nt(xb, wq[...]) + vq[...]).astype(BF16).astype(F32) * HEAD_DIM**-0.5).astype(BF16)
@@ -111,14 +118,20 @@
         for half in range(2):
             mine = (lane < HEAD_DIM) if half == 0 else (lane >= HEAD_DIM)
             qm = jnp.where(mine, q_out[:, at], jnp.zeros((), BF16))
-            scores = nt(qm, k_pad[:, at]) + bias[...]
+            scores = nt(qm, k_pad[:MAIN, at]) + bias[...]
+            last = nt(qm[MAIN:], k_pad[MAIN:, at]) + last_bias[...]
             peak = jnp.max(scores, axis=-1, keepdims=True)
+            last_peak = jnp.maximum(peak[MAIN:], jnp.max(last, axis=-1, keepdims=True))
+            peak = jnp.concatenate([peak[:MAIN], last_peak], axis=0)
             expos = jnp.exp2((scores - peak) * LOG2E)
-            total = jnp.sum(expos, axis=-1, keepdims=True)
-            narrow_e = expos.astype(BF16)
+            last = jnp.exp2((last - last_peak) * LOG2E)
+            total = plus_last(jnp.sum(expos, axis=-1, keepdims=True), jnp.sum(last, axis=-1, keepdims=True))
+            narrow_e, last = expos.astype(BF16), last.astype(BF16)
             e_out[2 * pair + half] = narrow_e
+            last_out[2 * pair + half] = last
+            weighted = plus_last(nn(narrow_e, v_pad[:MAIN, at]), nn(last, v_pad[MAIN:, at]))
             totals = jnp.where(lane == step * 4 + 2 * pair + half, total, totals)
-            halves.append(nn(narrow_e, v_pad[:, at]) / total)
+            halves.append(weighted / total)
         mixed_out[:, at] = jnp.where(lane < HEAD_DIM, halves[0], halves[1]).astype(BF16)
     total_out[...] = totals
     branch[...] += nt(mixed_out[...], wo[...])
@@ -165,19 +178,21 @@
         ],
         out_specs=[
             rows_block, rows_block, rows_block,
-            pl.BlockSpec((4, ROWS, KEYS), lambda i: (i, 0, 0)),
+            pl.BlockSpec((4, ROWS, MAIN), lambda i: (i, 0, 0)),
+            pl.BlockSpec((4, ROWS - MAIN, LAST), lambda i: (i, 0, 0)),
             stats, rows_block, full, full, stats, full, full,
         ],
         out_shape=[
             shape((ROWS, width), BF16), shape((ROWS, width), BF16), shape((ROWS, width), BF16),
-            shape((HEADS, ROWS, KEYS), BF16),
+            shape((HEADS, ROWS, MAIN), BF16), shape((HEADS, ROWS - MAIN, LAST), BF16),
             shape((ROWS, 128), F32), shape((ROWS, width), BF16),
             shape((ROWS, width), F32), shape((ROWS, width), F32), shape((ROWS, 128), F32),
             shape((ROWS, width), BF16), shape((ROWS, width), BF16),
         ],
         scratch_shapes=[
             pltpu.VMEM((ROWS, width), F32),
-            pltpu.VMEM((ROWS, KEYS), F32),
+            pltpu.VMEM((ROWS, MAIN), F32),
+            pltpu.VMEM((ROWS - MAIN, LAST), F32),
             pltpu.VMEM((KEYS, QUAD), BF16),
             pltpu.VMEM((KEYS, QUAD), BF16),
             pltpu.VMEM((ROWS, width), F32),
@@ -328,8 +343,46 @@
     )
 
 
+def backward_pair(pair, step, q, e, last, total, mixed, gm, k_pad, v_pad, gq_out, gk_out, gv_out):
+    lane = lax.broadcasted_iota(jnp.int32, (ROWS, 128), 1)
+    at = slice(128 * pair, 128 * pair + 128)
+    grad = gm[:, at].astype(F32)
+    product = grad * mixed[:, at].astype(F32)
+    totals = total[...]
+    rates, inners = [], []
+    for half in range(2):
+        mine = (lane < HEAD_DIM) if half == 0 else (lane >= HEAD_DIM)
+        head = step * 4 + 2 * pair + half
+        rate = 1.0 / jnp.sum(jnp.where(lane == head, totals, 0.0), axis=-1, keepdims=True)
+        rates.append(rate)
+        inners.append(jnp.sum(jnp.where(mine, product, 0.0), axis=-1, keepdims=True) * rate)
+    scaled = (grad * jnp.where(lane < HEAD_DIM, rates[0], rates[1])).astype(BF16)
+    scaled_t = scaled.T
+    query_t = q[:, at].T
+    gq, gk, gv = [], [], []
+    for half in range(2):
+        mine = (lane < HEAD_DIM) if half == 0 else (lane >= HEAD_DIM)
+        rows = slice(HEAD_DIM * half, HEAD_DIM * half + HEAD_DIM)
+        inner = inners[half]
+        gmm = jnp.where(mine, scaled, jnp.zeros((), BF16))
+        dp = nt(gmm, v_pad[:MAIN, at])
+        last_dp = nt(gmm[MAIN:], v_pad[MAIN:, at])
+        narrow_e, narrow_last = e[2 * pair + half], last[2 * pair + half]
+        ds = (narrow_e.astype(F32) * (dp - inner)).astype(BF16)
+        last_ds = (narrow_last.astype(F32) * (last_dp - inner[MAIN:])).astype(BF16)
+        gq.append(plus_last(nn(ds, k_pad[:MAIN, at]), nn(last_ds, k_pad[MAIN:, at])))
+        gk.append(jnp.concatenate([nn(query_t[rows, :], ds), nn(query_t[rows, MAIN:], last_ds)], axis=1))
+        gv.append(
+            jnp.concatenate([nn(scaled_t[rows, :], narrow_e), nn(scaled_t[rows, MAIN:], narrow_last)], axis=1)
+        )
+    gq_pair = jnp.where(lane < HEAD_DIM, gq[0], gq[1]) * HEAD_DIM**-0.5
+    gq_out[:, at] = gq_pair.astype(BF16)
+    gk_out[:, at] = jnp.concatenate(gk, axis=0).T[:ROWS].astype(BF16)
+    gv_out[:, at] = jnp.concatenate(gv, axis=0).T[:ROWS].astype(BF16)
+
+
 def attention_backward_kernel(
-    q, k, v, e, total, mixed, gm, dfirst, wq, wk, wv,
+    q, k, v, e, last, total, mixed, gm, dfirst, wq, wk, wv,
     gq_out, gk_out, gv_out, dx_out, vq_out, vv_out,
     k_pad, v_pad,
 ):
@@ -343,37 +396,8 @@
 
     k_pad[:ROWS, :] = k[...]
     v_pad[:ROWS, :] = v[...]
-    lane = lax.broadcasted_iota(jnp.int32, (ROWS, 128), 1)
     for pair in range(2):
-        at = slice(128 * pair, 128 * pair + 128)
-        grad = gm[:, at].astype(F32)
-        product = grad * mixed[:, at].astype(F32)
-        totals = total[...]
-        rates, inners = [], []
-        for half in range(2):
-            mine = (lane < HEAD_DIM) if half == 0 else (lane >= HEAD_DIM)
-            head = step * 4 + 2 * pair + half
-            rate = 1.0 / jnp.sum(jnp.where(lane == head, totals, 0.0), axis=-1, keepdims=True)
-            rates.append(rate)
-            inners.append(jnp.sum(jnp.where(mine, product, 0.0), axis=-1, keepdims=True) * rate)
-        scaled = (grad * jnp.where(lane < HEAD_DIM, rates[0], rates[1])).astype(BF16)
-        scaled_t = scaled.T
-        query_t = q[:, at].T
-        gq, gk, gv = [], [], []
-        for half in range(2):
-            mine = (lane < HEAD_DIM) if half == 0 else (lane >= HEAD_DIM)
-            rows = slice(HEAD_DIM * half, HEAD_DIM * half + HEAD_DIM)
-            gmm = jnp.where(mine, scaled, jnp.zeros((), BF16))
-            dp = nt(gmm, v_pad[:, at])
-            narrow_e = e[2 * pair + half]
-            ds = (narrow_e.astype(F32) * (dp - inners[half])).astype(BF16)
-            gq.append(nn(ds, k_pad[:, at]))
-            gk.append(nn(query_t[rows, :], ds))
-            gv.append(nn(scaled_t[rows, :], narrow_e))
-        gq_pair = jnp.where(lane < HEAD_DIM, gq[0], gq[1]) * HEAD_DIM**-0.5
-        gq_out[:, at] = gq_pair.astype(BF16)
-        gk_out[:, at] = jnp.concatenate(gk, axis=0).T[:ROWS].astype(BF16)
-        gv_out[:, at] = jnp.concatenate(gv, axis=0).T[:ROWS].astype(BF16)
+        backward_pair(pair, step, q, e, last, total, mixed, gm, k_pad, v_pad, gq_out, gk_out, gv_out)
     vq_out[...] = column_sum(gq_out[...].astype(F32))
     vv_out[...] = column_sum(gv_out[...].astype(F32))
     dx_out[...] += (
@@ -393,7 +417,8 @@
         grid=(width // QUAD,),
         in_specs=[
             rows_block, rows_block, rows_block,
-            pl.BlockSpec((4, ROWS, KEYS), lambda i: (i, 0, 0)),
+            pl.BlockSpec((4, ROWS, MAIN), lambda i: (i, 0, 0)),
+            pl.BlockSpec((4, ROWS - MAIN, LAST), lambda i: (i, 0, 0)),
             whole((ROWS, 128)), rows_block, rows_block, full, row_block, row_block, row_block,
         ],
         out_specs=[rows_block, rows_block, rows_block, full, sums, sums],
@@ -405,7 +430,7 @@
         compiler_params=params(),
         name="attention_backward",
     )(
-        saved["q"], saved["k"], saved["v"], saved["e"], saved["total"], saved["mixed"],
+        saved["q"], saved["k"], saved["v"], saved["e"], saved["last"], saved["total"], saved["mixed"],
         gm, dfirst, weights["q"], weights["k"], weights["v"],
     )
 
@@ -1048,12 +1073,12 @@
     words = jnp.pad(text[0].astype(F32), ((0, 0), (MEMORY, ROWS - MEMORY - TEXT), (0, 0)))
 
     def forward(segment, edge):
-        q, k, v, e, total, mixed, hidden, normed1, inverse1, xb, hb = attention_forward(
+        q, k, v, e, last, total, mixed, hidden, normed1, inverse1, xb, hb = attention_forward(
             segment, tail_lengths, picture_starts, words, edge, weights
         )
         act, slope, y, edge, normed2, inverse2 = feed_forward(hidden, hb, weights)
         saved = dict(
-            x=xb, q=q, k=k, v=v, e=e, total=total, mixed=mixed, hidden=hb,
+            x=xb, q=q, k=k, v=v, e=e, last=last, total=total, mixed=mixed, hidden=hb,
             normed1=normed1, inverse1=inverse1, act=act, slope=slope, normed2=normed2, inverse2=inverse2,
         )
         return y, edge, saved

time: 360 us -> 359 us (level)
    pallas_call x2, Pallas kernels: 35.7 us -> 31.7 us  [attention_backward(): pl.pallas_call(attention_backward_kernel, grid=(width // QUAD,), in_specs...]
where the time goes in v4:
time: 359 us; the launch traced here: 354 us
  Pallas kernels  329 us (92%)
  other arithmetic  12.1 us (3%)
  local copies, waits for them, and re-layouts  11.2 us (3%)
    pallas_call x1, Pallas kernels, fetch_by_kernel(): pl.pallas_call(gather_kernel, out_shape=[shape((width, width), BF16)] * 4...  76.1 us
    pallas_call x1, Pallas kernels, scatter_by_kernel(): pl.pallas_call(scatter_kernel, out_shape=[jax.ShapeDtypeStruct(block, F32...  74.9 us
    pallas_call x2, Pallas kernels, attention_forward(): pl.pallas_call(functools.partial(attention_forward_kernel, segment), grid...  39.8 us
    pallas_call x2, Pallas kernels, feed_forward(): pl.pallas_call(feed_forward_kernel, grid=(units // UNITS,), in_specs=[ful...  35.3 us
    pallas_call x2, Pallas kernels, feed_backward(): pl.pallas_call(functools.partial(feed_backward_kernel, segment), grid=(un...  34.3 us
    pallas_call x2, Pallas kernels, attention_backward(): pl.pallas_call(attention_backward_kernel, grid=(width // QUAD,), in_specs...  31.7 us
    pallas_call x2, Pallas kernels, product_t(): pl.pallas_call(product_kernel, grid=(units // UNITS,), in_specs=[whole((R...  22.4 us
    pallas_call x1, Pallas kernels, square_gradients(): pl.pallas_call(square_kernel, in_specs=[local] * len(operands), out_specs...  12.9 us

profile of v4, /device:TPU:0, one launch (start us, length us, event | category | flops | bytes accessed | tf_op | source)
XLA Modules:
  0.0 354.5 jit_solution(16926467989365861734)
XLA Ops:
  1.3 0.8 reshape.62
  2.1 0.8 concatenate.3
  2.9 0.6 pad.18.vectors
  3.5 1.7 copy.39.wd
  5.2 2.0 pack.1
  7.2 0.0 copy-start
  7.2 1.7 copy.49
  8.9 0.2 copy-done
  9.1 0.2 copy.48
  9.3 2.0 pad_convert_fusion.dy
  11.3 2.0 pad_convert_fusion.1.words
  13.3 76.1 %gather.1 = (bf16[768,768]{1,0:T(8,128)(2,1)}, bf16[768,768]{1,0:T(8,128)(2,1)}, bf16[768,768]{1,0:T(8,128)(2,1)}, bf16[768,768]{1,0:T(8,128)(2,1)}, f32[1,768]{...) custom-call(bf16[112,768]{1,0:T(8,128)(2,1)} %get-tuple-element.99.s, ...), custom_call_target="tpu_custom_call" | custom-call | tf_op jit(solution)/shard_map/gather/pallas_call | solution.py:689
  89.3 19.6 %attention_forward.2 = (bf16[528,768]{1,0:T(8,128)(2,1)}, bf16[528,768]{1,0:T(8,128)(2,1)}, bf16[528,768]{1,0:T(8,128)(2,1)}, bf16[12,528,512]{2,1,0:T(8,128)(2,...) custom-call(s32[1]{0:T(128)S(6)} %copy.52.tails, ...), custom_call_target="tpu_custom_call" | custom-call | tf_op jit(solution)/shard_map/attention_forward/pallas_call | solution.py:171
  109.0 17.6 %feed_forward.2 = (bf16[528,3072]{1,0:T(8,128)(2,1)}, bf16[528,3072]{1,0:T(8,128)(2,1)}, bf16[528,768]{1,0:T(8,128)(2,1)}, f32[16,768]{1,0:T(8,128)}, f32[528,768]{1,0:T(8,128)}, /*index=5*/f32[528,128]{1,0:T(8,128)}) custom-call(f32[528,768]{1,0:T(8,128)} %get-tuple-element.110.hidden, bf16[528,768]{1,0:T(8,128)(2,1)} %get-tuple-element.111.narrow.left1, ...), custom_call_target="tpu_custom_call" | custom-call | tf_op jit(solution)/shard_map/feed_forward/pallas_call | solution.py:242
  126.6 20.1 %attention_forward.3 = (bf16[528,768]{1,0:T(8,128)(2,1)}, bf16[528,768]{1,0:T(8,128)(2,1)}, bf16[528,768]{1,0:T(8,128)(2,1)}, bf16[12,528,512]{2,1,0:T(8,128)(2,...) custom-call(s32[1]{0:T(128)S(6)} %copy.52.tails, ...), custom_call_target="tpu_custom_call" | custom-call | tf_op jit(solution)/shard_map/attention_forward/pallas_call | solution.py:171
  146.7 0.0 copy-start.1
  146.8 17.7 %feed_forward.3 = (bf16[528,3072]{1,0:T(8,128)(2,1)}, bf16[528,3072]{1,0:T(8,128)(2,1)}, bf16[528,768]{1,0:T(8,128)(2,1)}, f32[16,768]{1,0:T(8,128)}, f32[528,768]{1,0:T(8,128)}, /*index=5*/f32[528,128]{1,0:T(8,128)}) custom-call(f32[528,768]{1,0:T(8,128)} %get-tuple-element.120.hidden, bf16[528,768]{1,0:T(8,128)(2,1)} %get-tuple-element.121.narrow.left2, ...), custom_call_target="tpu_custom_call" | custom-call | tf_op jit(solution)/shard_map/feed_forward/pallas_call | solution.py:242
  164.4 0.0 copy-done.1
  164.4 4.5 %broadcast_select_fusion = bf16[1,2,522,768]{3,1,2,0:T(2,128)(2,1)} fusion(pred[2]{0:T(512)(128)(4,1)S(1)} %iota_compare_fusion, bf16[522,768]{1,0:T(8,128)(2,1)} %bitcast.58, bf16[522,768]{1,0:T(8,128)(2,1)S(1)} %bitcast.57), kind=kLoop, calls=%fused_computation | loop fusion | flops 801792 | bytes 3207170 | tf_op jit(solution)/shard_map/jit(_where)/select_n | solution.py:1089
  168.9 17.3 %feed_backward.2 = (bf16[528,768]{1,0:T(8,128)(2,1)}, bf16[528,3072]{1,0:T(8,128)(2,1)}, bf16[528,768]{1,0:T(8,128)(2,1)}, f32[528,768]{1,0:T(8,128)}, bf16[528,...) custom-call(f32[2,528,768]{2,1,0:T(8,128)} %pad_convert_fusion.dy, ...), custom_call_target="tpu_custom_call" | custom-call | tf_op jit(solution)/shard_map/feed_backward/pallas_call | solution.py:316
  186.2 15.8 %attention_backward.2 = (bf16[528,768]{1,0:T(8,128)(2,1)}, bf16[528,768]{1,0:T(8,128)(2,1)}, bf16[528,768]{1,0:T(8,128)(2,1)}, f32[528,768]{1,0:T(8,128)}, f32[1,768]{1,0:T(1,128)}, /*index=5*/f32[1,768]{1,0:T(1,128)}) custom-call(bf16[528,768]{1,0:T(8,128)(2,1)} %get-tuple-element.130.q, bf16[528,768]{1,0:T(8,128)(2,1)} %get-tuple-element.131.k, ...), custom_call_target="tpu_custom_call" | custom-call | tf_op jit(solution)/shard_map/attention_backward/pallas_call | solution.py:415
  202.1 17.0 %feed_backward.3 = (bf16[528,768]{1,0:T(8,128)(2,1)}, bf16[528,3072]{1,0:T(8,128)(2,1)}, bf16[528,768]{1,0:T(8,128)(2,1)}, f32[528,768]{1,0:T(8,128)}, bf16[528,...) custom-call(f32[2,528,768]{2,1,0:T(8,128)} %pad_convert_fusion.dy, ...), custom_call_target="tpu_custom_call" | custom-call | tf_op jit(solution)/shard_map/feed_backward/pallas_call | solution.py:316
  219.0 11.1 %weight_gradient.3.lower = bf16[768,3072]{1,0:T(8,128)(2,1)} custom-call(bf16[528,768]{1,0:T(8,128)(2,1)} %get-tuple-element.173.left1, bf16[528,768]{1,0:T(8,128)(2,1)} %get-tuple-element.174.left2, bf16[528,3072]{1,0:T(8,128)(2,1)} %get-tuple-element.175.right1, bf16[528,3072]{1,0:T(8,128)(2,1)} %get-tuple-element.176.right2), custom_call_target="tpu_custom_call" | custom-call | tf_op jit(solution)/shard_map/weight_gradient/pallas_call | solution.py:930
  230.1 11.3 %weight_gradient.2.upper = bf16[768,3072]{1,0:T(8,128)(2,1)} custom-call(bf16[528,768]{1,0:T(8,128)(2,1)} %get-tuple-element.111.narrow.left1, bf16[528,768]{1,0:T(8,128)(2,1)} %get-tuple-element.121.narrow.left2, bf16[528,3072]{1,0:T(8,128)(2,1)} %get-tuple-element.171.right1, bf16[528,3072]{1,0:T(8,128)(2,1)} %get-tuple-element.172.right2), custom_call_target="tpu_custom_call" | custom-call | tf_op jit(solution)/shard_map/weight_gradient/pallas_call | solution.py:930
  241.4 15.8 %attention_backward.3 = (bf16[528,768]{1,0:T(8,128)(2,1)}, bf16[528,768]{1,0:T(8,128)(2,1)}, bf16[528,768]{1,0:T(8,128)(2,1)}, f32[528,768]{1,0:T(8,128)}, f32[1,768]{1,0:T(1,128)}, /*index=5*/f32[1,768]{1,0:T(1,128)}) custom-call(bf16[528,768]{1,0:T(8,128)(2,1)} %get-tuple-element.123.q, bf16[528,768]{1,0:T(8,128)(2,1)} %get-tuple-element.124.k, ...), custom_call_target="tpu_custom_call" | custom-call | tf_op jit(solution)/shard_map/attention_backward/pallas_call | solution.py:415
  257.2 12.9 %square_gradients.1.square = bf16[32,112,768]{2,1,0:T(8,128)(2,1)} custom-call(bf16[528,768]{1,0:T(8,128)(2,1)} %get-tuple-element.153.gq1, bf16[528,768]{1,0:T(8,128)(2,1)} %get-tuple-element.154.gq2, bf16[528,768]{1,0:T(8,128)(2,1)} %get-tuple-element.155.gk1, bf16[528,768]{1,0:T(8,128)(2,1)} %get-tuple-element.156.gk2, ...), custom_call_target="tpu_custom_call" | custom-call | tf_op jit(solution)/shard_map/square_gradients/pallas_call | solution.py:991
  270.1 0.0 copy-start.2
  270.1 74.9 %scatter.1 = (f32[112,768]{1,0:T(8,128)S(1)}, f32[192,384]{1,0:T(8,128)S(1)}, f32[96,768]{1,0:T(8,128)S(1)}) custom-call(bf16[32,112,768]{2,1,0:T(8,128)(2,1)} %square_gradients.1.square, bf16[768,3072]{1,0:T(8,128)(2,1)} %weight_gradient.2.upper, bf16[768,3072]{1,0:T(8,128)(2,1)} %weight_gradient.3.lower), custom_call_target="tpu_custom_call" | custom-call | tf_op jit(solution)/shard_map/scatter/pallas_call | solution.py:898
  345.1 0.7 reshape.64
  345.7 0.5 slice_bitcast_fusion.4
  346.3 0.0 copy-done.2
  346.3 0.6 fusion
  346.9 0.1 slice.72
  347.1 0.2 copy.45
  347.2 0.8 slice_bitcast_fusion
  348.0 1.5 slice.73
  349.5 3.1 select_convert_fusion
  352.6 0.7 copy.53
  353.3 0.7 copy.54
  (3 shorter events, 0.0 us)
Async XLA Ops:
  7.2 1.9 copy-start
  146.7 17.7 %copy-start.1 = (bf16[528,768]{1,0:T(8,128)(2,1)S(1)}, bf16[528,768]{1,0:T(8,128)(2,1)}, u32[]{:S(2)}) copy-start(bf16[528,768]{1,0:T(8,128)(2,1)} %get-tuple-element.118) | copy-start | bytes 2433028
  270.1 76.1 %copy-start.2 = (f32[528,768]{1,0:T(8,128)S(1)}, f32[528,768]{1,0:T(8,128)}, u32[]{:S(2)}) copy-start(f32[528,768]{1,0:T(8,128)} %get-tuple-element.152) | copy-start | bytes 4866052

commit v5 on v4

--- a/solution.py
+++ b/solution.py
@@ -704,214 +704,6 @@
     return dict(zip(names, whole_arrays))
 
 
-def scatter_kernel(square, upper, lower, square_out, upper_out, lower_out, *scratch):
-    mine, theirs, corner, side, lined = (scratch[3 * at : 3 * at + 3] for at in range(5))
-    send, recv, own = scratch[15:]
-    rows, cols = ROWS_MESH, square.shape[0] // ROWS_MESH
-    place = Place(cols)
-    outs = (square_out, upper_out, lower_out)
-    length = place.length
-
-    def source(which, row, col):
-        count, wide = outs[which].shape
-        if which == 0:
-            return square.at[row * cols + col]
-        array, high, level = (upper, row, col) if which == 1 else (lower, col, row)
-        return array.at[
-            pl.ds(pl.multiple_of(high * count, 16), count),
-            pl.ds(pl.multiple_of(level * wide, 128), wide),
-        ]
-
-    def load(which, row, line):
-        return pltpu.make_async_copy(
-            source(which, row, 2 * line + place.core),
-            mine[which].at[row * length + line], own.at[which, row * length + line],
-        )
-
-    def share(which, row, line, core):
-        at = row * length + line
-        return pltpu.make_async_remote_copy(
-            src_ref=source(which, row, 2 * line + core), dst_ref=theirs[which].at[at],
-            send_sem=send.at[which, SHARE + row, line], recv_sem=recv.at[which, SHARE + row, line],
-            device_id=place.partner, device_id_type=MESH_IDS,
-        )
-
-    def remote(which, kind, line, here, there, device):
-        return pltpu.make_async_remote_copy(
-            src_ref=here, dst_ref=there,
-            send_sem=send.at[which, kind, line], recv_sem=recv.at[which, kind, line],
-            device_id=device, device_id_type=MESH_IDS,
-        )
-
-    def corner_copy(which, kind, line):
-        begin, size = splits(outs[which].shape[0])[kind - HALF_ACROSS]
-        part = pl.ds(begin, size)
-        here = mine[which].at[place.corner_row * length + line, part]
-        there = corner[which].at[line, part]
-        return remote(which, kind, line, here, there, place.across if kind == HALF_ACROSS else place.along)
-
-    def side_copy(which, kind, line):
-        row, device = (place.across_row, place.across) if kind == ACROSS else (place.along_row, place.along)
-        here = mine[which].at[row * length + line]
-        return remote(which, kind, line, here, side[which].at[kind - ACROSS, line], device)
-
-    def line_copy(which, kind, line):
-        here = mine[which].at[place.row * length + line]
-        return remote(which, kind, line, here, lined[which].at[kind, line], place.up if kind == Z_UP else place.down)
-
-    def add(which, at, arrived, part=None):
-        block = mine[which].at[at] if part is None else mine[which].at[at, pl.ds(*part)]
-        block[...] = (block[...].astype(F32) + arrived[...].astype(F32)).astype(BF16)
-
-    place.greet()
-
-    def spread(distance, visit):
-        place.at_distance(distance, lambda line, upward: visit(line))
-
-    farthest = range(length - 1, -1, -1)
-    order = ("corner_row", "across_row", "along_row", "row")
-    for which in range(3):
-        for distance in farthest:
-
-            def begin(line):
-                for name in order:
-                    row = getattr(place, name)
-                    load(which, row, line).start()
-                    share(which, row, line, place.other_core).start()
-
-            spread(distance, begin)
-
-    def merge(which, row, line):
-        load(which, row, line).wait()
-        share(which, row, line, place.core).wait_recv()
-        at = row * length + line
-        add(which, at, theirs[which].at[at])
-
-    def cores(which, distance):
-        def visit(line):
-            merge(which, place.corner_row, line)
-            merge(which, place.across_row, line)
-            corner_copy(which, HALF_ACROSS, line).start()
-            corner_copy(which, HALF_ALONG, line).start()
-            merge(which, place.along_row, line)
-            merge(which, place.row, line)
-
-        spread(distance, visit)
-
-    def corners(which, distance):
-        first, second = splits(outs[which].shape[0])
-
-        def visit(line):
-            corner_copy(which, HALF_ACROSS, line).wait_recv()
-            add(which, place.along_row * length + line, corner[which].at[line, pl.ds(*first)], first)
-            corner_copy(which, HALF_ALONG, line).wait_recv()
-            add(which, place.across_row * length + line, corner[which].at[line, pl.ds(*second)], second)
-            side_copy(which, ALONG, line).start()
-            side_copy(which, ACROSS, line).start()
-
-        spread(distance, visit)
-
-    def sides(which, distance):
-        def visit(line):
-            at = place.row * length + line
-            side_copy(which, ACROSS, line).wait_recv()
-            add(which, at, side[which].at[0, line])
-            side_copy(which, ALONG, line).wait_recv()
-            add(which, at, side[which].at[1, line])
-
-        spread(distance, visit)
-
-    def lines(which, distance):
-        def visit(line, downward):
-            at = place.row * length + line
-            kind = Z_DOWN if downward else Z_UP
-            onward = place.line < length - 1 if downward else place.line > 0
-
-            @pl.when(onward)
-            def _():
-                line_copy(which, kind, line).wait_recv()
-                add(which, at, lined[which].at[kind, line])
-
-            line_copy(which, kind, line).start()
-
-        place.at_distance(distance, visit)
-
-    def result(which):
-        at = place.row * length + place.line
-        for kind, there in ((Z_UP, place.line > 0), (Z_DOWN, place.line < length - 1)):
-
-            @pl.when(there)
-            def _():
-                line_copy(which, kind, place.line).wait_recv()
-                add(which, at, lined[which].at[kind, place.line])
-
-        outs[which][...] = mine[which][at].astype(F32)
-
-    def drain(which):
-        for distance in farthest:
-
-            def visit(line, downward):
-                for row in range(rows):
-                    share(which, row, line, place.other_core).wait_send()
-                for kind in (HALF_ACROSS, HALF_ALONG):
-                    corner_copy(which, kind, line).wait_send()
-                for kind in (ACROSS, ALONG):
-                    side_copy(which, kind, line).wait_send()
-                if downward is not None:
-                    line_copy(which, Z_DOWN if downward else Z_UP, line).wait_send()
-
-            place.at_distance(distance, visit)
-
-    for step in range(length + 3 + 4):
-        for which in range(3):
-            stage = step - 2 * which
-            if 0 <= stage < length:
-                cores(which, length - 1 - stage)
-            if 1 <= stage < length + 1:
-                corners(which, length - stage)
-            if 2 <= stage < length + 2:
-                sides(which, length + 1 - stage)
-            if 3 <= stage < length + 2:
-                lines(which, length + 2 - stage)
-            if stage == length + 2:
-                result(which)
-    for which in range(3):
-        drain(which)
-
-
-def scatter_by_kernel(square, upper, lower):
-    cols = square.shape[0] // ROWS_MESH
-    length = cols // 2
-    count, wide = square.shape[1:]
-    blocks = (
-        (count, wide),
-        (upper.shape[0] // ROWS_MESH, upper.shape[1] // cols),
-        (lower.shape[0] // cols, lower.shape[1] // ROWS_MESH),
-    )
-    kinds = (3, SHARE + ROWS_MESH, length)
-    anywhere, local = pl.BlockSpec(memory_space=pl.ANY), pl.BlockSpec(memory_space=pltpu.VMEM)
-    buffers = [
-        pltpu.VMEM((*lead, *block), BF16)
-        for lead in ((ROWS_MESH * length,), (ROWS_MESH * length,), (length,), (2, length), (2, length))
-        for block in blocks
-    ]
-    return pl.pallas_call(
-        scatter_kernel,
-        out_shape=[jax.ShapeDtypeStruct(block, F32) for block in blocks],
-        in_specs=[anywhere] * 3,
-        out_specs=[local] * 3,
-        scratch_shapes=[
-            *buffers,
-            pltpu.SemaphoreType.DMA(kinds), pltpu.SemaphoreType.DMA(kinds),
-            pltpu.SemaphoreType.DMA((3, ROWS_MESH * length)),
-        ],
-        compiler_params=pltpu.CompilerParams(
-            collective_id=1, has_side_effects=True, vmem_limit_bytes=50 * 1024 * 1024
-        ),
-        name="scatter",
-    )(square, upper, lower)
-
-
 def joined(first, second):
     return jnp.concatenate([first, second], axis=0)
 
@@ -942,61 +734,335 @@
 SUM_ROWS = (5, 3, 4, 2, 0, 1)
 
 
-def square_kernel(
-    gq1, gq2, gk1, gk2, gv1, gv2, gb1, gb2, x1, x2, mixed1, mixed2,
-    vq1, vq2, vv1, vv2, sums1, sums2, vu1, vu2, out, total
+class Scatter:
+    def __init__(self, square, upper, lower, outs, scratch):
+        self.square, self.upper, self.lower, self.outs = square, upper, lower, outs
+        held, self.theirs, self.corner, self.side, self.lined = (
+            scratch[:2], scratch[2:5], scratch[5:8], scratch[8:11], scratch[11:14]
+        )
+        self.held = (None, *held)
+        self.send, self.recv, self.own = scratch[14:]
+        self.cols = square.shape[0] // ROWS_MESH
+        self.place = Place(self.cols)
+        self.length = self.place.length
+        self.stages = self.length + 3
+
+    def source(self, which, row, col):
+        count, wide = self.outs[which].shape
+        if which == 0:
+            return self.square.at[row * self.cols + col]
+        array, high, level = (self.upper, row, col) if which == 1 else (self.lower, col, row)
+        return array.at[
+            pl.ds(pl.multiple_of(high * count, 16), count),
+            pl.ds(pl.multiple_of(level * wide, 128), wide),
+        ]
+
+    def mine(self, which, row, line, part=None):
+        if which == 0:
+            array, at = self.square, row * self.cols + 2 * line + self.place.core
+        else:
+            array, at = self.held[which], row * self.length + line
+        return array.at[at] if part is None else array.at[at, pl.ds(*part)]
+
+    def load(self, which, row, line):
+        at = row * self.length + line
+        return pltpu.make_async_copy(
+            self.source(which, row, 2 * line + self.place.core),
+            self.held[which].at[at], self.own.at[which - 1, at],
+        )
+
+    def remote(self, which, kind, line, here, there, device):
+        return pltpu.make_async_remote_copy(
+            src_ref=here, dst_ref=there,
+            send_sem=self.send.at[which, kind, line], recv_sem=self.recv.at[which, kind, line],
+            device_id=device, device_id_type=MESH_IDS,
+        )
+
+    def share(self, which, row, line, core):
+        here = self.source(which, row, 2 * line + core)
+        there = self.theirs[which].at[row * self.length + line]
+        return self.remote(which, SHARE + row, line, here, there, self.place.partner)
+
+    def corner_copy(self, which, kind, line):
+        part = splits(self.outs[which].shape[0])[kind - HALF_ACROSS]
+        here = self.mine(which, self.place.corner_row, line, part)
+        there = self.corner[which].at[line, pl.ds(*part)]
+        device = self.place.across if kind == HALF_ACROSS else self.place.along
+        return self.remote(which, kind, line, here, there, device)
+
+    def side_copy(self, which, kind, line):
+        place = self.place
+        row, device = (place.across_row, place.across) if kind == ACROSS else (place.along_row, place.along)
+        there = self.side[which].at[kind - ACROSS, line]
+        return self.remote(which, kind, line, self.mine(which, row, line), there, device)
+
+    def line_copy(self, which, kind, line):
+        device = self.place.up if kind == Z_UP else self.place.down
+        here = self.mine(which, self.place.row, line)
+        return self.remote(which, kind, line, here, self.lined[which].at[kind, line], device)
+
+    def add(self, block, arrived):
+        block[...] = (block[...].astype(F32) + arrived[...].astype(F32)).astype(BF16)
+
+    def begin(self, which):
+        place = self.place
+        for distance in range(self.length - 1, -1, -1):
+
+            def visit(line, downward):
+                for row in (place.corner_row, place.across_row, place.along_row, place.row):
+                    if which:
+                        self.load(which, row, line).start()
+                    self.share(which, row, line, place.other_core).start()
+
+            place.at_distance(distance, visit)
+
+    def merge(self, which, row, line):
+        if which:
+            self.load(which, row, line).wait()
+        self.share(which, row, line, self.place.core).wait_recv()
+        self.add(self.mine(which, row, line), self.theirs[which].at[row * self.length + line])
+
+    def cores(self, which, distance):
+        place = self.place
+
+        def visit(line, downward):
+            self.merge(which, place.corner_row, line)
+            self.merge(which, place.across_row, line)
+            self.corner_copy(which, HALF_ACROSS, line).start()
+            self.corner_copy(which, HALF_ALONG, line).start()
+            self.merge(which, place.along_row, line)
+            self.merge(which, place.row, line)
+
+        place.at_distance(distance, visit)
+
+    def corners(self, which, distance):
+        place = self.place
+        first, second = splits(self.outs[which].shape[0])
+
+        def visit(line, downward):
+            for kind, row, part in (
+                (HALF_ACROSS, place.along_row, first), (HALF_ALONG, place.across_row, second)
+            ):
+                self.corner_copy(which, kind, line).wait_recv()
+                self.add(self.mine(which, row, line, part), self.corner[which].at[line, pl.ds(*part)])
+            self.side_copy(which, ALONG, line).start()
+            self.side_copy(which, ACROSS, line).start()
+
+        place.at_distance(distance, visit)
+
+    def sides(self, which, distance):
+        def visit(line, downward):
+            for kind in (ACROSS, ALONG):
+                self.side_copy(which, kind, line).wait_recv()
+                self.add(self.mine(which, self.place.row, line), self.side[which].at[kind - ACROSS, line])
+
+        self.place.at_distance(distance, visit)
+
+    def lines(self, which, distance):
+        place = self.place
+
+        def visit(line, downward):
+            kind = Z_DOWN if downward else Z_UP
+            onward = place.line < self.length - 1 if downward else place.line > 0
+
+            @pl.when(onward)
+            def _():
+                self.line_copy(which, kind, line).wait_recv()
+                self.add(self.mine(which, place.row, line), self.lined[which].at[kind, line])
+
+            self.line_copy(which, kind, line).start()
+
+        place.at_distance(distance, visit)
+
+    def result(self, which):
+        place = self.place
+        block = self.mine(which, place.row, place.line)
+        for kind, there in ((Z_UP, place.line > 0), (Z_DOWN, place.line < self.length - 1)):
+
+            @pl.when(there)
+            def _():
+                self.line_copy(which, kind, place.line).wait_recv()
+                self.add(block, self.lined[which].at[kind, place.line])
+
+        self.outs[which][...] = block[...].astype(F32)
+
+    def stage(self, which, stage):
+        length = self.length
+        if 0 <= stage < length:
+            self.cores(which, length - 1 - stage)
+        if 1 <= stage < length + 1:
+            self.corners(which, length - stage)
+        if 2 <= stage < length + 2:
+            self.sides(which, length + 1 - stage)
+        if 3 <= stage < length + 2:
+            self.lines(which, length + 2 - stage)
+        if stage == length + 2:
+            self.result(which)
+
+    def drain(self, which):
+        for distance in range(self.length):
+
+            def visit(line, downward):
+                for row in range(ROWS_MESH):
+                    self.share(which, row, line, self.place.other_core).wait_send()
+                for kind in (HALF_ACROSS, HALF_ALONG):
+                    self.corner_copy(which, kind, line).wait_send()
+                for kind in (ACROSS, ALONG):
+                    self.side_copy(which, kind, line).wait_send()
+                if downward is not None:
+                    self.line_copy(which, Z_DOWN if downward else Z_UP, line).wait_send()
+
+            self.place.at_distance(distance, visit)
+
+
+PAIRS = QUAD // 128
+
+
+def last_backward_kernel(
+    q, k, v, e, last, total, mixed, gm, dfirst, wq, wk, wv,
+    gq2, gk2, gv2, gb1, gb2, x1, x2, mixed1, mixed2, vq2, vv2, sums1, sums2, vu1, vu2, upper, lower,
+    dx_out, square_out, upper_out, lower_out,
+    k_pad, v_pad, gq, gk, gv, vq, vv, totals, blocks, *scratch,
 ):
-    rows = ROWS_MESH
-    cols = out.shape[0] // rows
-    width = out.shape[2]
-    across, depth = width // cols, width // rows
-    sums = sums1[...] + sums2[...]
-    wide = vu1[...] + vu2[...]
-    vectors = jnp.concatenate(
-        [vq1[...] + vq2[...], vv1[...] + vv2[...]] + [sums[at : at + 1] for at in SUM_ROWS], axis=0
+    step = pl.program_id(0)
+    quads = gq.shape[0]
+    travel = Scatter(blocks, upper, lower, (square_out, upper_out, lower_out), scratch)
+    moves = [(which, at - 2 * which + 2) for at in range(travel.stages + 2) for which in (1, 2)]
+    moves = [(which, stage) for which, stage in moves if 0 <= stage < travel.stages]
+    slots = quads * PAIRS + 4
+
+    def advance(slot):
+        for which, stage in moves[len(moves) * slot // slots : len(moves) * (slot + 1) // slots]:
+            travel.stage(which, stage)
+
+    @pl.when(step == 0)
+    def _():
+        travel.place.greet()
+        travel.begin(1)
+        travel.begin(2)
+        dx_out[...] = dfirst[...]
+        k_pad[...] = jnp.zeros_like(k_pad)
+        v_pad[...] = jnp.zeros_like(v_pad)
+
+    @pl.when(step < quads)
+    def _():
+        outs = gq.at[step], gk.at[step], gv.at[step]
+        k_pad[:ROWS, :] = k[...]
+        v_pad[:ROWS, :] = v[...]
+        for pair in range(PAIRS):
+            backward_pair(pair, step, q, e, last, total, mixed, gm, k_pad, v_pad, *outs)
+            for at in range(quads):
+                pl.when(step == at)(functools.partial(advance, at * PAIRS + pair))
+        vq[step] = column_sum(outs[0][...].astype(F32))
+        vv[step] = column_sum(outs[2][...].astype(F32))
+        dx_out[...] += nn(outs[0][...], wq[...]) + nn(outs[1][...], wk[...]) + nn(outs[2][...], wv[...])
+
+    @pl.when(step == quads)
+    def _():
+        rows, cols = ROWS_MESH, travel.cols
+        width = blocks.shape[2]
+        across, depth = width // cols, width // rows
+        inputs = joined(x1[...], x2[...])
+        for at, (first, second) in enumerate(((gq, gq2), (gk, gk2), (gv, gv2))):
+            for quad in range(quads):
+                part = slice(QUAD * quad, QUAD * quad + QUAD)
+                totals[at, part, :] = nn(joined(first[quad], second[:, part]).T, inputs).astype(BF16)
+            advance(quads * PAIRS + at)
+        totals[3] = nn(joined(gb1[...], gb2[...]).T, joined(mixed1[...], mixed2[...])).astype(BF16)
+        sums = sums1[...] + sums2[...]
+        wide = vu1[...] + vu2[...]
+        vectors = jnp.concatenate(
+            [
+                jnp.concatenate([vq[quad] for quad in range(quads)], axis=1) + vq2[...],
+                jnp.concatenate([vv[quad] for quad in range(quads)], axis=1) + vv2[...],
+            ]
+            + [sums[at : at + 1] for at in SUM_ROWS],
+            axis=0,
+        )
+        share = wide.shape[1] // cols // across
+        for col in range(cols):
+            begin = across * col
+            narrow = jnp.concatenate(
+                [vectors[:, begin : begin + across]]
+                + [wide[:, across * (col * share + at) : across * (col * share + at + 1)] for at in range(share)]
+                + [jnp.zeros((LINES - 8 - share, across), F32)],
+                axis=0,
+            )
+            narrow = jnp.pad(narrow, ((0, 0), (0, width - across))).astype(BF16)
+            for row in range(rows):
+                block = row * cols + col
+                blocks[block, :across, :] = jnp.concatenate(
+                    [totals[at, begin : begin + across, depth * row : depth * row + depth] for at in range(4)],
+                    axis=1,
+                )
+                blocks[block, across:, :] = narrow
+        travel.begin(0)
+        advance(slots - 1)
+        for stage in range(travel.stages):
+            travel.stage(0, stage)
+        for which in range(3):
+            travel.drain(which)
+
+
+def last_backward(saved1, saved2, gm, dfirst, weights, grads1, grads2, upper, lower, cols):
+    width = dfirst.shape[1]
+    quads = width // QUAD
+    length = cols // 2
+    across, depth = width // cols, width // ROWS_MESH
+    units = upper.shape[1]
+    sizes = ((across + LINES, width), (depth, units // cols), (across, units // ROWS_MESH))
+    kinds = (3, SHARE + ROWS_MESH, length)
+
+    def once(array):
+        return pl.BlockSpec(array.shape, lambda i: (0,) * array.ndim, pipeline_mode=pl.Buffered(1))
+
+    def turn(i):
+        return jnp.minimum(i, quads - 1)
+
+    rows_block = pl.BlockSpec((ROWS, QUAD), lambda i: (0, turn(i)))
+    row_block = pl.BlockSpec((QUAD, width), lambda i: (turn(i), 0))
+    anywhere = pl.BlockSpec(memory_space=pl.ANY)
+    singles = (
+        grads2["gq"], grads2["gk"], grads2["gv"], grads1["gb"], grads2["gb"], saved1["x"], saved2["x"],
+        saved1["mixed"], saved2["mixed"], grads2["vq"], grads2["vv"],
+        grads1["sums"], grads2["sums"], grads1["vu"], grads2["vu"],
     )
-    lefts = ((gq1, gq2), (gk1, gk2), (gv1, gv2), (gb1, gb2))
-    for at, (left1, left2) in enumerate(lefts):
-        right1, right2 = (x1, x2) if at < 3 else (mixed1, mixed2)
-        left, right = joined(left1[...], left2[...]), joined(right1[...], right2[...])
-        total[at] = nn(left.T, right).astype(BF16)
-    share = wide.shape[1] // cols // across
-    for col in range(cols):
-        begin = across * col
-        narrow = jnp.concatenate(
-            [vectors[:, begin : begin + across]]
-            + [wide[:, across * (col * share + at) : across * (col * share + at + 1)] for at in range(share)]
-            + [jnp.zeros((LINES - 8 - share, across), F32)],
-            axis=0,
-        )
-        narrow = jnp.pad(narrow, ((0, 0), (0, out.shape[2] - across))).astype(BF16)
-        for row in range(rows):
-            block = row * cols + col
-            out[block, :across, :] = jnp.concatenate(
-                [total[at, begin : begin + across, depth * row : depth * row + depth] for at in range(4)],
-                axis=1,
-            )
-            out[block, across:, :] = narrow
-
-
-def square_gradients(grads1, grads2, saved1, saved2, cols):
-    width = grads1["gq"].shape[1]
-    operands = []
-    for name in ("gq", "gk", "gv", "gb"):
-        operands += [grads1[name], grads2[name]]
-    operands += [saved1["x"], saved2["x"], saved1["mixed"], saved2["mixed"]]
-    for name in ("vq", "vv", "sums", "vu"):
-        operands += [grads1[name], grads2[name]]
-    local = pl.BlockSpec(memory_space=pltpu.VMEM)
+    buffers = [
+        pltpu.VMEM((*lead, *size), BF16)
+        for lead in ((ROWS_MESH * length,), (ROWS_MESH * length,), (length,), (2, length), (2, length))
+        for size in sizes
+    ][1:]
+    shape = jax.ShapeDtypeStruct
     return pl.pallas_call(
-        square_kernel,
-        in_specs=[local] * len(operands),
-        out_specs=local,
-        out_shape=jax.ShapeDtypeStruct((ROWS_MESH * cols, width // cols + LINES, width), BF16),
-        scratch_shapes=[pltpu.VMEM((4, width, width), BF16)],
-        compiler_params=pltpu.CompilerParams(vmem_limit_bytes=58 * 1024 * 1024),
-        name="square_gradients",
-    )(*operands)
+        last_backward_kernel,
+        grid=(quads + 1,),
+        in_specs=[
+            rows_block, rows_block, rows_block,
+            pl.BlockSpec((4, ROWS, MAIN), lambda i: (turn(i), 0, 0)),
+            pl.BlockSpec((4, ROWS - MAIN, LAST), lambda i: (turn(i), 0, 0)),
+            once(saved1["total"]), rows_block, rows_block, once(dfirst), row_block, row_block, row_block,
+            *(once(item) for item in singles), anywhere, anywhere,
+        ],
+        out_specs=[whole((ROWS, width)), *(whole(size) for size in sizes)],
+        out_shape=[shape((ROWS, width), F32), *(shape(size, F32) for size in sizes)],
+        scratch_shapes=[
+            pltpu.VMEM((KEYS, QUAD), BF16), pltpu.VMEM((KEYS, QUAD), BF16),
+            *[pltpu.VMEM((quads, ROWS, QUAD), BF16)] * 3, *[pltpu.VMEM((quads, 1, QUAD), F32)] * 2,
+            pltpu.VMEM((4, width, width), BF16),
+            pltpu.VMEM((ROWS_MESH * cols, *sizes[0]), BF16),
+            *buffers,
+            pltpu.SemaphoreType.DMA(kinds), pltpu.SemaphoreType.DMA(kinds),
+            pltpu.SemaphoreType.DMA((2, ROWS_MESH * length)),
+        ],
+        compiler_params=pltpu.CompilerParams(
+            dimension_semantics=("arbitrary",), collective_id=1, has_side_effects=True,
+            vmem_limit_bytes=63 * 1024 * 1024,
+        ),
+        name="last_backward",
+    )(
+        saved1["q"], saved1["k"], saved1["v"], saved1["e"], saved1["last"], saved1["total"], saved1["mixed"],
+        gm, dfirst, weights["q"], weights["k"], weights["v"], *singles, upper, lower,
+    )
 
 
 def gather_all(part):
@@ -1092,27 +1158,32 @@
     y2, edge2, saved2 = forward(1, edge1)
     layer_output = paired(y1, y2, 0, SEG_ROWS)
 
-    def backward(segment, later, saved):
+    def feed(segment, later, saved):
         gd, gu, gb, dfirst, gm, vu, sums = feed_backward(segment, cotangent, later, saved, weights)
+        return gm, dfirst, dict(gd=gd, gu=gu, gb=gb, vu=vu, sums=sums)
+
+    def attend(saved, gm, dfirst):
         gq, gk, gv, dx, vq, vv = attention_backward(saved, gm, dfirst, weights)
-        return dx, dict(gd=gd, gu=gu, gb=gb, gq=gq, gk=gk, gv=gv, vu=vu, sums=sums, vq=vq, vv=vv)
+        return dx, dict(gq=gq, gk=gk, gv=gv, vq=vq, vv=vv)
 
     cotangent = jnp.pad(grad_out[0].astype(F32), ((0, 0), (0, ROWS - SEG_ROWS), (0, 0)))
-    dx2, grads2 = backward(1, saved2["normed2"], saved2)
-    dx1, grads1 = backward(0, dx2, saved1)
-    memory_grad = (dx1[:MEMORY] + dx1[MEMORY + TEXT : SEG_ROWS]).astype(BF16)[None]
-    text_grad = paired(dx1, dx2, MEMORY, TEXT)
-
+    gm2, dfirst2, grads2 = feed(1, saved2["normed2"], saved2)
+    dx2, more = attend(saved2, gm2, dfirst2)
+    grads2.update(more)
+    gm1, dfirst1, grads1 = feed(0, dx2, saved1)
     upper = product_t(saved1["hidden"], saved2["hidden"], grads1["gu"], grads2["gu"])
     lower = product_t(grads1["gd"], grads2["gd"], saved1["act"], saved2["act"])
     if by_kernel:
-        square = square_gradients(grads1, grads2, saved1, saved2, cols)
-        square, upper, lower = scatter_by_kernel(square, upper, lower)
+        dx1, square, upper, lower = last_backward(
+            saved1, saved2, gm1, dfirst1, weights, grads1, grads2, upper, lower, cols
+        )
         table = square[across : across + LINES, :across]
         square = square[:across]
         lines = [table[at] for at in range(8)]
         lines.insert(5, table[8 : 8 + upper.shape[1] // across].reshape(-1))
     else:
+        dx1, more = attend(saved1, gm1, dfirst1)
+        grads1.update(more)
         square = jnp.stack(
             [
                 product_t(grads1["gq"], grads2["gq"], saved1["x"], saved2["x"]),
@@ -1132,6 +1203,8 @@
         square, upper, lower, line = scatter(square, upper, lower, table)
         lines = [line[at * across : at * across + across] for at in range(8)]
         lines.insert(5, line[8 * across :])
+    memory_grad = (dx1[:MEMORY] + dx1[MEMORY + TEXT : SEG_ROWS]).astype(BF16)[None]
+    text_grad = paired(dx1, dx2, MEMORY, TEXT)
     own = square.reshape(across, 4, depth)
     result = [own[:, at].T for at in range(4)] + [upper, lower.T]
     return (layer_output, text_grad, memory_grad, *result, *lines)

time: 359 us -> 355 us (0.989)
  Pallas kernels: 329 us -> 320 us
  local copies, waits for them, and re-layouts: 11.2 us -> 15.3 us
    pallas_call x2 -> x1, Pallas kernels: 31.7 us -> 15.8 us  [attention_backward(): pl.pallas_call(attention_backward_kernel, grid=(width // QUAD,), in_specs...]
    pallas_call x2 -> x1, Pallas kernels: 87.8 us -> 95.2 us  [last_backward(): pl.pallas_call(last_backward_kernel, grid=(quads + 1,), in_specs=[rows_bl...]
where the time goes in v5:
time: 355 us; the launch traced here: 350 us
  Pallas kernels  320 us (90%)
  local copies, waits for them, and re-layouts  15.3 us (4%)
  other arithmetic  13 us (4%)
    pallas_call x1, Pallas kernels, last_backward(): pl.pallas_call(last_backward_kernel, grid=(quads + 1,), in_specs=[rows_bl...  95.2 us
    pallas_call x1, Pallas kernels, fetch_by_kernel(): pl.pallas_call(gather_kernel, out_shape=[shape((width, width), BF16)] * 4...  76.1 us
    pallas_call x2, Pallas kernels, attention_forward(): pl.pallas_call(functools.partial(attention_forward_kernel, segment), grid...  39.4 us
    pallas_call x2, Pallas kernels, feed_forward(): pl.pallas_call(feed_forward_kernel, grid=(units // UNITS,), in_specs=[ful...  35.3 us
    pallas_call x2, Pallas kernels, feed_backward(): pl.pallas_call(functools.partial(feed_backward_kernel, segment), grid=(un...  34.5 us
    pallas_call x2, Pallas kernels, product_t(): pl.pallas_call(product_kernel, grid=(units // UNITS,), in_specs=[whole((R...  22.2 us
    pallas_call x1, Pallas kernels, attention_backward(): pl.pallas_call(attention_backward_kernel, grid=(width // QUAD,), in_specs...  15.8 us

profile of v5, /device:TPU:0, one launch (start us, length us, event | category | flops | bytes accessed | tf_op | source)
XLA Modules:
  0.0 350.3 jit_solution(2778926220188312515)
XLA Ops:
  1.3 0.8 reshape.62
  2.1 0.8 concatenate.3
  2.9 0.6 pad.18.vectors
  3.5 1.7 copy.39.wd
  5.2 2.0 pack.1
  7.2 0.0 copy-start
  7.2 1.7 copy.49
  8.9 0.2 copy-done
  9.1 0.2 copy.48
  9.3 2.0 pad_convert_fusion.dy
  11.3 2.0 pad_convert_fusion.1.words
  13.3 76.1 %gather.1 = (bf16[768,768]{1,0:T(8,128)(2,1)}, bf16[768,768]{1,0:T(8,128)(2,1)}, bf16[768,768]{1,0:T(8,128)(2,1)}, bf16[768,768]{1,0:T(8,128)(2,1)}, f32[1,768]{...) custom-call(bf16[112,768]{1,0:T(8,128)(2,1)} %get-tuple-element.94.s, ...), custom_call_target="tpu_custom_call" | custom-call | tf_op jit(solution)/shard_map/gather/pallas_call | solution.py:689
  89.3 19.6 %attention_forward.2 = (bf16[528,768]{1,0:T(8,128)(2,1)}, bf16[528,768]{1,0:T(8,128)(2,1)}, bf16[528,768]{1,0:T(8,128)(2,1)}, bf16[12,528,512]{2,1,0:T(8,128)(2,...) custom-call(s32[1]{0:T(128)S(6)} %copy.52.tails, ...), custom_call_target="tpu_custom_call" | custom-call | tf_op jit(solution)/shard_map/attention_forward/pallas_call | solution.py:171
  109.0 17.6 %feed_forward.2 = (bf16[528,3072]{1,0:T(8,128)(2,1)}, bf16[528,3072]{1,0:T(8,128)(2,1)}, bf16[528,768]{1,0:T(8,128)(2,1)}, f32[16,768]{1,0:T(8,128)}, f32[528,768]{1,0:T(8,128)}, /*index=5*/f32[528,128]{1,0:T(8,128)}) custom-call(f32[528,768]{1,0:T(8,128)} %get-tuple-element.105.hidden, bf16[528,768]{1,0:T(8,128)(2,1)} %get-tuple-element.106.narrow.left1, ...), custom_call_target="tpu_custom_call" | custom-call | tf_op jit(solution)/shard_map/feed_forward/pallas_call | solution.py:242
  126.6 19.8 %attention_forward.3 = (bf16[528,768]{1,0:T(8,128)(2,1)}, bf16[528,768]{1,0:T(8,128)(2,1)}, bf16[528,768]{1,0:T(8,128)(2,1)}, bf16[12,528,512]{2,1,0:T(8,128)(2,...) custom-call(s32[1]{0:T(128)S(6)} %copy.52.tails, ...), custom_call_target="tpu_custom_call" | custom-call | tf_op jit(solution)/shard_map/attention_forward/pallas_call | solution.py:171
  146.4 0.0 copy-start.1
  146.4 17.7 %feed_forward.3 = (bf16[528,3072]{1,0:T(8,128)(2,1)}, bf16[528,3072]{1,0:T(8,128)(2,1)}, bf16[528,768]{1,0:T(8,128)(2,1)}, f32[16,768]{1,0:T(8,128)}, f32[528,768]{1,0:T(8,128)}, /*index=5*/f32[528,128]{1,0:T(8,128)}) custom-call(f32[528,768]{1,0:T(8,128)} %get-tuple-element.115.hidden, bf16[528,768]{1,0:T(8,128)(2,1)} %get-tuple-element.116.narrow.left2, ...), custom_call_target="tpu_custom_call" | custom-call | tf_op jit(solution)/shard_map/feed_forward/pallas_call | solution.py:242
  164.1 0.0 copy-done.1
  164.1 4.5 %broadcast_select_fusion = bf16[1,2,522,768]{3,1,2,0:T(2,128)(2,1)} fusion(pred[2]{0:T(512)(128)(4,1)S(1)} %iota_compare_fusion, bf16[522,768]{1,0:T(8,128)(2,1)} %bitcast.57, bf16[522,768]{1,0:T(8,128)(2,1)S(1)} %bitcast.56), kind=kLoop, calls=%fused_computation | loop fusion | flops 801792 | bytes 3207170 | tf_op jit(solution)/shard_map/jit(_where)/select_n | solution.py:1155
  168.6 17.5 %feed_backward.2 = (bf16[528,768]{1,0:T(8,128)(2,1)}, bf16[528,3072]{1,0:T(8,128)(2,1)}, bf16[528,768]{1,0:T(8,128)(2,1)}, f32[528,768]{1,0:T(8,128)}, bf16[528,...) custom-call(f32[2,528,768]{2,1,0:T(8,128)} %pad_convert_fusion.dy, ...), custom_call_target="tpu_custom_call" | custom-call | tf_op jit(solution)/shard_map/feed_backward/pallas_call | solution.py:316
  186.1 15.8 %attention_backward.1 = (bf16[528,768]{1,0:T(8,128)(2,1)}, bf16[528,768]{1,0:T(8,128)(2,1)}, bf16[528,768]{1,0:T(8,128)(2,1)}, f32[528,768]{1,0:T(8,128)}, f32[1,768]{1,0:T(1,128)}, /*index=5*/f32[1,768]{1,0:T(1,128)}) custom-call(bf16[528,768]{1,0:T(8,128)(2,1)} %get-tuple-element.125.q, bf16[528,768]{1,0:T(8,128)(2,1)} %get-tuple-element.126.k, ...), custom_call_target="tpu_custom_call" | custom-call | tf_op jit(solution)/shard_map/attention_backward/pallas_call | solution.py:415
  201.9 17.0 %feed_backward.3 = (bf16[528,768]{1,0:T(8,128)(2,1)}, bf16[528,3072]{1,0:T(8,128)(2,1)}, bf16[528,768]{1,0:T(8,128)(2,1)}, f32[528,768]{1,0:T(8,128)}, bf16[528,...) custom-call(f32[2,528,768]{2,1,0:T(8,128)} %pad_convert_fusion.dy, ...), custom_call_target="tpu_custom_call" | custom-call | tf_op jit(solution)/shard_map/feed_backward/pallas_call | solution.py:316
  218.9 11.1 %weight_gradient.3.lower = bf16[768,3072]{1,0:T(8,128)(2,1)} custom-call(bf16[528,768]{1,0:T(8,128)(2,1)} %get-tuple-element.162.left1, bf16[528,768]{1,0:T(8,128)(2,1)} %get-tuple-element.163.left2, bf16[528,3072]{1,0:T(8,128)(2,1)} %get-tuple-element.164.right1, bf16[528,3072]{1,0:T(8,128)(2,1)} %get-tuple-element.165.right2), custom_call_target="tpu_custom_call" | custom-call | tf_op jit(solution)/shard_map/weight_gradient/pallas_call | solution.py:722
  230.0 11.1 %weight_gradient.2.upper = bf16[768,3072]{1,0:T(8,128)(2,1)} custom-call(bf16[528,768]{1,0:T(8,128)(2,1)} %get-tuple-element.106.narrow.left1, bf16[528,768]{1,0:T(8,128)(2,1)} %get-tuple-element.116.narrow.left2, bf16[528,3072]{1,0:T(8,128)(2,1)} %get-tuple-element.160.right1, bf16[528,3072]{1,0:T(8,128)(2,1)} %get-tuple-element.161.right2), custom_call_target="tpu_custom_call" | custom-call | tf_op jit(solution)/shard_map/weight_gradient/pallas_call | solution.py:722
  241.1 95.2 %last_backward.1 = (f32[528,768]{1,0:T(8,128)}, f32[112,768]{1,0:T(8,128)}, f32[192,384]{1,0:T(8,128)}, f32[96,768]{1,0:T(8,128)}) custom-call(bf16[528,768]{1,0:T(8,128)(2,1)} %get-tuple-element.118.q, bf16[528,768]{1,0:T(8,128)(2,1)} %get-tuple-element.119.k, bf16[528,768]{1,0:T(8,128)(2,1)} %get-tuple-element.120.v, ...), custom_call_target="tpu_custom_call" | custom-call | tf_op jit(solution)/shard_map/last_backward/pallas_call | solution.py:1036
  336.3 0.7 slice.86
  337.0 0.7 reshape.64
  337.6 1.5 slice_bitcast_fusion.4
  339.1 1.0 slice.76
  340.1 1.4 fusion
  341.6 1.5 slice.72
  343.1 0.2 copy.45
  343.3 0.8 slice_bitcast_fusion
  344.0 1.5 slice.73
  345.6 0.0 copy-start.3
  345.6 0.0 copy-start.2
  345.6 3.1 select_convert_fusion
  348.7 0.0 copy-done.3
  348.7 0.7 copy.53
  349.4 0.0 copy-done.2
  349.4 0.7 copy.54
  (1 shorter events, 0.0 us)
Async XLA Ops:
  7.2 1.9 copy-start
  146.4 17.7 %copy-start.1 = (bf16[528,768]{1,0:T(8,128)(2,1)S(1)}, bf16[528,768]{1,0:T(8,128)(2,1)}, u32[]{:S(2)}) copy-start(bf16[528,768]{1,0:T(8,128)(2,1)} %get-tuple-element.113) | copy-start | bytes 2433028
  345.6 3.1 copy-start.3
  345.6 3.8 %copy-start.2 = (f32[96,768]{1,0:T(8,128)S(1)}, f32[96,768]{1,0:T(8,128)}, u32[]{:S(2)}) copy-start(f32[96,768]{1,0:T(8,128)} %get-tuple-element.169) | copy-start | bytes 884740

commit v6 on v5

--- a/solution.py
+++ b/solution.py
@@ -745,7 +745,6 @@
         self.cols = square.shape[0] // ROWS_MESH
         self.place = Place(self.cols)
         self.length = self.place.length
-        self.stages = self.length + 3
 
     def source(self, which, row, col):
         count, wide = self.outs[which].shape
@@ -886,17 +885,20 @@
 
         self.outs[which][...] = block[...].astype(F32)
 
-    def stage(self, which, stage):
-        length = self.length
-        if 0 <= stage < length:
-            self.cores(which, length - 1 - stage)
-        if 1 <= stage < length + 1:
-            self.corners(which, length - stage)
-        if 2 <= stage < length + 2:
-            self.sides(which, length + 1 - stage)
-        if 3 <= stage < length + 2:
-            self.lines(which, length + 2 - stage)
-        if stage == length + 2:
+    def all_cores(self, which):
+        for distance in range(self.length - 1, -1, -1):
+            self.cores(which, distance)
+
+    def all_corners(self, which):
+        for distance in range(self.length - 1, -1, -1):
+            self.corners(which, distance)
+
+    def step(self, which, at):
+        if at < self.length:
+            self.sides(which, self.length - 1 - at)
+        if 1 <= at < self.length:
+            self.lines(which, self.length - at)
+        if at == self.length:
             self.result(which)
 
     def drain(self, which):
@@ -927,13 +929,27 @@
     step = pl.program_id(0)
     quads = gq.shape[0]
     travel = Scatter(blocks, upper, lower, (square_out, upper_out, lower_out), scratch)
-    moves = [(which, at - 2 * which + 2) for at in range(travel.stages + 2) for which in (1, 2)]
-    moves = [(which, stage) for which, stage in moves if 0 <= stage < travel.stages]
-    slots = quads * PAIRS + 4
+    length = travel.length
+    steps = [functools.partial(travel.step, which, at) for which in (1, 2) for at in range(length + 1)]
+    early = {
+        0: (functools.partial(travel.all_cores, 1),), 1: (functools.partial(travel.all_cores, 2),),
+        2: (functools.partial(travel.all_corners, 1),), 4: (functools.partial(travel.all_corners, 2),),
+    }
+    taken = 0
+    for slot in range(quads * PAIRS, quads * PAIRS + 3):
+        early[slot], taken = (steps[taken],), taken + 1
+    squares = [functools.partial(travel.all_cores, 0), functools.partial(travel.all_corners, 0)]
+    squares += [functools.partial(travel.step, 0, at) for at in range(length + 1)]
+    late = []
+    while steps[taken:] or squares:
+        late += steps[taken : taken + 2] if len(squares) > length else steps[taken : taken + 1]
+        taken += 2 if len(squares) > length else 1
+        late += squares[:1]
+        squares = squares[1:]
 
     def advance(slot):
-        for which, stage in moves[len(moves) * slot // slots : len(moves) * (slot + 1) // slots]:
-            travel.stage(which, stage)
+        for move in early.get(slot, ()):
+            move()
 
     @pl.when(step == 0)
     def _():
@@ -997,9 +1013,8 @@
                 )
                 blocks[block, across:, :] = narrow
         travel.begin(0)
-        advance(slots - 1)
-        for stage in range(travel.stages):
-            travel.stage(0, stage)
+        for move in late:
+            move()
         for which in range(3):
             travel.drain(which)
 

time: 355 us -> 349 us (0.983)
  Pallas kernels: 320 us -> 314 us
    pallas_call x1, Pallas kernels: 95.2 us -> 89.1 us  [last_backward(): pl.pallas_call(last_backward_kernel, grid=(quads + 1,), in_specs=[rows_bl...]
where the time goes in v6:
time: 349 us; the launch traced here: 344 us
  Pallas kernels  314 us (90%)
  local copies, waits for them, and re-layouts  15.3 us (4%)
  other arithmetic  13 us (4%)
    pallas_call x1, Pallas kernels, last_backward(): pl.pallas_call(last_backward_kernel, grid=(quads + 1,), in_specs=[rows_bl...  89.1 us
    pallas_call x1, Pallas kernels, fetch_by_kernel(): pl.pallas_call(gather_kernel, out_shape=[shape((width, width), BF16)] * 4...  76.1 us
    pallas_call x2, Pallas kernels, attention_forward(): pl.pallas_call(functools.partial(attention_forward_kernel, segment), grid...  39.4 us
    pallas_call x2, Pallas kernels, feed_forward(): pl.pallas_call(feed_forward_kernel, grid=(units // UNITS,), in_specs=[ful...  35.3 us
    pallas_call x2, Pallas kernels, feed_backward(): pl.pallas_call(functools.partial(feed_backward_kernel, segment), grid=(un...  34.5 us
    pallas_call x2, Pallas kernels, product_t(): pl.pallas_call(product_kernel, grid=(units // UNITS,), in_specs=[whole((R...  22.2 us
    pallas_call x1, Pallas kernels, attention_backward(): pl.pallas_call(attention_backward_kernel, grid=(width // QUAD,), in_specs...  15.8 us

profile of v6, /device:TPU:0, one launch (start us, length us, event | category | flops | bytes accessed | tf_op | source)
XLA Modules:
  0.0 344.2 jit_solution(2002342174261230075)
XLA Ops:
  1.3 0.8 reshape.62
  2.1 0.8 concatenate.3
  2.9 0.6 pad.18.vectors
  3.5 1.7 copy.39.wd
  5.2 2.0 pack.1
  7.2 0.0 copy-start
  7.2 1.7 copy.49
  8.9 0.2 copy-done
  9.1 0.2 copy.48
  9.3 2.0 pad_convert_fusion.dy
  11.3 2.0 pad_convert_fusion.1.words
  13.3 76.1 %gather.1 = (bf16[768,768]{1,0:T(8,128)(2,1)}, bf16[768,768]{1,0:T(8,128)(2,1)}, bf16[768,768]{1,0:T(8,128)(2,1)}, bf16[768,768]{1,0:T(8,128)(2,1)}, f32[1,768]{...) custom-call(bf16[112,768]{1,0:T(8,128)(2,1)} %get-tuple-element.94.s, ...), custom_call_target="tpu_custom_call" | custom-call | tf_op jit(solution)/shard_map/gather/pallas_call | solution.py:689
  89.3 19.6 %attention_forward.2 = (bf16[528,768]{1,0:T(8,128)(2,1)}, bf16[528,768]{1,0:T(8,128)(2,1)}, bf16[528,768]{1,0:T(8,128)(2,1)}, bf16[12,528,512]{2,1,0:T(8,128)(2,...) custom-call(s32[1]{0:T(128)S(6)} %copy.52.tails, ...), custom_call_target="tpu_custom_call" | custom-call | tf_op jit(solution)/shard_map/attention_forward/pallas_call | solution.py:171
  109.0 17.6 %feed_forward.2 = (bf16[528,3072]{1,0:T(8,128)(2,1)}, bf16[528,3072]{1,0:T(8,128)(2,1)}, bf16[528,768]{1,0:T(8,128)(2,1)}, f32[16,768]{1,0:T(8,128)}, f32[528,768]{1,0:T(8,128)}, /*index=5*/f32[528,128]{1,0:T(8,128)}) custom-call(f32[528,768]{1,0:T(8,128)} %get-tuple-element.105.hidden, bf16[528,768]{1,0:T(8,128)(2,1)} %get-tuple-element.106.narrow.left1, ...), custom_call_target="tpu_custom_call" | custom-call | tf_op jit(solution)/shard_map/feed_forward/pallas_call | solution.py:242
  126.6 19.8 %attention_forward.3 = (bf16[528,768]{1,0:T(8,128)(2,1)}, bf16[528,768]{1,0:T(8,128)(2,1)}, bf16[528,768]{1,0:T(8,128)(2,1)}, bf16[12,528,512]{2,1,0:T(8,128)(2,...) custom-call(s32[1]{0:T(128)S(6)} %copy.52.tails, ...), custom_call_target="tpu_custom_call" | custom-call | tf_op jit(solution)/shard_map/attention_forward/pallas_call | solution.py:171
  146.4 0.0 copy-start.1
  146.4 17.7 %feed_forward.3 = (bf16[528,3072]{1,0:T(8,128)(2,1)}, bf16[528,3072]{1,0:T(8,128)(2,1)}, bf16[528,768]{1,0:T(8,128)(2,1)}, f32[16,768]{1,0:T(8,128)}, f32[528,768]{1,0:T(8,128)}, /*index=5*/f32[528,128]{1,0:T(8,128)}) custom-call(f32[528,768]{1,0:T(8,128)} %get-tuple-element.115.hidden, bf16[528,768]{1,0:T(8,128)(2,1)} %get-tuple-element.116.narrow.left2, ...), custom_call_target="tpu_custom_call" | custom-call | tf_op jit(solution)/shard_map/feed_forward/pallas_call | solution.py:242
  164.1 0.0 copy-done.1
  164.1 4.5 %broadcast_select_fusion = bf16[1,2,522,768]{3,1,2,0:T(2,128)(2,1)} fusion(pred[2]{0:T(512)(128)(4,1)S(1)} %iota_compare_fusion, bf16[522,768]{1,0:T(8,128)(2,1)} %bitcast.57, bf16[522,768]{1,0:T(8,128)(2,1)S(1)} %bitcast.56), kind=kLoop, calls=%fused_computation | loop fusion | flops 801792 | bytes 3207170 | tf_op jit(solution)/shard_map/jit(_where)/select_n | solution.py:1170
  168.6 17.5 %feed_backward.2 = (bf16[528,768]{1,0:T(8,128)(2,1)}, bf16[528,3072]{1,0:T(8,128)(2,1)}, bf16[528,768]{1,0:T(8,128)(2,1)}, f32[528,768]{1,0:T(8,128)}, bf16[528,...) custom-call(f32[2,528,768]{2,1,0:T(8,128)} %pad_convert_fusion.dy, ...), custom_call_target="tpu_custom_call" | custom-call | tf_op jit(solution)/shard_map/feed_backward/pallas_call | solution.py:316
  186.1 15.8 %attention_backward.1 = (bf16[528,768]{1,0:T(8,128)(2,1)}, bf16[528,768]{1,0:T(8,128)(2,1)}, bf16[528,768]{1,0:T(8,128)(2,1)}, f32[528,768]{1,0:T(8,128)}, f32[1,768]{1,0:T(1,128)}, /*index=5*/f32[1,768]{1,0:T(1,128)}) custom-call(bf16[528,768]{1,0:T(8,128)(2,1)} %get-tuple-element.125.q, bf16[528,768]{1,0:T(8,128)(2,1)} %get-tuple-element.126.k, ...), custom_call_target="tpu_custom_call" | custom-call | tf_op jit(solution)/shard_map/attention_backward/pallas_call | solution.py:415
  201.9 17.0 %feed_backward.3 = (bf16[528,768]{1,0:T(8,128)(2,1)}, bf16[528,3072]{1,0:T(8,128)(2,1)}, bf16[528,768]{1,0:T(8,128)(2,1)}, f32[528,768]{1,0:T(8,128)}, bf16[528,...) custom-call(f32[2,528,768]{2,1,0:T(8,128)} %pad_convert_fusion.dy, ...), custom_call_target="tpu_custom_call" | custom-call | tf_op jit(solution)/shard_map/feed_backward/pallas_call | solution.py:316
  218.9 11.1 %weight_gradient.3.lower = bf16[768,3072]{1,0:T(8,128)(2,1)} custom-call(bf16[528,768]{1,0:T(8,128)(2,1)} %get-tuple-element.162.left1, bf16[528,768]{1,0:T(8,128)(2,1)} %get-tuple-element.163.left2, bf16[528,3072]{1,0:T(8,128)(2,1)} %get-tuple-element.164.right1, bf16[528,3072]{1,0:T(8,128)(2,1)} %get-tuple-element.165.right2), custom_call_target="tpu_custom_call" | custom-call | tf_op jit(solution)/shard_map/weight_gradient/pallas_call | solution.py:722
  230.0 11.1 %weight_gradient.2.upper = bf16[768,3072]{1,0:T(8,128)(2,1)} custom-call(bf16[528,768]{1,0:T(8,128)(2,1)} %get-tuple-element.106.narrow.left1, bf16[528,768]{1,0:T(8,128)(2,1)} %get-tuple-element.116.narrow.left2, bf16[528,3072]{1,0:T(8,128)(2,1)} %get-tuple-element.160.right1, bf16[528,3072]{1,0:T(8,128)(2,1)} %get-tuple-element.161.right2), custom_call_target="tpu_custom_call" | custom-call | tf_op jit(solution)/shard_map/weight_gradient/pallas_call | solution.py:722
  241.1 89.1 %last_backward.1 = (f32[528,768]{1,0:T(8,128)}, f32[112,768]{1,0:T(8,128)}, f32[192,384]{1,0:T(8,128)}, f32[96,768]{1,0:T(8,128)}) custom-call(bf16[528,768]{1,0:T(8,128)(2,1)} %get-tuple-element.118.q, bf16[528,768]{1,0:T(8,128)(2,1)} %get-tuple-element.119.k, bf16[528,768]{1,0:T(8,128)(2,1)} %get-tuple-element.120.v, ...), custom_call_target="tpu_custom_call" | custom-call | tf_op jit(solution)/shard_map/last_backward/pallas_call | solution.py:1051
  330.2 0.7 slice.86
  330.9 0.7 reshape.64
  331.5 1.5 slice_bitcast_fusion.4
  333.1 1.0 slice.76
  334.0 1.4 fusion
  335.5 1.5 slice.72
  337.0 0.2 copy.45
  337.2 0.8 slice_bitcast_fusion
  337.9 1.5 slice.73
  339.5 0.0 copy-start.3
  339.5 0.0 copy-start.2
  339.5 3.1 select_convert_fusion
  342.6 0.0 copy-done.3
  342.6 0.7 copy.53
  343.3 0.0 copy-done.2
  343.3 0.7 copy.54
  (1 shorter events, 0.0 us)
Async XLA Ops:
  7.2 1.9 copy-start
  146.4 17.7 %copy-start.1 = (bf16[528,768]{1,0:T(8,128)(2,1)S(1)}, bf16[528,768]{1,0:T(8,128)(2,1)}, u32[]{:S(2)}) copy-start(bf16[528,768]{1,0:T(8,128)(2,1)} %get-tuple-element.113) | copy-start | bytes 2433028
  339.5 3.1 copy-start.3
  339.5 3.8 %copy-start.2 = (f32[96,768]{1,0:T(8,128)S(1)}, f32[96,768]{1,0:T(8,128)}, u32[]{:S(2)}) copy-start(f32[96,768]{1,0:T(8,128)} %get-tuple-element.169) | copy-start | bytes 884740
